TPU v7x, 32 devices: a whole 2x2x4 slice. The times are simulated.
32 devices in a mesh: ctx: 16 (over z, x, core), head: 2 (over y).
Axes of the slice: x: 2, y: 2, z: 4, core: 2. Of those that a mesh axis runs over, the one named last changes fastest.
Arguments:
- query_vectors: bfloat16 [2048, 5120], P('ctx', 'head'), may hold values from -128 to 128
- key_vectors: bfloat16 [2048, 5120], P('ctx', 'head'), may hold values from -128 to 128
- value_vectors: bfloat16 [2048, 5120], P('ctx', 'head'), may hold values from -24 to 24
- output_grad: bfloat16 [2048, 5120], P('ctx', 'head'), may hold values from -6 to 6
- query_gain: float32 [5120], P('head'), may hold values from 0.1 to 1.9
- key_gain: float32 [5120], P('head'), may hold values from 0.1 to 1.9
- block_pairs: int32 [16, 7, 2], P('ctx'), may hold values from 0 to 15, as said below
- pair_counts: int32 [16], P('ctx'), may hold values from 1 to 7, as said below
Outputs:
- attended: bfloat16 [2048, 5120], P('ctx', 'head')
- query_grad: bfloat16 [2048, 5120], P('ctx', 'head')
- key_grad: bfloat16 [2048, 5120], P('ctx', 'head')
- value_grad: bfloat16 [2048, 5120], P('ctx', 'head')
Inputs may be any that keep to these rules, and one draw needn't show every extreme that they name: For span c the first pair_counts[c] slots of block_pairs[c] hold distinct pairs; the query block is c (a mask block is one 128-token span) and the key block is c - o, where o is 0 or plus or minus a power of two no larger than 4; the pair (c, c) is always present. Later slots are to be ignored. `pair_counts`: some span uses all 7 slots.
All inputs are finite; a program needn't handle non-finite values.
Results may differ from a plain program's by a relative error of at most 0.0085.
The roundings to bfloat16 on the way count: a program that leaves them out, or rounds other values in their place, can miss the bound.
Values may be sent and summed in bfloat16 or wider, within the bound.
No kernel may reach another device: no remote copies, remote signals or barrier semaphores. Data moves between devices by JAX's collectives and lax.ppermute only.
A program may use at most 128 MiB of HBM per device.

v0:
```python
import functools

import jax
import jax.numpy as jnp
from jax import lax
from jax.experimental import pallas as pl
from jax.experimental.pallas import tpu as pltpu
from jax.sharding import Mesh
from jax.sharding import PartitionSpec as P

HEAD = 128
epsilon = 1e-06
lowest = -1e30
LOG2E = 1.4426950408889634
SCALE = HEAD ** (-0.5)
bf16 = jnp.bfloat16
f32 = jnp.float32


def offset_list(levels):
    result = [0]
    for height in range(levels):
        result = result + [2**height, -(2**height)]
    return result


def plan(spans, heads_here):
    levels = spans.bit_length() - 2
    reach = 2 ** (levels - 1)
    group = reach if heads_here % reach == 0 and spans % reach == 0 else 1
    offsets = sorted(offset_list(levels), reverse=True)
    if group > 1:
        distances = [-1, 0, 1]
    else:
        distances = sorted(-o for o in offsets)
    return group, offsets, distances


def dot(a, b, ca, cb):
    return lax.dot_general(a, b, (((ca,), (cb,)), ((), ())), preferred_element_type=f32)


def attend(place, *refs, group, offsets, distances):
    nd = len(distances)
    ng = group * nd
    noff = len(offsets)
    it = iter(refs)
    qd = [next(it) for _ in range(group)]
    kv = [[next(it) for _ in range(group)] for _ in range(nd)]
    rstd_ref, bias_ref, qgain_ref, kgain_ref = (next(it) for _ in range(4))
    out_o = [next(it) for _ in range(group)]
    out_q = [next(it) for _ in range(group)]
    out_kv = [next(it) for _ in range(nd)]
    inner_ref = next(it)
    keys, vals, dkeys, dvals, inners, rcols = (next(it) for _ in range(6))
    home = distances.index(0)
    head = pl.program_id(0)
    r = place[0]

    @pl.when(head == 0)
    def _():
        rcols[...] = jnp.transpose(rstd_ref[...])
        inners[...] = jnp.zeros_like(inners)

    qgain = qgain_ref[...]
    kgain = kgain_ref[...]

    def rows(slot):
        return pl.ds(pl.multiple_of(slot * HEAD, HEAD), HEAD)

    def column(i):
        return rcols[:, i : i + 1]

    for d in range(nd):
        for m in range(group):
            at = rows(d * group + (m ^ r))
            unit = kv[d][m][0].astype(f32) * column(group + d * group + m)
            keys[at, :] = (unit * kgain).astype(bf16)
            vals[at, :] = kv[d][m][1]
    dkeys[...] = jnp.zeros_like(dkeys)
    dvals[...] = jnp.zeros_like(dvals)

    for m in range(group):
        s = m ^ r
        unit = qd[m][0].astype(f32) * column(m)
        q = (unit * qgain).astype(bf16)
        g = qd[m][1]
        if group > 1:
            slots = [home * group + s - o for o in offsets]
        else:
            slots = [distances.index(-o) for o in offsets]
        k = jnp.concatenate([keys[rows(x), :] for x in slots], axis=0)
        v = jnp.concatenate([vals[rows(x), :] for x in slots], axis=0)
        scores = dot(q, k, 1, 1) * (SCALE * LOG2E) + bias_ref[m : m + 1, :]
        top = jnp.max(scores, axis=1, keepdims=True)
        e = jnp.exp2(scores - top)
        p = e * (1.0 / jnp.sum(e, axis=1, keepdims=True))
        p_low = p.astype(bf16)
        o = dot(p_low, v, 1, 0).astype(bf16)
        out_o[m][...] = o
        delta = jnp.sum(g.astype(f32) * o.astype(f32), axis=1, keepdims=True)
        dp = dot(g, v, 1, 1)
        ds = (p * SCALE * (dp - delta)).astype(bf16)
        dq = dot(ds, k, 1, 0)
        out_q[m][...] = dq
        inners[m] += dq * qgain * unit
        dk = dot(ds, q, 0, 0)
        dv = dot(p_low, g, 0, 0)
        for j in range(noff):
            dkeys[rows(slots[j]), :] += dk[j * HEAD : (j + 1) * HEAD]
            dvals[rows(slots[j]), :] += dv[j * HEAD : (j + 1) * HEAD]

    for d in range(nd):
        for m in range(group):
            at = rows(d * group + (m ^ r))
            unit = kv[d][m][0].astype(f32) * column(group + d * group + m)
            dk = dkeys[at, :]
            inners[group + d * group + m] += dk * kgain * unit
            out_kv[d][0, m] = dk.astype(out_kv[d].dtype)
            out_kv[d][1, m] = dvals[at, :].astype(out_kv[d].dtype)

    @pl.when(head == pl.num_programs(0) - 1)
    def _():
        lanes = lax.broadcasted_iota(jnp.int32, (HEAD, HEAD), 1)
        table = jnp.zeros((HEAD, HEAD), f32)
        for base in range(0, group + ng, group):
            for m in range(group):
                total = jnp.sum(inners[base + m], axis=1, keepdims=True)
                table = jnp.where(lanes == base + (m ^ r), total, table)
        inner_ref[...] = jnp.transpose(table)


def attention(place, qd, kv, rstd, bias, query_gain, key_gain, group, offsets, distances):
    width = qd[0].shape[2]
    heads = width // HEAD
    nd = len(distances)
    ng = nd * group
    noff = len(offsets)
    pair = pl.BlockSpec((2, HEAD, HEAD), lambda h, _: (0, 0, h))
    flat = pl.BlockSpec((HEAD, HEAD), lambda h, _: (0, h))
    table = pl.BlockSpec((HEAD, HEAD), lambda h, _: (0, 0))
    gain = pl.BlockSpec((1, HEAD), lambda h, _: (0, h))
    grads = pl.BlockSpec((2, group, HEAD, HEAD), lambda h, _: (0, 0, 0, h))
    home = distances.index(0)
    outs = (
        [jax.ShapeDtypeStruct((HEAD, width), bf16)] * group
        + [jax.ShapeDtypeStruct((HEAD, width), f32)] * group
        + [
            jax.ShapeDtypeStruct((2, group, HEAD, width), f32 if d == home else bf16)
            for d in range(nd)
        ]
        + [jax.ShapeDtypeStruct((HEAD, HEAD), f32)]
    )
    work = heads * group * noff * 6 * 2 * HEAD**3
    result = pl.pallas_call(
        functools.partial(attend, group=group, offsets=offsets, distances=distances),
        grid_spec=pltpu.PrefetchScalarGridSpec(
            num_scalar_prefetch=1,
            grid=(heads,),
            in_specs=[pair] * (group + ng)
            + [table, pl.BlockSpec((group, noff * HEAD), lambda h, _: (0, 0)), gain, gain],
            out_specs=[flat] * (2 * group) + [grads] * nd + [table],
            scratch_shapes=[
                pltpu.VMEM((ng * HEAD, HEAD), bf16),
                pltpu.VMEM((ng * HEAD, HEAD), bf16),
                pltpu.VMEM((ng * HEAD, HEAD), f32),
                pltpu.VMEM((ng * HEAD, HEAD), f32),
                pltpu.VMEM((group + ng, HEAD, HEAD), f32),
                pltpu.VMEM((HEAD, HEAD), f32),
            ],
        ),
        out_shape=outs,
        compiler_params=pltpu.CompilerParams(vmem_limit_bytes=40 * 2**20),
        cost_estimate=pl.CostEstimate(
            flops=work, bytes_accessed=12 * 2**20, transcendentals=work // 1536
        ),
        name="attend",
    )(
        place,
        *qd,
        *[piece for block in kv for piece in block],
        rstd,
        bias,
        query_gain,
        key_gain,
    )
    return (
        result[:group],
        result[group : 2 * group],
        result[2 * group : 2 * group + nd],
        result[2 * group + nd],
    )


def local(
    query_vectors,
    key_vectors,
    value_vectors,
    output_grad,
    query_gain,
    key_gain,
    block_pairs,
    pair_counts,
    *,
    group,
    offsets,
    distances,
    heads_all,
):
    row_count, col_count = query_vectors.shape
    width = col_count // group
    features = heads_all * HEAD
    blocks = lax.axis_size("block")
    block = lax.axis_index("block")
    r = lax.axis_index("place")
    span = block * group + r
    home = distances.index(0)

    def chunk(array, index):
        return lax.dynamic_slice_in_dim(array, index * width, width, axis=1)

    def swap(x, m):
        return lax.ppermute(x, "place", [(i, i ^ m) for i in range(group)]) if m else x

    def moved(x, by):
        return lax.ppermute(
            x, "block", [(i, i + by) for i in range(blocks) if 0 <= i + by < blocks]
        )

    def pieces(a, b):
        return [swap(jnp.stack([chunk(a, r ^ m), chunk(b, r ^ m)]), m) for m in range(group)]

    kv_home = pieces(key_vectors, value_vectors)
    kv = [
        [moved(x, -by) if by else x for x in kv_home]
        for by in distances
    ]
    qd = pieces(query_vectors, output_grad)

    query_float = query_vectors.astype(f32)
    key_float = key_vectors.astype(f32)
    live = jnp.arange(block_pairs.shape[1], dtype=jnp.int32) < pair_counts[0]
    steps = block_pairs[0, :, 0] - block_pairs[0, :, 1]
    wanted = jnp.array(offsets, jnp.int32)
    flags = jnp.any(live[:, None] & (steps[:, None] == wanted[None, :]), axis=0)
    flag_row = jnp.zeros((HEAD,), f32).at[: len(offsets)].set(flags.astype(f32))
    mine = jnp.stack(
        [jnp.sum(query_float * query_float, axis=1), jnp.sum(key_float * key_float, axis=1), flag_row]
    )
    slots = jnp.arange(group, dtype=jnp.int32)
    sums = lax.psum(
        jnp.where((slots == r)[:, None, None], mine[None], 0.0), ("place", "head")
    )
    sums = sums[slots ^ r]
    key_sums = jnp.concatenate([moved(sums[:, 1], -by) if by else sums[:, 1] for by in distances])
    rstd = lax.rsqrt(jnp.concatenate([sums[:, 0], key_sums]) / features + epsilon)
    bias = jnp.where(sums[:, 2, : len(offsets)] > 0.5, 0.0, lowest)
    bias = jnp.repeat(bias, HEAD, axis=1)
    own_gains = [chunk(x[None, :], r) for x in (query_gain, key_gain)]

    o_parts, q_parts, kv_parts, inner = attention(
        jnp.reshape(r, (1,)).astype(jnp.int32),
        qd,
        kv,
        jnp.pad(rstd, ((0, HEAD - rstd.shape[0]), (0, 0))),
        bias,
        *own_gains,
        group,
        offsets,
        distances,
    )

    def gathered(parts):
        stacked = jnp.stack([swap(x, m) for m, x in enumerate(parts)])
        return jnp.concatenate(
            [lax.dynamic_index_in_dim(stacked, j ^ r, 0, keepdims=False) for j in range(group)],
            axis=-1,
        )

    attended = gathered(o_parts)
    back = [moved(kv_parts[d], by) for d, by in enumerate(distances) if by]
    key_inner = inner[group + home * group : 2 * group + home * group]
    for d, by in enumerate(distances):
        if by:
            key_inner = key_inner + moved(inner[group + d * group : 2 * group + d * group], by)
    inners = lax.psum(jnp.stack([inner[:group], key_inner]), ("place", "head")) / features
    inners = inners[:, slots ^ r]

    def finished(raw, rstd_row, gain, grad, inner_row):
        unit = raw.astype(f32) * rstd_row[:, None]
        return (rstd_row[:, None] * (gain * grad - unit * inner_row[:, None])).astype(bf16)

    query_grad = gathered(
        [
            finished(qd[m][0], rstd[m], own_gains[0], q_parts[m], inners[0, m])
            for m in range(group)
        ]
    )
    both = []
    for m in range(group):
        total = kv_parts[home][:, m]
        for x in back:
            total = total + x[:, m].astype(f32)
        key_part = finished(
            kv_home[m][0], rstd[group + home * group + m], own_gains[1], total[0], inners[1, m]
        )
        both.append(jnp.stack([key_part, total[1].astype(bf16)]))
    both = gathered(both)
    return (attended, query_grad, both[0], both[1])


def solution(mesh):
    spans, head_groups = mesh.devices.shape
    heads_all = 5120 // HEAD
    group, offsets, distances = plan(spans, heads_all // head_groups)
    inner_mesh = Mesh(
        mesh.devices.reshape(spans // group, group, head_groups), ("block", "place", "head")
    )
    ctx = ("block", "place")
    placed = (
        P(ctx, "head"),
        P(ctx, "head"),
        P(ctx, "head"),
        P(ctx, "head"),
        P("head"),
        P("head"),
        P(ctx, None, None),
        P(ctx),
    )
    return jax.shard_map(
        functools.partial(
            local, group=group, offsets=offsets, distances=distances, heads_all=heads_all
        ),
        mesh=inner_mesh,
        in_specs=placed,
        out_specs=(P(ctx, "head"),) * 4,
        check_vma=False,
    )
```

profile of v0, /device:TPU:0, one launch (start us, length us, event | category | flops | bytes accessed | tf_op | source)
XLA Modules:
  0.0 179.6 jit_solution(18406295985930514360)
XLA Ops:
  0.7 1.6 dynamic-slice_bitcast_fusion.12
  2.3 1.4 collective-permute-start.10
  3.8 5.6 %collective-permute-start.3 = (bf16[2,128,640]{2,1,0:T(8,128)(2,1)S(1)}, bf16[2,128,640]{2,1,0:T(8,128)(2,1)S(1)}, u32[]{:S(2)}, u32[]{:S(2)}) collective-permute-start(bf16[2,128,640]{2,1,0:T(8,128)(2,1)S(1)} %pad_maximum_fusion.10.refs_8_), channel_id=1, source_target_pairs={{0,8},{8,16},{16,24},{1,9},{9,17},{17,25},{2,10},{10,18},{18,26},{... | collective-permute-start | bytes 983048 | tf_op jit(solution)/shard_map/ppermute | solution.py:226
  10.7 14.3 %psum.14 = f32[4,3,128]{2,1,0:T(4,128)S(1)} all-reduce(f32[4,3,128]{2,1,0:T(4,128)S(1)} %broadcast_select_fusion), channel_id=1, replica_groups=mesh['block'=4,'place'=4,'head'=2] {'place','head'}, use_global_device_ids=true, to_apply=%region_3.0 | all-reduce | flops 1536 | bytes 12288 | tf_op jit(solution)/shard_map/psum | solution.py:251
  26.9 1.5 collective-permute-start.6
  28.6 1.3 dynamic-slice_bitcast_fusion.19
  31.1 3.5 %collective-permute-start.14 = (f32[4,128]{1,0:T(4,128)S(1)}, f32[4,128]{1,0:T(4,128)S(1)}, u32[]{:S(2)}, u32[]{:S(2)}) collective-permute-start(f32[4,128]{1,0:T(4,128)S(1)} %bitcast.214), channel_id=1, source_target_pairs={{0,8},{8,16},{16,24},{1,9},{9,17},{17,25},{2,10},{10,18},{18,26},{... | collective-permute-start | bytes 6152 | tf_op jit(solution)/shard_map/ppermute | solution.py:226
  36.7 1.5 collective-permute-start.1
  41.6 4.3 %collective-permute-done.8.refs_11_ = bf16[2,128,640]{2,1,0:T(8,128)(2,1)S(1)} collective-permute-done((bf16[2,128,640]{2,1,0:T(8,128)(2,1)S(1)}, bf16[2,128,640]{2,1,0:T(8,128)(2,1)S(1)}, u32[]{:S(2)}, u32[]{:S(2)}) %collective-permute-start.8) | collective-permute-done | bytes 327712 | tf_op jit(solution)/shard_map/ppermute | solution.py:223
  45.9 4.2 %collective-permute-start.7 = (bf16[2,128,640]{2,1,0:T(8,128)(2,1)S(1)}, bf16[2,128,640]{2,1,0:T(8,128)(2,1)S(1)}, u32[]{:S(2)}, u32[]{:S(2)}) collective-permute-start(bf16[2,128,640]{2,1,0:T(8,128)(2,1)S(1)} %collective-permute-done.6.refs_10_), channel_id=1, source_target_pairs={{0,8},{8,16},{16,24},{1,9},{9,17},{17,25},{2,10},{10,18},{18,26},{... | collective-permute-start | bytes 983048 | tf_op jit(solution)/shard_map/ppermute | solution.py:226
  50.1 2.7 %collective-permute-done.1.refs_2_ = bf16[2,128,640]{2,1,0:T(8,128)(2,1)S(1)} collective-permute-done((bf16[2,128,640]{2,1,0:T(8,128)(2,1)S(1)}, bf16[2,128,640]{2,1,0:T(8,128)(2,1)S(1)}, u32[]{:S(2)}, u32[]{:S(2)}) %collective-permute-start.1) | collective-permute-done | bytes 327712 | tf_op jit(solution)/shard_map/ppermute | solution.py:223
  55.5 4.8 %collective-permute-start.5 = (bf16[2,128,640]{2,1,0:T(8,128)(2,1)S(1)}, bf16[2,128,640]{2,1,0:T(8,128)(2,1)S(1)}, u32[]{:S(2)}, u32[]{:S(2)}) collective-permute-start(bf16[2,128,640]{2,1,0:T(8,128)(2,1)S(1)} %collective-permute-done.4.refs_9_), channel_id=1, source_target_pairs={{0,8},{8,16},{16,24},{1,9},{9,17},{17,25},{2,10},{10,18},{18,26},{... | collective-permute-start | bytes 983048 | tf_op jit(solution)/shard_map/ppermute | solution.py:226
  63.1 4.6 %collective-permute-start.9 = (bf16[2,128,640]{2,1,0:T(8,128)(2,1)S(1)}, bf16[2,128,640]{2,1,0:T(8,128)(2,1)S(1)}, u32[]{:S(2)}, u32[]{:S(2)}) collective-permute-start(bf16[2,128,640]{2,1,0:T(8,128)(2,1)S(1)} %collective-permute-done.8.refs_11_), channel_id=1, source_target_pairs={{0,8},{8,16},{16,24},{1,9},{9,17},{17,25},{2,10},{10,18},{18,26},{... | collective-permute-start | bytes 983048 | tf_op jit(solution)/shard_map/ppermute | solution.py:226
  89.1 24.3 %attend.1 = (bf16[128,640]{1,0:T(8,128)(2,1)S(1)}, bf16[128,640]{1,0:T(8,128)(2,1)}, bf16[128,640]{1,0:T(8,128)(2,1)}, bf16[128,640]{1,0:T(8,128)(2,1)}, f32[128...) custom-call(s32[1]{0:T(128)} %bitcast.place, ...), custom_call_target="tpu_custom_call" | custom-call | flops 3523215360 | bytes 12582912 | tf_op jit(solution)/shard_map/attend/pallas_call | solution.py:155
  115.5 4.4 %collective-permute-start.20 = (f32[4,128]{1,0:T(4,128)S(1)}, f32[4,128]{1,0:T(4,128)S(1)}, u32[]{:S(2)}, u32[]{:S(2)}) collective-permute-start(f32[4,128]{1,0:T(4,128)S(1)} %get-tuple-element.75), channel_id=1, source_target_pairs={{0,8},{8,16},{16,24},{1,9},{9,17},{17,25},{2,10},{10,18},{18,26},{... | collective-permute-start | bytes 6152 | tf_op jit(solution)/shard_map/ppermute | solution.py:226
  120.0 1.3 collective-permute-start.19
  125.4 5.3 %collective-permute-start.25 = (bf16[2,4,128,640]{3,2,1,0:T(8,128)(2,1)}, bf16[2,4,128,640]{3,2,1,0:T(8,128)(2,1)}, u32[]{:S(2)}, u32[]{:S(2)}) collective-permute-start(bf16[2,4,128,640]{3,2,1,0:T(8,128)(2,1)} %get-tuple-element.39), channel_id=1, source_target_pairs={{0,8},{8,16},{16,24},{1,9},{9,17},{17,25},{2,10},{10,18},{18,26},{... | collective-permute-start | bytes 3932168 | tf_op jit(solution)/shard_map/ppermute | solution.py:226
  130.8 12.7 %psum.15 = f32[2,4,128]{2,1,0:T(4,128)S(1)} all-reduce(f32[2,4,128]{2,1,0:T(4,128)S(1)} %pad_maximum_fusion.17), channel_id=1, replica_groups=mesh['block'=4,'place'=4,'head'=2] {'place','head'}, use_global_device_ids=true, to_apply=%region_4.5 | all-reduce | flops 1024 | bytes 8192 | tf_op jit(solution)/shard_map/psum | solution.py:286
  144.1 1.8 %fusion.28 = (bf16[1,128,640]{2,1,0:T(8,128)(2,1)S(1)}, bf16[128,640]{1,0:T(8,128)(2,1)S(1)}, bf16[128,640]{1,0:T(8,128)(2,1)S(1)}, bf16[128,640]{1,0:T(8,128)(2,1)S(1)}) fusion(f32[128,640]{1,0:T(8,128)S(1)} %get-tuple-element.32, f32[128]{0:T(128)S(1)} %get-tuple-element.93, f32[640]{0:T(1024)S(1)} %dynamic-slice.11, f32[128]{0:T(128)S(1)} %get-tuple-element.84, ...), kind=kLoop, calls=%fused_computation.72 | loop fusion | flops 2293760 | bytes 2628100 | tf_op jit(solution)/shard_map/stack | solution.py:274
  149.9 3.4 %collective-permute-done.22 = bf16[128,640]{1,0:T(8,128)(2,1)S(1)} collective-permute-done((bf16[128,640]{1,0:T(8,128)(2,1)S(1)}, bf16[128,640]{1,0:T(8,128)(2,1)S(1)}, u32[]{:S(2)}, u32[]{:S(2)}) %collective-permute-start.22) | collective-permute-done | bytes 163872 | tf_op jit(solution)/shard_map/ppermute | solution.py:223
  153.2 2.3 %collective-permute-done.23 = bf16[128,640]{1,0:T(8,128)(2,1)S(1)} collective-permute-done((bf16[128,640]{1,0:T(8,128)(2,1)S(1)}, bf16[128,640]{1,0:T(8,128)(2,1)S(1)}, u32[]{:S(2)}, u32[]{:S(2)}) %collective-permute-start.23) | collective-permute-done | bytes 163872 | tf_op jit(solution)/shard_map/ppermute | solution.py:223
  158.6 2.1 %convert_add_fusion.3 = (f32[2,1,128,640]{3,2,1,0:T(8,128)S(1)}, f32[2,1,128,640]{3,2,1,0:T(8,128)S(1)}, f32[2,1,128,640]{3,2,1,0:T(8,128)S(1)}, f32[2,1,128,640]{3,2,1,0:T(8,128)S(1)}) fusion(f32[2,4,128,640]{3,2,1,0:T(8,128)S(1)} %get-tuple-element.37, bf16[2,4,128,640]{3,2,1,0:T(8,128)(2,1)} %collective-permute-done.25, ...), kind=kLoop, calls=%fused_computation.15 | loop fusion | flops 2621440 | bytes 7864320 | tf_op jit(solution)/shard_map/add | solution.py:303
  164.4 7.4 %collective-permute-done.27 = bf16[2,128,640]{2,1,0:T(8,128)(2,1)S(1)} collective-permute-done((bf16[2,128,640]{2,1,0:T(8,128)(2,1)S(1)}, bf16[2,128,640]{2,1,0:T(8,128)(2,1)S(1)}, u32[]{:S(2)}, u32[]{:S(2)}) %collective-permute-start.27) | collective-permute-done | bytes 327712 | tf_op jit(solution)/shard_map/ppermute | solution.py:223
  171.8 6.2 %collective-permute-done.28 = bf16[2,128,640]{2,1,0:T(8,128)(2,1)S(1)} collective-permute-done((bf16[2,128,640]{2,1,0:T(8,128)(2,1)S(1)}, bf16[2,128,640]{2,1,0:T(8,128)(2,1)S(1)}, u32[]{:S(2)}, u32[]{:S(2)}) %collective-permute-start.28) | collective-permute-done | bytes 327712 | tf_op jit(solution)/shard_map/ppermute | solution.py:223
  (175 shorter events, 55.2 us)
Async XLA Ops:
  2.3 35.8 %collective-permute-start.10 = (bf16[2,128,640]{2,1,0:T(8,128)(2,1)S(1)}, bf16[2,128,640]{2,1,0:T(8,128)(2,1)S(1)}, u32[]{:S(2)}, u32[]{:S(2)}) collective-permute-start(bf16[2,128,640]{2,1,0:T(8,128)(2,1)S(1)} %pad_maximum_fusion.10.refs_8_), channel_id=1, source_target_pairs={{8,0},{16,8},{24,16},{9,1},{17,9},{25,17},{10,2},{18,10},{26,18},{... | collective-permute-start | bytes 983048 | tf_op jit(solution)/shard_map/ppermute | solution.py:226
  3.8 35.8 %collective-permute-start.3 = (bf16[2,128,640]{2,1,0:T(8,128)(2,1)S(1)}, bf16[2,128,640]{2,1,0:T(8,128)(2,1)S(1)}, u32[]{:S(2)}, u32[]{:S(2)}) collective-permute-start(bf16[2,128,640]{2,1,0:T(8,128)(2,1)S(1)} %pad_maximum_fusion.10.refs_8_), channel_id=1, source_target_pairs={{0,8},{8,16},{16,24},{1,9},{9,17},{17,25},{2,10},{10,18},{18,26},{... | collective-permute-start | bytes 983048 | tf_op jit(solution)/shard_map/ppermute | solution.py:226
  26.9 9.7 %collective-permute-start.6 = (bf16[2,128,640]{2,1,0:T(8,128)(2,1)S(1)}, bf16[2,128,640]{2,1,0:T(8,128)(2,1)S(1)}, u32[]{:S(2)}, u32[]{:S(2)}) collective-permute-start(bf16[2,128,640]{2,1,0:T(8,128)(2,1)S(1)} %pad_maximum_fusion.12), channel_id=1, source_target_pairs={{0,4},{2,6},{4,0},{6,2},{1,5},{3,7},{5,1},{7,3},{8,12},{10,14},{12... | collective-permute-start | bytes 983048 | tf_op jit(solution)/shard_map/ppermute | solution.py:223
  28.5 9.6 %collective-permute-start.4 = (bf16[2,128,640]{2,1,0:T(8,128)(2,1)S(1)}, bf16[2,128,640]{2,1,0:T(8,128)(2,1)S(1)}, u32[]{:S(2)}, u32[]{:S(2)}) collective-permute-start(bf16[2,128,640]{2,1,0:T(8,128)(2,1)S(1)} %pad_maximum_fusion.11), channel_id=1, source_target_pairs={{0,2},{2,0},{4,6},{6,4},{1,3},{3,1},{5,7},{7,5},{8,10},{10,8},{12,... | collective-permute-start | bytes 983048 | tf_op jit(solution)/shard_map/ppermute | solution.py:223
  35.9 10.0 %collective-permute-start.8 = (bf16[2,128,640]{2,1,0:T(8,128)(2,1)S(1)}, bf16[2,128,640]{2,1,0:T(8,128)(2,1)S(1)}, u32[]{:S(2)}, u32[]{:S(2)}) collective-permute-start(bf16[2,128,640]{2,1,0:T(8,128)(2,1)S(1)} %pad_maximum_fusion.13), channel_id=1, source_target_pairs={{0,6},{2,4},{4,2},{6,0},{1,7},{3,5},{5,3},{7,1},{8,14},{10,12},{12... | collective-permute-start | bytes 983048 | tf_op jit(solution)/shard_map/ppermute | solution.py:223
  36.7 16.1 %collective-permute-start.1 = (bf16[2,128,640]{2,1,0:T(8,128)(2,1)S(1)}, bf16[2,128,640]{2,1,0:T(8,128)(2,1)S(1)}, u32[]{:S(2)}, u32[]{:S(2)}) collective-permute-start(bf16[2,128,640]{2,1,0:T(8,128)(2,1)S(1)} %pad_maximum_fusion.8), channel_id=1, source_target_pairs={{0,4},{2,6},{4,0},{6,2},{1,5},{3,7},{5,1},{7,3},{8,12},{10,14},{12... | collective-permute-start | bytes 983048 | tf_op jit(solution)/shard_map/ppermute | solution.py:223
  38.1 16.7 %collective-permute-start = (bf16[2,128,640]{2,1,0:T(8,128)(2,1)S(1)}, bf16[2,128,640]{2,1,0:T(8,128)(2,1)S(1)}, u32[]{:S(2)}, u32[]{:S(2)}) collective-permute-start(bf16[2,128,640]{2,1,0:T(8,128)(2,1)S(1)} %pad_maximum_fusion.7), channel_id=1, source_target_pairs={{0,2},{2,0},{4,6},{6,4},{1,3},{3,1},{5,7},{7,5},{8,10},{10,8},{12,... | collective-permute-start | bytes 983048 | tf_op jit(solution)/shard_map/ppermute | solution.py:223
  38.9 21.5 %collective-permute-start.2 = (bf16[2,128,640]{2,1,0:T(8,128)(2,1)S(1)}, bf16[2,128,640]{2,1,0:T(8,128)(2,1)S(1)}, u32[]{:S(2)}, u32[]{:S(2)}) collective-permute-start(bf16[2,128,640]{2,1,0:T(8,128)(2,1)S(1)} %pad_maximum_fusion.9), channel_id=1, source_target_pairs={{0,6},{2,4},{4,2},{6,0},{1,7},{3,5},{5,3},{7,1},{8,14},{10,12},{12... | collective-permute-start | bytes 983048 | tf_op jit(solution)/shard_map/ppermute | solution.py:223
  40.3 22.1 %collective-permute-start.12 = (bf16[2,128,640]{2,1,0:T(8,128)(2,1)S(1)}, bf16[2,128,640]{2,1,0:T(8,128)(2,1)S(1)}, u32[]{:S(2)}, u32[]{:S(2)}) collective-permute-start(bf16[2,128,640]{2,1,0:T(8,128)(2,1)S(1)} %collective-permute-done.6.refs_10_), channel_id=1, source_target_pairs={{8,0},{16,8},{24,16},{9,1},{17,9},{25,17},{10,2},{18,10},{26,18},{... | collective-permute-start | bytes 983048 | tf_op jit(solution)/shard_map/ppermute | solution.py:226
  45.9 24.2 %collective-permute-start.7 = (bf16[2,128,640]{2,1,0:T(8,128)(2,1)S(1)}, bf16[2,128,640]{2,1,0:T(8,128)(2,1)S(1)}, u32[]{:S(2)}, u32[]{:S(2)}) collective-permute-start(bf16[2,128,640]{2,1,0:T(8,128)(2,1)S(1)} %collective-permute-done.6.refs_10_), channel_id=1, source_target_pairs={{0,8},{8,16},{16,24},{1,9},{9,17},{17,25},{2,10},{10,18},{18,26},{... | collective-permute-start | bytes 983048 | tf_op jit(solution)/shard_map/ppermute | solution.py:226
  53.5 17.4 %collective-permute-start.11 = (bf16[2,128,640]{2,1,0:T(8,128)(2,1)S(1)}, bf16[2,128,640]{2,1,0:T(8,128)(2,1)S(1)}, u32[]{:S(2)}, u32[]{:S(2)}) collective-permute-start(bf16[2,128,640]{2,1,0:T(8,128)(2,1)S(1)} %collective-permute-done.4.refs_9_), channel_id=1, source_target_pairs={{8,0},{16,8},{24,16},{9,1},{17,9},{25,17},{10,2},{18,10},{26,18},{... | collective-permute-start | bytes 983048 | tf_op jit(solution)/shard_map/ppermute | solution.py:226
  55.5 16.1 %collective-permute-start.5 = (bf16[2,128,640]{2,1,0:T(8,128)(2,1)S(1)}, bf16[2,128,640]{2,1,0:T(8,128)(2,1)S(1)}, u32[]{:S(2)}, u32[]{:S(2)}) collective-permute-start(bf16[2,128,640]{2,1,0:T(8,128)(2,1)S(1)} %collective-permute-done.4.refs_9_), channel_id=1, source_target_pairs={{0,8},{8,16},{16,24},{1,9},{9,17},{17,25},{2,10},{10,18},{18,26},{... | collective-permute-start | bytes 983048 | tf_op jit(solution)/shard_map/ppermute | solution.py:226
  61.1 11.7 %collective-permute-start.13 = (bf16[2,128,640]{2,1,0:T(8,128)(2,1)S(1)}, bf16[2,128,640]{2,1,0:T(8,128)(2,1)S(1)}, u32[]{:S(2)}, u32[]{:S(2)}) collective-permute-start(bf16[2,128,640]{2,1,0:T(8,128)(2,1)S(1)} %collective-permute-done.8.refs_11_), channel_id=1, source_target_pairs={{8,0},{16,8},{24,16},{9,1},{17,9},{25,17},{10,2},{18,10},{26,18},{... | collective-permute-start | bytes 983048 | tf_op jit(solution)/shard_map/ppermute | solution.py:226
  63.1 11.6 %collective-permute-start.9 = (bf16[2,128,640]{2,1,0:T(8,128)(2,1)S(1)}, bf16[2,128,640]{2,1,0:T(8,128)(2,1)S(1)}, u32[]{:S(2)}, u32[]{:S(2)}) collective-permute-start(bf16[2,128,640]{2,1,0:T(8,128)(2,1)S(1)} %collective-permute-done.8.refs_11_), channel_id=1, source_target_pairs={{0,8},{8,16},{16,24},{1,9},{9,17},{17,25},{2,10},{10,18},{18,26},{... | collective-permute-start | bytes 983048 | tf_op jit(solution)/shard_map/ppermute | solution.py:226
  115.5 7.7 %collective-permute-start.20 = (f32[4,128]{1,0:T(4,128)S(1)}, f32[4,128]{1,0:T(4,128)S(1)}, u32[]{:S(2)}, u32[]{:S(2)}) collective-permute-start(f32[4,128]{1,0:T(4,128)S(1)} %get-tuple-element.75), channel_id=1, source_target_pairs={{0,8},{8,16},{16,24},{1,9},{9,17},{17,25},{2,10},{10,18},{18,26},{... | collective-permute-start | bytes 6152 | tf_op jit(solution)/shard_map/ppermute | solution.py:226
  121.3 24.6 %collective-permute-start.16 = (bf16[128,640]{1,0:T(8,128)(2,1)}, bf16[128,640]{1,0:T(8,128)(2,1)S(1)}, u32[]{:S(2)}, u32[]{:S(2)}) collective-permute-start(bf16[128,640]{1,0:T(8,128)(2,1)} %get-tuple-element.29), channel_id=1, source_target_pairs={{0,2},{2,0},{4,6},{6,4},{1,3},{3,1},{5,7},{7,5},{8,10},{10,8},{12,... | collective-permute-start | bytes 491528 | tf_op jit(solution)/shard_map/ppermute | solution.py:223
  121.4 24.8 %collective-permute-start.17 = (bf16[128,640]{1,0:T(8,128)(2,1)}, bf16[128,640]{1,0:T(8,128)(2,1)S(1)}, u32[]{:S(2)}, u32[]{:S(2)}) collective-permute-start(bf16[128,640]{1,0:T(8,128)(2,1)} %get-tuple-element.30), channel_id=1, source_target_pairs={{0,4},{2,6},{4,0},{6,2},{1,5},{3,7},{5,1},{7,3},{8,12},{10,14},{12... | collective-permute-start | bytes 491528 | tf_op jit(solution)/shard_map/ppermute | solution.py:223
  122.5 24.7 %collective-permute-start.18 = (bf16[128,640]{1,0:T(8,128)(2,1)}, bf16[128,640]{1,0:T(8,128)(2,1)}, u32[]{:S(2)}, u32[]{:S(2)}) collective-permute-start(bf16[128,640]{1,0:T(8,128)(2,1)} %get-tuple-element.31), channel_id=1, source_target_pairs={{0,6},{2,4},{4,2},{6,0},{1,7},{3,5},{5,3},{7,1},{8,14},{10,12},{12... | collective-permute-start | bytes 491528 | tf_op jit(solution)/shard_map/ppermute | solution.py:223
  123.2 34.1 %collective-permute-start.24 = (bf16[2,4,128,640]{3,2,1,0:T(8,128)(2,1)}, bf16[2,4,128,640]{3,2,1,0:T(8,128)(2,1)}, u32[]{:S(2)}, u32[]{:S(2)}) collective-permute-start(bf16[2,4,128,640]{3,2,1,0:T(8,128)(2,1)} %get-tuple-element.38), channel_id=1, source_target_pairs={{8,0},{16,8},{24,16},{9,1},{17,9},{25,17},{10,2},{18,10},{26,18},{... | collective-permute-start | bytes 3932168 | tf_op jit(solution)/shard_map/ppermute | solution.py:226
  125.4 33.1 %collective-permute-start.25 = (bf16[2,4,128,640]{3,2,1,0:T(8,128)(2,1)}, bf16[2,4,128,640]{3,2,1,0:T(8,128)(2,1)}, u32[]{:S(2)}, u32[]{:S(2)}) collective-permute-start(bf16[2,4,128,640]{3,2,1,0:T(8,128)(2,1)} %get-tuple-element.39), channel_id=1, source_target_pairs={{0,8},{8,16},{16,24},{1,9},{9,17},{17,25},{2,10},{10,18},{18,26},{... | collective-permute-start | bytes 3932168 | tf_op jit(solution)/shard_map/ppermute | solution.py:226
  146.2 7.0 %collective-permute-start.22 = (bf16[128,640]{1,0:T(8,128)(2,1)S(1)}, bf16[128,640]{1,0:T(8,128)(2,1)S(1)}, u32[]{:S(2)}, u32[]{:S(2)}) collective-permute-start(bf16[128,640]{1,0:T(8,128)(2,1)S(1)} %get-tuple-element.100), channel_id=1, source_target_pairs={{0,4},{2,6},{4,0},{6,2},{1,5},{3,7},{5,1},{7,3},{8,12},{10,14},{12... | collective-permute-start | bytes 491528 | tf_op jit(solution)/shard_map/ppermute | solution.py:223
  147.2 8.4 %collective-permute-start.23 = (bf16[128,640]{1,0:T(8,128)(2,1)S(1)}, bf16[128,640]{1,0:T(8,128)(2,1)S(1)}, u32[]{:S(2)}, u32[]{:S(2)}) collective-permute-start(bf16[128,640]{1,0:T(8,128)(2,1)S(1)} %get-tuple-element.101), channel_id=1, source_target_pairs={{0,6},{2,4},{4,2},{6,0},{1,7},{3,5},{5,3},{7,1},{8,14},{10,12},{12... | collective-permute-start | bytes 491528 | tf_op jit(solution)/shard_map/ppermute | solution.py:223
  161.2 10.6 %collective-permute-start.27 = (bf16[2,128,640]{2,1,0:T(8,128)(2,1)S(1)}, bf16[2,128,640]{2,1,0:T(8,128)(2,1)S(1)}, u32[]{:S(2)}, u32[]{:S(2)}) collective-permute-start(bf16[2,128,640]{2,1,0:T(8,128)(2,1)S(1)} %pad_maximum_fusion.15), channel_id=1, source_target_pairs={{0,4},{2,6},{4,0},{6,2},{1,5},{3,7},{5,1},{7,3},{8,12},{10,14},{12... | collective-permute-start | bytes 983048 | tf_op jit(solution)/shard_map/ppermute | solution.py:223
  162.4 15.6 %collective-permute-start.28 = (bf16[2,128,640]{2,1,0:T(8,128)(2,1)S(1)}, bf16[2,128,640]{2,1,0:T(8,128)(2,1)S(1)}, u32[]{:S(2)}, u32[]{:S(2)}) collective-permute-start(bf16[2,128,640]{2,1,0:T(8,128)(2,1)S(1)} %pad_maximum_fusion.16), channel_id=1, source_target_pairs={{0,6},{2,4},{4,2},{6,0},{1,7},{3,5},{5,3},{7,1},{8,14},{10,12},{12... | collective-permute-start | bytes 983048 | tf_op jit(solution)/shard_map/ppermute | solution.py:223
  (43 other events, 163.3 us)
where the time goes:
time: 182 us; the launch traced here: 180 us
  starting transfers between devices  51.2 us (28%)
  waiting for transfers between devices  33.8 us (19%)
  local copies, waits for them, and re-layouts  31.8 us (17%)
  blocking collectives  27 us (15%)
  Pallas kernels  24.3 us (13%)
  other arithmetic  9.61 us (5%)
  between operations  1.93 us (1%)
    ppermute x14, starting transfers between devices, moved(): lax.ppermute(x, 'block', [(i, i + by) for i in range(blocks) if 0 <= i +...  41.6 us
    ppermute x15, waiting for transfers between devices, swap(): lax.ppermute(x, 'place', [(i, i ^ m) for i in range(group)])  27 us
    unnamed x78, local copies, waits for them, and re-layouts  24.7 us
    pallas_call x1, Pallas kernels, attention(): pl.pallas_call(functools.partial(attend, group=group, offsets=offsets, di...  24.3 us
    psum x1, blocking collectives, local(): lax.psum(jnp.where((slots == r)[:, None, None], mine[None], 0.0), ('place...  14.3 us
    psum x1, blocking collectives, local(): lax.psum(jnp.stack([inner[:group], key_inner]), ('place', 'head'))  12.7 us
    ppermute x15, starting transfers between devices, swap(): lax.ppermute(x, 'place', [(i, i ^ m) for i in range(group)])  9.61 us
    ppermute x14, waiting for transfers between devices, moved(): lax.ppermute(x, 'block', [(i, i + by) for i in range(blocks) if 0 <= i +...  6.78 us
  transfers between devices with their start and end apart: 29, of which 14 were waited for; matrix products, arithmetic and copies ran while one was open for 6% of the time, Pallas kernels for 0%

commit v1 on v0

v1 whole, which is shorter than its diff:
```python
import functools

import jax
import jax.numpy as jnp
import numpy as np
from jax import lax
from jax.experimental import pallas as pl
from jax.experimental.pallas import tpu as pltpu
from jax.sharding import Mesh
from jax.sharding import PartitionSpec as P

DIM = 5120
HEAD = 128
TAIL = 16
epsilon = 1e-06
lowest = -1e30
LOG2E = 1.4426950408889634
SCALE = HEAD ** (-0.5)
bf16 = jnp.bfloat16
f32 = jnp.float32
WIDE = pltpu.CompilerParams(vmem_limit_bytes=60 * 2**20)


def offset_list(levels):
    result = [0]
    for height in range(levels):
        result = result + [2**height, -(2**height)]
    return result


class Plan:
    def __init__(self, spans, heads_here):
        levels = spans.bit_length() - 2
        reach = 2 ** (levels - 1)
        whole = heads_here % reach == 0 and spans % reach == 0
        self.group = reach if whole else 1
        self.offsets = sorted(offset_list(levels), reverse=True)
        self.distances = [-1, 0, 1] if self.group > 1 else sorted(self.offsets)
        self.home = self.distances.index(0)
        self.heads = heads_here // self.group
        self.chunks = CHUNKS(self.heads)
        if self.group > 1:
            self.slots = [[self.group + s - o for o in self.offsets] for s in range(self.group)]
        else:
            self.slots = [[self.distances.index(-o) for o in self.offsets]]


def CHUNKS(heads):
    return [(0, heads)]


def dot(a, b, ca, cb):
    return lax.dot_general(a, b, (((ca,), (cb,)), ((), ())), preferred_element_type=f32)


def attend(place, *refs, plan):
    group, nd, noff = plan.group, len(plan.distances), len(plan.offsets)
    it = iter(refs)
    qd = [next(it) for _ in range(group)]
    kv = [[next(it) for _ in range(group)] for _ in range(nd)]
    out_oq = [next(it) for _ in range(group)]
    out_kv = [next(it) for _ in range(nd)]
    keys, vals, queries, grads, weights, scored, outs, dqs, allow = (next(it) for _ in range(9))
    r = place[0]

    def rows(slot):
        if isinstance(slot, int):
            return pl.ds(slot * HEAD, HEAD)
        return pl.ds(pl.multiple_of(slot * HEAD, HEAD), HEAD)

    for m in range(group):
        at = rows(m ^ r)
        queries[at, :] = qd[m][0:HEAD]
        grads[at, :] = qd[m][HEAD : 2 * HEAD]
        allow[m ^ r] = qd[m][2 * HEAD : 2 * HEAD + TAIL].astype(f32)
        for d in range(nd):
            at = rows(d * group + (m ^ r))
            keys[at, :] = kv[d][m][0]
            vals[at, :] = kv[d][m][1]

    for s in range(group):
        q = queries[rows(s), :]
        g = grads[rows(s), :]
        k = jnp.concatenate([keys[rows(x), :] for x in plan.slots[s]], axis=0)
        v = jnp.concatenate([vals[rows(x), :] for x in plan.slots[s]], axis=0)
        bias = jnp.concatenate([allow[s, j : j + 1, :] for j in range(noff)], axis=1)
        scores = dot(q, k, 1, 1) * (SCALE * LOG2E) + bias
        top = jnp.max(scores, axis=1, keepdims=True)
        e = jnp.exp2(scores - top)
        p = e * (1.0 / jnp.sum(e, axis=1, keepdims=True))
        p_low = p.astype(bf16)
        o = dot(p_low, v, 1, 0).astype(bf16)
        delta = jnp.sum(g.astype(f32) * o.astype(f32), axis=1, keepdims=True)
        ds = (p * SCALE * (dot(g, v, 1, 1) - delta)).astype(bf16)
        weights[rows(s), :] = p_low
        scored[rows(s), :] = ds
        outs[rows(s), :] = o
        dqs[rows(s), :] = dot(ds, k, 1, 0).astype(bf16)

    for m in range(group):
        out_oq[m][0] = outs[rows(m ^ r), :]
        out_oq[m][1] = dqs[rows(m ^ r), :]

    for d in range(nd):
        for s in range(group):
            users = [
                (t, j)
                for t in range(group)
                for j in range(noff)
                if plan.slots[t][j] == d * group + s
            ]

            def stacked(ref):
                return jnp.concatenate([ref[rows(t), rows(j)] for t, j in users], axis=0)

            q = jnp.concatenate([queries[rows(t), :] for t, _ in users], axis=0)
            g = jnp.concatenate([grads[rows(t), :] for t, _ in users], axis=0)
            out_kv[d][s ^ r, 1] = dot(stacked(scored), q, 0, 0).astype(out_kv[d].dtype)
            out_kv[d][s ^ r, 0] = dot(stacked(weights), g, 0, 0).astype(out_kv[d].dtype)


def attention(place, qd, kv, plan):
    width = qd[0].shape[1]
    heads = width // HEAD
    group, nd, noff = plan.group, len(plan.distances), len(plan.offsets)
    ng = nd * group
    query = pl.BlockSpec((2 * HEAD + TAIL, HEAD), lambda h, _: (0, h))
    pair = pl.BlockSpec((2, HEAD, HEAD), lambda h, _: (0, 0, h))
    grads = pl.BlockSpec((group, 2, HEAD, HEAD), lambda h, _: (0, 0, 0, h))
    outs = [jax.ShapeDtypeStruct((2, HEAD, width), bf16)] * group + [
        jax.ShapeDtypeStruct((group, 2, HEAD, width), f32 if by == 0 else bf16)
        for by in plan.distances
    ]
    work = heads * group * noff * 6 * 2 * HEAD**3
    result = pl.pallas_call(
        functools.partial(attend, plan=plan),
        grid_spec=pltpu.PrefetchScalarGridSpec(
            num_scalar_prefetch=1,
            grid=(heads,),
            in_specs=[query] * group + [pair] * ng,
            out_specs=[pair] * group + [grads] * nd,
            scratch_shapes=[pltpu.VMEM((ng * HEAD, HEAD), bf16)] * 2
            + [pltpu.VMEM((group * HEAD, HEAD), bf16)] * 2
            + [pltpu.VMEM((group * HEAD, noff * HEAD), bf16)] * 2
            + [pltpu.VMEM((group * HEAD, HEAD), bf16)] * 2
            + [pltpu.VMEM((group, TAIL, HEAD), f32)],
        ),
        out_shape=outs,
        compiler_params=WIDE,
        cost_estimate=pl.CostEstimate(
            flops=work, bytes_accessed=2 * heads * 2**20, transcendentals=work // 1536
        ),
        name="attend",
    )(place, *qd, *[piece for block in kv for piece in block])
    return result[:group], result[group:]


def split(place, a_ref, b_ref, rstd_ref, gain_ref, *refs, plan, allowed):
    r = place[0]
    width = plan.heads * HEAD
    outs = iter(refs[allowed:])
    for first, count in plan.chunks:
        for m in range(plan.group):
            at = pl.ds(pl.multiple_of((m ^ r) * width + first * HEAD, HEAD), count * HEAD)
            a = (a_ref[:, at].astype(f32) * rstd_ref[:, 0:1] * gain_ref[:, at]).astype(bf16)
            out = next(outs)
            if allowed:
                out[0:HEAD, :] = a
                out[HEAD : 2 * HEAD, :] = b_ref[:, at]
                for h in range(count):
                    out[2 * HEAD : 2 * HEAD + TAIL, h * HEAD : (h + 1) * HEAD] = refs[0][...]
            else:
                out[0] = a
                out[1] = b_ref[:, at]


def pieces_of(place, a, b, rstd, gain, allow, plan):
    shapes = [
        jax.ShapeDtypeStruct(
            (2, HEAD, count * HEAD) if allow is None else (2 * HEAD + TAIL, count * HEAD), bf16
        )
        for _, count in plan.chunks
        for _ in range(plan.group)
    ]
    args = [a, b, rstd, gain] + ([] if allow is None else [allow])
    whole = pl.BlockSpec(memory_space=pltpu.VMEM)
    result = pl.pallas_call(
        functools.partial(split, plan=plan, allowed=allow is not None),
        grid_spec=pltpu.PrefetchScalarGridSpec(
            num_scalar_prefetch=1,
            grid=(),
            in_specs=[whole] * len(args),
            out_specs=[whole] * len(shapes),
        ),
        out_shape=shapes,
        compiler_params=pltpu.CompilerParams(vmem_limit_bytes=24 * 2**20),
        name="split",
    )(place, *args)
    return [
        result[c * plan.group : (c + 1) * plan.group] for c in range(len(plan.chunks))
    ]


def join(place, *refs, plan):
    group = plan.group
    count = len(plan.chunks) * group
    parts = refs[:count]
    raw_ref, rstd_ref, gain_ref, plain, normed, inner = refs[count:]
    r = place[0]
    width = plan.heads * HEAD
    total = jnp.zeros((HEAD, HEAD), f32)
    for c, (first, heads) in enumerate(plan.chunks):
        for m in range(group):
            base = (m ^ r) * width + first * HEAD
            part = parts[c * group + m]
            for h in range(heads):
                at = pl.ds(pl.multiple_of(base + h * HEAD, HEAD), HEAD)
                here = slice(h * HEAD, (h + 1) * HEAD)
                plain[:, at] = part[0, :, here]
                low = part[1, :, here]
                normed[:, at] = low
                total += low.astype(f32) * gain_ref[:, at] * raw_ref[:, at].astype(f32)
    inner[...] = jnp.broadcast_to(
        jnp.sum(total, axis=1, keepdims=True) * rstd_ref[:, 0:1], (HEAD, HEAD)
    )


def joined(place, parts, raw, rstd, gain, plan):
    shape = raw.shape
    flat = [x for chunk in parts for x in chunk]
    whole = pl.BlockSpec(memory_space=pltpu.VMEM)
    return pl.pallas_call(
        functools.partial(join, plan=plan),
        grid_spec=pltpu.PrefetchScalarGridSpec(
            num_scalar_prefetch=1,
            grid=(),
            in_specs=[whole] * (len(flat) + 3),
            out_specs=[whole] * 3,
        ),
        out_shape=[
            jax.ShapeDtypeStruct(shape, bf16),
            jax.ShapeDtypeStruct(shape, bf16),
            jax.ShapeDtypeStruct((HEAD, HEAD), f32),
        ],
        compiler_params=pltpu.CompilerParams(vmem_limit_bytes=24 * 2**20),
        name="join",
    )(place, *flat, raw, rstd, gain)


def local(
    query_vectors,
    key_vectors,
    value_vectors,
    output_grad,
    query_gain,
    key_gain,
    block_pairs,
    pair_counts,
    *,
    plan,
):
    row_count, col_count = query_vectors.shape
    group, offsets, distances = plan.group, plan.offsets, plan.distances
    features = col_count * lax.axis_size("head")
    blocks = lax.axis_size("block")
    r = lax.axis_index("place")
    place = jnp.reshape(r, (1,)).astype(jnp.int32)

    def swap(x, m):
        return lax.ppermute(x, "place", [(i, i ^ m) for i in range(group)]) if m else x

    def moved(x, by):
        if by == 0:
            return x
        return lax.ppermute(
            x, "block", [(i, i + by) for i in range(blocks) if 0 <= i + by < blocks]
        )

    def summed(x):
        step, count = 1, lax.axis_size("head")
        while step < count:
            x = x + lax.ppermute(x, "head", [(i, i ^ step) for i in range(count)])
            step *= 2
        return x

    query_float = query_vectors.astype(f32)
    key_float = key_vectors.astype(f32)
    squares = summed(
        jnp.stack(
            [jnp.sum(key_float * key_float, axis=1), jnp.sum(query_float * query_float, axis=1)]
        )
    )
    rstd = jnp.broadcast_to(
        lax.rsqrt(squares / features + epsilon)[:, :, None], (2, row_count, HEAD)
    )
    query_gain = query_gain[None, :]
    key_gain = key_gain[None, :]

    kv_home = pieces_of(place, key_vectors, value_vectors, rstd[0], key_gain, None, plan)
    kv_all = []
    for pieces in kv_home:
        mine = [swap(x, m) for m, x in enumerate(pieces)]
        kv_all.append([[moved(x, -by) for x in mine] for by in distances])

    live = jnp.arange(block_pairs.shape[1], dtype=jnp.int32) < pair_counts[0]
    steps = block_pairs[0, :, 0] - block_pairs[0, :, 1]
    wanted = jnp.array(offsets, jnp.int32)
    flags = jnp.any(live[:, None] & (steps[:, None] == wanted[None, :]), axis=0)
    bias = jnp.pad(jnp.where(flags, 0.0, lowest), (0, TAIL - len(offsets)))
    allow = jnp.broadcast_to(bias[:, None], (TAIL, HEAD)).astype(bf16)

    query_late, grad_late, *_ = lax.optimization_barrier(
        (query_vectors, output_grad, *[block[0] for block in kv_all[0]])
    )
    qd_home = pieces_of(place, query_late, grad_late, rstd[1], query_gain, allow, plan)

    oq_back, kv_back = [], []
    for c in range(len(plan.chunks)):
        qd = [swap(x, m) for m, x in enumerate(qd_home[c])]
        oq_parts, kv_parts = attention(place, qd, kv_all[c], plan)
        oq_back.append([swap(x, m) for m, x in enumerate(oq_parts)])
        back = [moved(kv_parts[d], by) for d, by in enumerate(distances) if by]
        total = []
        for m in range(group):
            x = kv_parts[plan.home][m]
            for y in back:
                x = x + y[m].astype(f32)
            total.append(swap(x.astype(bf16), m))
        kv_back.append(total)

    attended, query_norm_grad, query_inner = joined(
        place, oq_back, query_vectors, rstd[1], query_gain, plan
    )
    value_grad, key_norm_grad, key_inner = joined(
        place, kv_back, key_vectors, rstd[0], key_gain, plan
    )

    def finished(raw, rstd_wide, gain, grad, inner):
        inner = summed(inner[:, 0])[:, None] / features
        rstd_col = rstd_wide[:, 0:1]
        unit = raw.astype(f32) * rstd_col
        return (rstd_col * (gain * grad.astype(f32) - unit * inner)).astype(bf16)

    query_grad = finished(query_vectors, rstd[1], query_gain, query_norm_grad, query_inner)
    key_grad = finished(key_vectors, rstd[0], key_gain, key_norm_grad, key_inner)
    return (attended, query_grad, key_grad, value_grad)


def solution(mesh):
    spans, head_groups = mesh.devices.shape
    plan = Plan(spans, DIM // HEAD // head_groups)
    blocks = Mesh(
        mesh.devices.reshape(spans // plan.group, plan.group, head_groups),
        ("block", "place", "head"),
    )
    ctx = ("block", "place")
    placed = (
        P(ctx, "head"),
        P(ctx, "head"),
        P(ctx, "head"),
        P(ctx, "head"),
        P("head"),
        P("head"),
        P(ctx, None, None),
        P(ctx),
    )
    return jax.shard_map(
        functools.partial(local, plan=plan),
        mesh=blocks,
        in_specs=placed,
        out_specs=(P(ctx, "head"),) * 4,
        check_vma=False,
    )
```

time: 182 us -> 137 us (0.75); the launches traced: 180 us -> 137 us
  blocking collectives: 27 us -> 0 us
  local copies, waits for them, and re-layouts: 31.8 us -> 5.52 us
  waiting for transfers between devices: 33.8 us -> 55.5 us
  starting transfers between devices: 51.2 us -> 42.7 us
  other arithmetic: 9.61 us -> 7.68 us
    psum x2 -> x0, blocking collectives: 27 us -> none  [the longest x1 14.3 us: local(): lax.psum(jnp.where((slots == r)[:, None, None], mine[None], 0.0), ('place...]
    unnamed x78 -> x50, local copies, waits for them, and re-layouts: 24.7 us -> 5.07 us
    ppermute x14 -> x10, starting transfers between devices: 41.6 us -> 28.6 us  [moved(): lax.ppermute(x, 'block', [(i, i + by) for i in range(blocks) if 0 <= i +...]
    ppermute x14 -> x10, waiting for transfers between devices: 6.78 us -> 16.5 us  [moved(): lax.ppermute(x, 'block', [(i, i + by) for i in range(blocks) if 0 <= i +...]
    ppermute x15 -> x12, waiting for transfers between devices: 27 us -> 35.4 us  [swap(): lax.ppermute(x, 'place', [(i, i ^ m) for i in range(group)])]
    ppermute x0 -> x3, starting transfers between devices: none -> 6.25 us  [summed(): x = x + lax.ppermute(x, 'head', [(i, i ^ step) for i in range(count)])]
    another operation x20 -> x2, other arithmetic: 4.7 us -> 0.02 us  [the longest x1 0.01 us: local(): jnp.stack([jnp.sum(key_float * key_float, axis=1), jnp.sum(query_float *...]
    convert_element_type x1 -> x3, other arithmetic: 0.27 us -> 4.84 us  [the longest x2 2.56 us: finished(): return (rstd_col * (gain * grad.astype(f32) - unit * inner)).astype(bf16)]
  transfers between devices with their start and end apart: 29 -> 25, of which waited for: 14 -> 14; matrix products, arithmetic and copies ran while one was open for 6% -> 1% of each run, Pallas kernels for 0% -> 1%
where the time goes in v1:
time: 137 us
  waiting for transfers between devices  55.5 us (41%)
  starting transfers between devices  42.7 us (31%)
  Pallas kernels  23.6 us (17%)
  other arithmetic  7.68 us (6%)
  local copies, waits for them, and re-layouts  5.52 us (4%)
  between operations  1.73 us (1%)
    ppermute x12, waiting for transfers between devices, swap(): lax.ppermute(x, 'place', [(i, i ^ m) for i in range(group)])  35.4 us
    ppermute x10, starting transfers between devices, moved(): lax.ppermute(x, 'block', [(i, i + by) for i in range(blocks) if 0 <= i +...  28.6 us
    pallas_call x1, Pallas kernels, attention(): pl.pallas_call(functools.partial(attend, plan=plan), grid_spec=pltpu.Pref...  20.4 us
    ppermute x10, waiting for transfers between devices, moved(): lax.ppermute(x, 'block', [(i, i + by) for i in range(blocks) if 0 <= i +...  16.5 us
    ppermute x12, starting transfers between devices, swap(): lax.ppermute(x, 'place', [(i, i ^ m) for i in range(group)])  7.84 us
    ppermute x3, starting transfers between devices, summed(): x = x + lax.ppermute(x, 'head', [(i, i ^ step) for i in range(count)])  6.25 us
    unnamed x50, local copies, waits for them, and re-layouts  5.07 us
    ppermute x3, waiting for transfers between devices, summed(): x = x + lax.ppermute(x, 'head', [(i, i ^ step) for i in range(count)])  3.56 us
  transfers between devices with their start and end apart: 25, of which 14 were waited for; matrix products, arithmetic and copies ran while one was open for 1% of the time, Pallas kernels for 1%

profile of v1, /device:TPU:0, one launch (start us, length us, event | category | flops | bytes accessed | tf_op | source)
XLA Modules:
  0.0 136.8 jit_solution(3247428862334953460)
XLA Ops:
  0.7 1.4 %fusion.5 = f32[128]{0:T(128)S(1)} fusion(bf16[128,2560]{1,0:T(8,128)(2,1)} %refs_4_.2), kind=kLoop, calls=%fused_computation.9 | loop fusion | flops 982912 | bytes 655872 | tf_op jit(solution)/shard_map/reduce_sum | solution.py:290
  3.4 3.0 %collective-permute-start = (f32[2,128]{1,0:T(2,128)S(1)}, f32[2,128]{1,0:T(2,128)S(1)}, u32[]{:S(2)}, u32[]{:S(2)}) collective-permute-start(f32[2,128]{1,0:T(2,128)S(1)} %pad_maximum_fusion), channel_id=1, source_target_pairs={{0,1},{1,0},{2,3},{3,2},{4,5},{5,4},{6,7},{7,6},{8,9},{9,8},{10,11... | collective-permute-start | bytes 3080 | tf_op jit(solution)/shard_map/ppermute | solution.py:282
  10.7 4.6 %collective-permute-start.1 = (bf16[2,128,640]{2,1,0:T(8,128)(2,1)S(1)}, bf16[2,128,640]{2,1,0:T(8,128)(2,1)S(1)}, u32[]{:S(2)}, u32[]{:S(2)}) collective-permute-start(bf16[2,128,640]{2,1,0:T(8,128)(2,1)S(1)} %get-tuple-element.27.refs_8_), channel_id=1, source_target_pairs={{0,8},{8,16},{16,24},{1,9},{9,17},{17,25},{2,10},{10,18},{18,26},{... | collective-permute-start | bytes 983048 | tf_op jit(solution)/shard_map/ppermute | solution.py:275
  15.5 2.0 %collective-permute-start.8 = (bf16[2,128,640]{2,1,0:T(8,128)(2,1)S(1)}, bf16[2,128,640]{2,1,0:T(8,128)(2,1)S(1)}, u32[]{:S(2)}, u32[]{:S(2)}) collective-permute-start(bf16[2,128,640]{2,1,0:T(8,128)(2,1)S(1)} %get-tuple-element.35), channel_id=1, source_target_pairs={{0,4},{2,6},{4,0},{6,2},{1,5},{3,7},{5,1},{7,3},{8,12},{10,14},{12... | collective-permute-start | bytes 983048 | tf_op jit(solution)/shard_map/ppermute | solution.py:270
  18.9 7.1 %collective-permute-done.8.refs_10_ = bf16[2,128,640]{2,1,0:T(8,128)(2,1)S(1)} collective-permute-done((bf16[2,128,640]{2,1,0:T(8,128)(2,1)S(1)}, bf16[2,128,640]{2,1,0:T(8,128)(2,1)S(1)}, u32[]{:S(2)}, u32[]{:S(2)}) %collective-permute-start.8) | collective-permute-done | bytes 327712 | tf_op jit(solution)/shard_map/ppermute | solution.py:270
  26.0 3.9 %collective-permute-start.7 = (bf16[2,128,640]{2,1,0:T(8,128)(2,1)S(1)}, bf16[2,128,640]{2,1,0:T(8,128)(2,1)S(1)}, u32[]{:S(2)}, u32[]{:S(2)}) collective-permute-start(bf16[2,128,640]{2,1,0:T(8,128)(2,1)S(1)} %collective-permute-done.6.refs_9_), channel_id=1, source_target_pairs={{0,8},{8,16},{16,24},{1,9},{9,17},{17,25},{2,10},{10,18},{18,26},{... | collective-permute-start | bytes 983048 | tf_op jit(solution)/shard_map/ppermute | solution.py:275
  31.3 4.6 %collective-permute-start.9 = (bf16[2,128,640]{2,1,0:T(8,128)(2,1)S(1)}, bf16[2,128,640]{2,1,0:T(8,128)(2,1)S(1)}, u32[]{:S(2)}, u32[]{:S(2)}) collective-permute-start(bf16[2,128,640]{2,1,0:T(8,128)(2,1)S(1)} %collective-permute-done.8.refs_10_), channel_id=1, source_target_pairs={{0,8},{8,16},{16,24},{1,9},{9,17},{17,25},{2,10},{10,18},{18,26},{... | collective-permute-start | bytes 983048 | tf_op jit(solution)/shard_map/ppermute | solution.py:275
  38.0 1.5 %collective-permute-start.4 = (bf16[272,640]{1,0:T(8,128)(2,1)S(1)}, bf16[272,640]{1,0:T(8,128)(2,1)S(1)}, u32[]{:S(2)}, u32[]{:S(2)}) collective-permute-start(bf16[272,640]{1,0:T(8,128)(2,1)S(1)} %get-tuple-element.32), channel_id=1, source_target_pairs={{0,4},{2,6},{4,0},{6,2},{1,5},{3,7},{5,1},{7,3},{8,12},{10,14},{12... | collective-permute-start | bytes 1044488 | tf_op jit(solution)/shard_map/ppermute | solution.py:270
  41.8 1.5 %collective-permute-done.9.refs_6_ = bf16[2,128,640]{2,1,0:T(8,128)(2,1)S(1)} collective-permute-done((bf16[2,128,640]{2,1,0:T(8,128)(2,1)S(1)}, bf16[2,128,640]{2,1,0:T(8,128)(2,1)S(1)}, u32[]{:S(2)}, u32[]{:S(2)}) %collective-permute-start.9) | collective-permute-done | bytes 327712 | tf_op jit(solution)/shard_map/ppermute | solution.py:275
  43.3 4.4 %collective-permute-start.11 = (bf16[2,128,640]{2,1,0:T(8,128)(2,1)S(1)}, bf16[2,128,640]{2,1,0:T(8,128)(2,1)S(1)}, u32[]{:S(2)}, u32[]{:S(2)}) collective-permute-start(bf16[2,128,640]{2,1,0:T(8,128)(2,1)S(1)} %collective-permute-done.10.refs_11_), channel_id=1, source_target_pairs={{0,8},{8,16},{16,24},{1,9},{9,17},{17,25},{2,10},{10,18},{18,26},{... | collective-permute-start | bytes 983048 | tf_op jit(solution)/shard_map/ppermute | solution.py:275
  47.7 4.8 %collective-permute-done.14.refs_15_ = bf16[2,128,640]{2,1,0:T(8,128)(2,1)S(1)} collective-permute-done((bf16[2,128,640]{2,1,0:T(8,128)(2,1)S(1)}, bf16[2,128,640]{2,1,0:T(8,128)(2,1)S(1)}, u32[]{:S(2)}, u32[]{:S(2)}) %collective-permute-start.14) | collective-permute-done | bytes 327712 | tf_op jit(solution)/shard_map/ppermute | solution.py:275
  53.7 1.8 %collective-permute-done.5.refs_3_ = bf16[272,640]{1,0:T(8,128)(2,1)S(1)} collective-permute-done((bf16[272,640]{1,0:T(8,128)(2,1)S(1)}, bf16[272,640]{1,0:T(8,128)(2,1)S(1)}, u32[]{:S(2)}, u32[]{:S(2)}) %collective-permute-start.5) | collective-permute-done | bytes 348192 | tf_op jit(solution)/shard_map/ppermute | solution.py:270
  56.2 20.4 %attend.1 = (bf16[2,128,640]{2,1,0:T(8,128)(2,1)}, bf16[2,128,640]{2,1,0:T(8,128)(2,1)}, bf16[2,128,640]{2,1,0:T(8,128)(2,1)}, bf16[2,128,640]{2,1,0:T(8,128)(2,...) custom-call(s32[1]{0:T(128)} %bitcast.place, ...), custom_call_target="tpu_custom_call" | custom-call | flops 3523215360 | bytes 10485760 | tf_op jit(solution)/shard_map/attend/pallas_call | solution.py:135
  78.0 4.6 %collective-permute-start.20 = (bf16[4,2,128,640]{3,2,1,0:T(8,128)(2,1)}, bf16[4,2,128,640]{3,2,1,0:T(8,128)(2,1)S(1)}, u32[]{:S(2)}, u32[]{:S(2)}) collective-permute-start(bf16[4,2,128,640]{3,2,1,0:T(8,128)(2,1)} %get-tuple-element.46), channel_id=1, source_target_pairs={{0,8},{8,16},{16,24},{1,9},{9,17},{17,25},{2,10},{10,18},{18,26},{... | collective-permute-start | bytes 3932168 | tf_op jit(solution)/shard_map/ppermute | solution.py:275
  82.7 1.5 %collective-permute-start.16 = (bf16[2,128,640]{2,1,0:T(8,128)(2,1)}, bf16[2,128,640]{2,1,0:T(8,128)(2,1)S(1)}, u32[]{:S(2)}, u32[]{:S(2)}) collective-permute-start(bf16[2,128,640]{2,1,0:T(8,128)(2,1)} %get-tuple-element.39), channel_id=1, source_target_pairs={{0,4},{2,6},{4,0},{6,2},{1,5},{3,7},{5,1},{7,3},{8,12},{10,14},{12... | collective-permute-start | bytes 983048 | tf_op jit(solution)/shard_map/ppermute | solution.py:270
  84.6 8.9 %collective-permute-done.16.refs_2_ = bf16[2,128,640]{2,1,0:T(8,128)(2,1)S(1)} collective-permute-done((bf16[2,128,640]{2,1,0:T(8,128)(2,1)}, bf16[2,128,640]{2,1,0:T(8,128)(2,1)S(1)}, u32[]{:S(2)}, u32[]{:S(2)}) %collective-permute-start.16) | collective-permute-done | bytes 327712 | tf_op jit(solution)/shard_map/ppermute | solution.py:270
  93.5 6.1 %collective-permute-done.17.refs_3_ = bf16[2,128,640]{2,1,0:T(8,128)(2,1)S(1)} collective-permute-done((bf16[2,128,640]{2,1,0:T(8,128)(2,1)}, bf16[2,128,640]{2,1,0:T(8,128)(2,1)S(1)}, u32[]{:S(2)}, u32[]{:S(2)}) %collective-permute-start.17) | collective-permute-done | bytes 327712 | tf_op jit(solution)/shard_map/ppermute | solution.py:270
  101.9 7.8 %collective-permute-done.19 = bf16[4,2,128,640]{3,2,1,0:T(8,128)(2,1)S(1)} collective-permute-done((bf16[4,2,128,640]{3,2,1,0:T(8,128)(2,1)}, bf16[4,2,128,640]{3,2,1,0:T(8,128)(2,1)S(1)}, u32[]{:S(2)}, u32[]{:S(2)}) %collective-permute-start.19) | collective-permute-done | bytes 1310752 | tf_op jit(solution)/shard_map/ppermute | solution.py:275
  111.0 2.3 %fusion.13 = (bf16[2,128,640]{2,1,0:T(8,128)(2,1)S(1)}, bf16[2,128,640]{2,1,0:T(8,128)(2,1)S(1)}, bf16[2,128,640]{2,1,0:T(8,128)(2,1)S(1)}, bf16[2,128,640]{2,1,0:T(8,128)(2,1)S(1)}) fusion(f32[4,2,128,640]{3,2,1,0:T(8,128)} %get-tuple-element.44, bf16[4,2,128,640]{3,2,1,0:T(8,128)(2,1)S(1)} %collective-permute-done.20, ...), kind=kLoop, calls=%fused_computation.21 | loop fusion | flops 3276800 | bytes 6553600 | tf_op jit(solution)/shard_map/convert_element_type | solution.py:328
  115.3 1.6 %collective-permute-start.18 = (f32[128]{0:T(128)S(1)}, f32[128]{0:T(128)S(1)}, u32[]{:S(2)}, u32[]{:S(2)}) collective-permute-start(f32[128]{0:T(128)S(1)} %slice_reduce_fusion.1), channel_id=1, source_target_pairs={{0,1},{1,0},{2,3},{3,2},{4,5},{5,4},{6,7},{7,6},{8,9},{9,8},{10,11... | collective-permute-start | bytes 1544 | tf_op jit(solution)/shard_map/ppermute | solution.py:282
  116.9 2.0 %collective-permute-done.18 = f32[128]{0:T(128)S(1)} collective-permute-done((f32[128]{0:T(128)S(1)}, f32[128]{0:T(128)S(1)}, u32[]{:S(2)}, u32[]{:S(2)}) %collective-permute-start.18) | collective-permute-done | bytes 544 | tf_op jit(solution)/shard_map/ppermute | solution.py:282
  119.0 4.4 %collective-permute-done.23.refs_3_ = bf16[2,128,640]{2,1,0:T(8,128)(2,1)S(1)} collective-permute-done((bf16[2,128,640]{2,1,0:T(8,128)(2,1)S(1)}, bf16[2,128,640]{2,1,0:T(8,128)(2,1)S(1)}, u32[]{:S(2)}, u32[]{:S(2)}) %collective-permute-start.23) | collective-permute-done | bytes 327712 | tf_op jit(solution)/shard_map/ppermute | solution.py:270
  123.3 7.1 %collective-permute-done.22.refs_2_ = bf16[2,128,640]{2,1,0:T(8,128)(2,1)S(1)} collective-permute-done((bf16[2,128,640]{2,1,0:T(8,128)(2,1)S(1)}, bf16[2,128,640]{2,1,0:T(8,128)(2,1)S(1)}, u32[]{:S(2)}, u32[]{:S(2)}) %collective-permute-start.22) | collective-permute-done | bytes 327712 | tf_op jit(solution)/shard_map/ppermute | solution.py:270
  131.9 1.6 %collective-permute-start.24 = (f32[128]{0:T(128)S(1)}, f32[128]{0:T(128)S(1)}, u32[]{:S(2)}, u32[]{:S(2)}) collective-permute-start(f32[128]{0:T(128)S(1)} %slice_reduce_fusion), channel_id=1, source_target_pairs={{0,1},{1,0},{2,3},{3,2},{4,5},{5,4},{6,7},{7,6},{8,9},{9,8},{10,11... | collective-permute-start | bytes 1544 | tf_op jit(solution)/shard_map/ppermute | solution.py:282
  (103 shorter events, 26.0 us)
Async XLA Ops:
  3.4 4.6 %collective-permute-start = (f32[2,128]{1,0:T(2,128)S(1)}, f32[2,128]{1,0:T(2,128)S(1)}, u32[]{:S(2)}, u32[]{:S(2)}) collective-permute-start(f32[2,128]{1,0:T(2,128)S(1)} %pad_maximum_fusion), channel_id=1, source_target_pairs={{0,1},{1,0},{2,3},{3,2},{4,5},{5,4},{6,7},{7,6},{8,9},{9,8},{10,11... | collective-permute-start | bytes 3080 | tf_op jit(solution)/shard_map/ppermute | solution.py:282
  9.4 20.5 %collective-permute-start.2 = (bf16[2,128,640]{2,1,0:T(8,128)(2,1)S(1)}, bf16[2,128,640]{2,1,0:T(8,128)(2,1)S(1)}, u32[]{:S(2)}, u32[]{:S(2)}) collective-permute-start(bf16[2,128,640]{2,1,0:T(8,128)(2,1)S(1)} %get-tuple-element.27.refs_8_), channel_id=1, source_target_pairs={{8,0},{16,8},{24,16},{9,1},{17,9},{25,17},{10,2},{18,10},{26,18},{... | collective-permute-start | bytes 983048 | tf_op jit(solution)/shard_map/ppermute | solution.py:275
  10.7 20.5 %collective-permute-start.1 = (bf16[2,128,640]{2,1,0:T(8,128)(2,1)S(1)}, bf16[2,128,640]{2,1,0:T(8,128)(2,1)S(1)}, u32[]{:S(2)}, u32[]{:S(2)}) collective-permute-start(bf16[2,128,640]{2,1,0:T(8,128)(2,1)S(1)} %get-tuple-element.27.refs_8_), channel_id=1, source_target_pairs={{0,8},{8,16},{16,24},{1,9},{9,17},{17,25},{2,10},{10,18},{18,26},{... | collective-permute-start | bytes 983048 | tf_op jit(solution)/shard_map/ppermute | solution.py:275
  15.4 2.2 %collective-permute-start.6 = (bf16[2,128,640]{2,1,0:T(8,128)(2,1)S(1)}, bf16[2,128,640]{2,1,0:T(8,128)(2,1)S(1)}, u32[]{:S(2)}, u32[]{:S(2)}) collective-permute-start(bf16[2,128,640]{2,1,0:T(8,128)(2,1)S(1)} %get-tuple-element.34), channel_id=1, source_target_pairs={{0,2},{2,0},{4,6},{6,4},{1,3},{3,1},{5,7},{7,5},{8,10},{10,8},{12,... | collective-permute-start | bytes 983048 | tf_op jit(solution)/shard_map/ppermute | solution.py:270
  15.5 10.6 %collective-permute-start.8 = (bf16[2,128,640]{2,1,0:T(8,128)(2,1)S(1)}, bf16[2,128,640]{2,1,0:T(8,128)(2,1)S(1)}, u32[]{:S(2)}, u32[]{:S(2)}) collective-permute-start(bf16[2,128,640]{2,1,0:T(8,128)(2,1)S(1)} %get-tuple-element.35), channel_id=1, source_target_pairs={{0,4},{2,6},{4,0},{6,2},{1,5},{3,7},{5,1},{7,3},{8,12},{10,14},{12... | collective-permute-start | bytes 983048 | tf_op jit(solution)/shard_map/ppermute | solution.py:270
  17.5 19.7 %collective-permute-start.10 = (bf16[2,128,640]{2,1,0:T(8,128)(2,1)S(1)}, bf16[2,128,640]{2,1,0:T(8,128)(2,1)S(1)}, u32[]{:S(2)}, u32[]{:S(2)}) collective-permute-start(bf16[2,128,640]{2,1,0:T(8,128)(2,1)S(1)} %get-tuple-element.36), channel_id=1, source_target_pairs={{0,6},{2,4},{4,2},{6,0},{1,7},{3,5},{5,3},{7,1},{8,14},{10,12},{12... | collective-permute-start | bytes 983048 | tf_op jit(solution)/shard_map/ppermute | solution.py:270
  17.6 19.6 %collective-permute-start.12 = (bf16[2,128,640]{2,1,0:T(8,128)(2,1)S(1)}, bf16[2,128,640]{2,1,0:T(8,128)(2,1)S(1)}, u32[]{:S(2)}, u32[]{:S(2)}) collective-permute-start(bf16[2,128,640]{2,1,0:T(8,128)(2,1)S(1)} %collective-permute-done.6.refs_9_), channel_id=1, source_target_pairs={{8,0},{16,8},{24,16},{9,1},{17,9},{25,17},{10,2},{18,10},{26,18},{... | collective-permute-start | bytes 983048 | tf_op jit(solution)/shard_map/ppermute | solution.py:275
  26.0 13.4 %collective-permute-start.7 = (bf16[2,128,640]{2,1,0:T(8,128)(2,1)S(1)}, bf16[2,128,640]{2,1,0:T(8,128)(2,1)S(1)}, u32[]{:S(2)}, u32[]{:S(2)}) collective-permute-start(bf16[2,128,640]{2,1,0:T(8,128)(2,1)S(1)} %collective-permute-done.6.refs_9_), channel_id=1, source_target_pairs={{0,8},{8,16},{16,24},{1,9},{9,17},{17,25},{2,10},{10,18},{18,26},{... | collective-permute-start | bytes 983048 | tf_op jit(solution)/shard_map/ppermute | solution.py:275
  30.0 10.5 %collective-permute-start.13 = (bf16[2,128,640]{2,1,0:T(8,128)(2,1)S(1)}, bf16[2,128,640]{2,1,0:T(8,128)(2,1)S(1)}, u32[]{:S(2)}, u32[]{:S(2)}) collective-permute-start(bf16[2,128,640]{2,1,0:T(8,128)(2,1)S(1)} %collective-permute-done.8.refs_10_), channel_id=1, source_target_pairs={{8,0},{16,8},{24,16},{9,1},{17,9},{25,17},{10,2},{18,10},{26,18},{... | collective-permute-start | bytes 983048 | tf_op jit(solution)/shard_map/ppermute | solution.py:275
  31.3 12.0 %collective-permute-start.9 = (bf16[2,128,640]{2,1,0:T(8,128)(2,1)S(1)}, bf16[2,128,640]{2,1,0:T(8,128)(2,1)S(1)}, u32[]{:S(2)}, u32[]{:S(2)}) collective-permute-start(bf16[2,128,640]{2,1,0:T(8,128)(2,1)S(1)} %collective-permute-done.8.refs_10_), channel_id=1, source_target_pairs={{0,8},{8,16},{16,24},{1,9},{9,17},{17,25},{2,10},{10,18},{18,26},{... | collective-permute-start | bytes 983048 | tf_op jit(solution)/shard_map/ppermute | solution.py:275
  37.1 16.5 %collective-permute-start.3 = (bf16[272,640]{1,0:T(8,128)(2,1)S(1)}, bf16[272,640]{1,0:T(8,128)(2,1)S(1)}, u32[]{:S(2)}, u32[]{:S(2)}) collective-permute-start(bf16[272,640]{1,0:T(8,128)(2,1)S(1)} %get-tuple-element.31), channel_id=1, source_target_pairs={{0,2},{2,0},{4,6},{6,4},{1,3},{3,1},{5,7},{7,5},{8,10},{10,8},{12,... | collective-permute-start | bytes 1044488 | tf_op jit(solution)/shard_map/ppermute | solution.py:270
  38.0 15.7 %collective-permute-start.4 = (bf16[272,640]{1,0:T(8,128)(2,1)S(1)}, bf16[272,640]{1,0:T(8,128)(2,1)S(1)}, u32[]{:S(2)}, u32[]{:S(2)}) collective-permute-start(bf16[272,640]{1,0:T(8,128)(2,1)S(1)} %get-tuple-element.32), channel_id=1, source_target_pairs={{0,4},{2,6},{4,0},{6,2},{1,5},{3,7},{5,1},{7,3},{8,12},{10,14},{12... | collective-permute-start | bytes 1044488 | tf_op jit(solution)/shard_map/ppermute | solution.py:270
  40.2 15.3 %collective-permute-start.5 = (bf16[272,640]{1,0:T(8,128)(2,1)S(1)}, bf16[272,640]{1,0:T(8,128)(2,1)S(1)}, u32[]{:S(2)}, u32[]{:S(2)}) collective-permute-start(bf16[272,640]{1,0:T(8,128)(2,1)S(1)} %get-tuple-element.33), channel_id=1, source_target_pairs={{0,6},{2,4},{4,2},{6,0},{1,7},{3,5},{5,3},{7,1},{8,14},{10,12},{12... | collective-permute-start | bytes 1044488 | tf_op jit(solution)/shard_map/ppermute | solution.py:270
  40.5 11.9 %collective-permute-start.14 = (bf16[2,128,640]{2,1,0:T(8,128)(2,1)S(1)}, bf16[2,128,640]{2,1,0:T(8,128)(2,1)S(1)}, u32[]{:S(2)}, u32[]{:S(2)}) collective-permute-start(bf16[2,128,640]{2,1,0:T(8,128)(2,1)S(1)} %collective-permute-done.10.refs_11_), channel_id=1, source_target_pairs={{8,0},{16,8},{24,16},{9,1},{17,9},{25,17},{10,2},{18,10},{26,18},{... | collective-permute-start | bytes 983048 | tf_op jit(solution)/shard_map/ppermute | solution.py:275
  43.3 10.4 %collective-permute-start.11 = (bf16[2,128,640]{2,1,0:T(8,128)(2,1)S(1)}, bf16[2,128,640]{2,1,0:T(8,128)(2,1)S(1)}, u32[]{:S(2)}, u32[]{:S(2)}) collective-permute-start(bf16[2,128,640]{2,1,0:T(8,128)(2,1)S(1)} %collective-permute-done.10.refs_11_), channel_id=1, source_target_pairs={{0,8},{8,16},{16,24},{1,9},{9,17},{17,25},{2,10},{10,18},{18,26},{... | collective-permute-start | bytes 983048 | tf_op jit(solution)/shard_map/ppermute | solution.py:275
  76.7 33.0 %collective-permute-start.19 = (bf16[4,2,128,640]{3,2,1,0:T(8,128)(2,1)}, bf16[4,2,128,640]{3,2,1,0:T(8,128)(2,1)S(1)}, u32[]{:S(2)}, u32[]{:S(2)}) collective-permute-start(bf16[4,2,128,640]{3,2,1,0:T(8,128)(2,1)} %get-tuple-element.45), channel_id=1, source_target_pairs={{8,0},{16,8},{24,16},{9,1},{17,9},{25,17},{10,2},{18,10},{26,18},{... | collective-permute-start | bytes 3932168 | tf_op jit(solution)/shard_map/ppermute | solution.py:275
  78.0 33.0 %collective-permute-start.20 = (bf16[4,2,128,640]{3,2,1,0:T(8,128)(2,1)}, bf16[4,2,128,640]{3,2,1,0:T(8,128)(2,1)S(1)}, u32[]{:S(2)}, u32[]{:S(2)}) collective-permute-start(bf16[4,2,128,640]{3,2,1,0:T(8,128)(2,1)} %get-tuple-element.46), channel_id=1, source_target_pairs={{0,8},{8,16},{16,24},{1,9},{9,17},{17,25},{2,10},{10,18},{18,26},{... | collective-permute-start | bytes 3932168 | tf_op jit(solution)/shard_map/ppermute | solution.py:275
  82.7 10.8 %collective-permute-start.16 = (bf16[2,128,640]{2,1,0:T(8,128)(2,1)}, bf16[2,128,640]{2,1,0:T(8,128)(2,1)S(1)}, u32[]{:S(2)}, u32[]{:S(2)}) collective-permute-start(bf16[2,128,640]{2,1,0:T(8,128)(2,1)} %get-tuple-element.39), channel_id=1, source_target_pairs={{0,4},{2,6},{4,0},{6,2},{1,5},{3,7},{5,1},{7,3},{8,12},{10,14},{12... | collective-permute-start | bytes 983048 | tf_op jit(solution)/shard_map/ppermute | solution.py:270
  84.2 15.4 %collective-permute-start.17 = (bf16[2,128,640]{2,1,0:T(8,128)(2,1)}, bf16[2,128,640]{2,1,0:T(8,128)(2,1)S(1)}, u32[]{:S(2)}, u32[]{:S(2)}) collective-permute-start(bf16[2,128,640]{2,1,0:T(8,128)(2,1)} %get-tuple-element.40), channel_id=1, source_target_pairs={{0,6},{2,4},{4,2},{6,0},{1,7},{3,5},{5,3},{7,1},{8,14},{10,12},{12... | collective-permute-start | bytes 983048 | tf_op jit(solution)/shard_map/ppermute | solution.py:270
  113.3 10.0 %collective-permute-start.23 = (bf16[2,128,640]{2,1,0:T(8,128)(2,1)S(1)}, bf16[2,128,640]{2,1,0:T(8,128)(2,1)S(1)}, u32[]{:S(2)}, u32[]{:S(2)}) collective-permute-start(bf16[2,128,640]{2,1,0:T(8,128)(2,1)S(1)} %get-tuple-element.50), channel_id=1, source_target_pairs={{0,6},{2,4},{4,2},{6,0},{1,7},{3,5},{5,3},{7,1},{8,14},{10,12},{12... | collective-permute-start | bytes 983048 | tf_op jit(solution)/shard_map/ppermute | solution.py:270
  113.6 16.8 %collective-permute-start.22 = (bf16[2,128,640]{2,1,0:T(8,128)(2,1)S(1)}, bf16[2,128,640]{2,1,0:T(8,128)(2,1)S(1)}, u32[]{:S(2)}, u32[]{:S(2)}) collective-permute-start(bf16[2,128,640]{2,1,0:T(8,128)(2,1)S(1)} %get-tuple-element.51), channel_id=1, source_target_pairs={{0,4},{2,6},{4,0},{6,2},{1,5},{3,7},{5,1},{7,3},{8,12},{10,14},{12... | collective-permute-start | bytes 983048 | tf_op jit(solution)/shard_map/ppermute | solution.py:270
  114.9 15.5 %collective-permute-start.21 = (bf16[2,128,640]{2,1,0:T(8,128)(2,1)S(1)}, bf16[2,128,640]{2,1,0:T(8,128)(2,1)S(1)}, u32[]{:S(2)}, u32[]{:S(2)}) collective-permute-start(bf16[2,128,640]{2,1,0:T(8,128)(2,1)S(1)} %get-tuple-element.52), channel_id=1, source_target_pairs={{0,2},{2,0},{4,6},{6,4},{1,3},{3,1},{5,7},{7,5},{8,10},{10,8},{12,... | collective-permute-start | bytes 983048 | tf_op jit(solution)/shard_map/ppermute | solution.py:270
  115.3 3.6 %collective-permute-start.18 = (f32[128]{0:T(128)S(1)}, f32[128]{0:T(128)S(1)}, u32[]{:S(2)}, u32[]{:S(2)}) collective-permute-start(f32[128]{0:T(128)S(1)} %slice_reduce_fusion.1), channel_id=1, source_target_pairs={{0,1},{1,0},{2,3},{3,2},{4,5},{5,4},{6,7},{7,6},{8,9},{9,8},{10,11... | collective-permute-start | bytes 1544 | tf_op jit(solution)/shard_map/ppermute | solution.py:282
  131.9 3.6 %collective-permute-start.24 = (f32[128]{0:T(128)S(1)}, f32[128]{0:T(128)S(1)}, u32[]{:S(2)}, u32[]{:S(2)}) collective-permute-start(f32[128]{0:T(128)S(1)} %slice_reduce_fusion), channel_id=1, source_target_pairs={{0,1},{1,0},{2,3},{3,2},{4,5},{5,4},{6,7},{7,6},{8,9},{9,8},{10,11... | collective-permute-start | bytes 1544 | tf_op jit(solution)/shard_map/ppermute | solution.py:282
  (26 other events, 359.4 us)

commit v2 on v1

v2 whole, which is shorter than its diff:
```python
import functools

import jax
import jax.numpy as jnp
import numpy as np
from jax import lax
from jax.experimental import pallas as pl
from jax.experimental.pallas import tpu as pltpu
from jax.sharding import Mesh
from jax.sharding import PartitionSpec as P

DIM = 5120
HEAD = 128
TAIL = 16
epsilon = 1e-06
lowest = -1e30
LOG2E = 1.4426950408889634
SCALE = HEAD ** (-0.5)
bf16 = jnp.bfloat16
f32 = jnp.float32
WIDE = pltpu.CompilerParams(vmem_limit_bytes=60 * 2**20)


def offset_list(levels):
    result = [0]
    for height in range(levels):
        result = result + [2**height, -(2**height)]
    return result


class Plan:
    def __init__(self, spans, heads_here):
        levels = spans.bit_length() - 2
        reach = 2 ** (levels - 1)
        whole = reach == 4 and heads_here % reach == 0 and spans % reach == 0
        self.group = reach if whole else 1
        self.offsets = sorted(offset_list(levels), reverse=True)
        self.distances = [-1, 0, 1] if self.group > 1 else sorted(self.offsets)
        self.home = self.distances.index(0)
        self.heads = heads_here // self.group
        self.chunks = chunks_of(self.heads)
        self.pack = min(self.group, 2)
        if self.group > 1:
            self.slots = [[self.group + s - o for o in self.offsets] for s in range(self.group)]
        else:
            self.slots = [[self.distances.index(-o) for o in self.offsets]]


def chunks_of(heads):
    return [(0, heads)]


def busy(us):
    return pl.CostEstimate(flops=int(us * 1.1e9), bytes_accessed=int(us * 3.5e6), transcendentals=0)


def dot(a, b, ca, cb):
    return lax.dot_general(a, b, (((ca,), (cb,)), ((), ())), preferred_element_type=f32)


def attend(place, *refs, plan, first, heads):
    group, nd, noff = plan.group, len(plan.distances), len(plan.offsets)
    it = iter(refs)
    packs = group // plan.pack

    def unpacked():
        return [ref.at[i] for ref in [next(it) for _ in range(packs)] for i in range(plan.pack)]

    qd = [next(it) for _ in range(group)]
    kv = [unpacked() for _ in range(nd)]
    out_oq = [next(it) for _ in range(group)]
    out_kv = [next(it) for _ in range(nd)]
    keys, vals, queries, grads, weights, scored, outs, dqs, allow = (next(it) for _ in range(9))
    r = place[0]

    def rows(slot):
        if isinstance(slot, int):
            return pl.ds(slot * HEAD, HEAD)
        return pl.ds(pl.multiple_of(slot * HEAD, HEAD), HEAD)

    def one_head(h, _):
        source = pl.ds(pl.multiple_of((first + h) * HEAD, HEAD), HEAD)
        target = pl.ds(pl.multiple_of(h * HEAD, HEAD), HEAD)
        for m in range(group):
            at = rows(m ^ r)
            queries[at, :] = qd[m][0:HEAD, source]
            grads[at, :] = qd[m][HEAD : 2 * HEAD, source]
            allow[m ^ r] = qd[m][2 * HEAD : 2 * HEAD + TAIL, source].astype(f32)
            for d in range(nd):
                at = rows(d * group + (m ^ r))
                keys[at, :] = kv[d][m][0, :, source]
                vals[at, :] = kv[d][m][1, :, source]

        def rows_of(j):
            return slice(j * HEAD, (j + 1) * HEAD)

        spans = range(group)
        q = [queries[rows(s), :] for s in spans]
        g = [grads[rows(s), :] for s in spans]
        k = [jnp.concatenate([keys[rows(x), :] for x in plan.slots[s]], axis=0) for s in spans]
        v = [jnp.concatenate([vals[rows(x), :] for x in plan.slots[s]], axis=0) for s in spans]
        raw = [dot(q[s], k[s], 1, 1) for s in spans]
        dp = [dot(g[s], v[s], 1, 1) for s in spans]
        p = []
        for s in spans:
            bias = jnp.concatenate([allow[s, j : j + 1, :] for j in range(noff)], axis=1)
            scores = raw[s] * (SCALE * LOG2E) + bias
            e = jnp.exp2(scores - jnp.max(scores, axis=1, keepdims=True))
            p.append(e * (1.0 / jnp.sum(e, axis=1, keepdims=True)))
        low = [x.astype(bf16) for x in p]
        o = [dot(low[s], v[s], 1, 0).astype(bf16) for s in spans]
        ds = []
        for s in spans:
            delta = jnp.sum(g[s].astype(f32) * o[s].astype(f32), axis=1, keepdims=True)
            ds.append((p[s] * SCALE * (dp[s] - delta)).astype(bf16))
        for s in spans:
            outs[rows(s), :] = o[s]
            dqs[rows(s), :] = dot(ds[s], k[s], 1, 0).astype(bf16)

        for m in range(group):
            out_oq[m][0, :, target] = outs[rows(m ^ r), :]
            out_oq[m][1, :, target] = dqs[rows(m ^ r), :]

        for d in range(nd):
            for s in range(group):
                users = [
                    (t, j)
                    for t in range(group)
                    for j in range(noff)
                    if plan.slots[t][j] == d * group + s
                ]

                def stacked(values):
                    return jnp.concatenate([values[t][:, rows_of(j)] for t, j in users], axis=0)

                qs = jnp.concatenate([q[t] for t, _ in users], axis=0)
                gs = jnp.concatenate([g[t] for t, _ in users], axis=0)
                out_kv[d][s ^ r, 1, :, target] = dot(stacked(ds), qs, 0, 0).astype(out_kv[d].dtype)
                out_kv[d][s ^ r, 0, :, target] = dot(stacked(low), gs, 0, 0).astype(out_kv[d].dtype)
        return 0

    lax.fori_loop(0, heads, one_head, 0)


def attention(place, qd, kv, plan, first, heads):
    width = heads * HEAD
    group, nd, noff = plan.group, len(plan.distances), len(plan.offsets)
    ng = nd * group
    packs = group // plan.pack
    query = pl.BlockSpec((2 * HEAD + TAIL, HEAD), lambda h, _: (0, h + first))
    keyed = pl.BlockSpec((plan.pack, 2, HEAD, HEAD), lambda h, _: (0, 0, 0, h + first))
    packs = group // plan.pack
    whole = pl.BlockSpec(memory_space=pltpu.VMEM)
    outs = [jax.ShapeDtypeStruct((2, HEAD, width), bf16)] * group + [
        jax.ShapeDtypeStruct((group, 2, HEAD, width), f32 if by == 0 else bf16)
        for by in plan.distances
    ]
    result = pl.pallas_call(
        functools.partial(attend, plan=plan, first=first, heads=heads),
        grid_spec=pltpu.PrefetchScalarGridSpec(
            num_scalar_prefetch=1,
            grid=(),
            in_specs=[whole] * (group + nd * packs),
            out_specs=[whole] * (group + nd),
            scratch_shapes=[pltpu.VMEM((ng * HEAD, HEAD), bf16)] * 2
            + [pltpu.VMEM((group * HEAD, HEAD), bf16)] * 2
            + [pltpu.VMEM((group * HEAD, noff * HEAD), bf16)] * 2
            + [pltpu.VMEM((group * HEAD, HEAD), bf16)] * 2
            + [pltpu.VMEM((group, TAIL, HEAD), f32)],
        ),
        out_shape=outs,
        compiler_params=pltpu.CompilerParams(vmem_limit_bytes=36 * 2**20),
        cost_estimate=busy(4 * heads),
        name="attend",
    )(place, *qd, *[pack for block in kv for pack in block])
    return result[:group], result[group:]


def join(place, *refs, plan):
    group = plan.group
    count = len(plan.chunks) * group
    parts = refs[:count]
    raw_ref, rstd_ref, gain_ref, plain, normed, inner = refs[count:]
    r = place[0]
    column = jnp.transpose(jnp.broadcast_to(rstd_ref[...], (HEAD, HEAD)))[:, 0:1]
    width = plan.heads * HEAD
    total = jnp.zeros((HEAD, HEAD), f32)
    for c, (first, heads) in enumerate(plan.chunks):
        for m in range(group):
            base = (m ^ r) * width + first * HEAD
            part = parts[c * group + m]
            for h in range(heads):
                at = pl.ds(pl.multiple_of(base + h * HEAD, HEAD), HEAD)
                here = slice(h * HEAD, (h + 1) * HEAD)
                plain[:, at] = part[0, :, here]
                low = part[1, :, here]
                normed[:, at] = low
                total += low.astype(f32) * gain_ref[:, at] * raw_ref[:, at].astype(f32)
    inner[...] = jnp.broadcast_to(
        jnp.sum(total, axis=1, keepdims=True) * column, (HEAD, HEAD)
    )


def joined(place, parts, raw, rstd, gain, plan):
    shape = raw.shape
    flat = [x for chunk in parts for x in chunk]
    whole = pl.BlockSpec(memory_space=pltpu.VMEM)
    return pl.pallas_call(
        functools.partial(join, plan=plan),
        grid_spec=pltpu.PrefetchScalarGridSpec(
            num_scalar_prefetch=1,
            grid=(),
            in_specs=[whole] * (len(flat) + 3),
            out_specs=[whole] * 3,
        ),
        out_shape=[
            jax.ShapeDtypeStruct(shape, bf16),
            jax.ShapeDtypeStruct(shape, bf16),
            jax.ShapeDtypeStruct((HEAD, HEAD), f32),
        ],
        compiler_params=pltpu.CompilerParams(vmem_limit_bytes=24 * 2**20),
        cost_estimate=busy(2),
        name="join",
    )(place, *flat, raw, rstd, gain)


def local(
    query_vectors,
    key_vectors,
    value_vectors,
    output_grad,
    query_gain,
    key_gain,
    block_pairs,
    pair_counts,
    *,
    plan,
):
    row_count, col_count = query_vectors.shape
    group, offsets, distances = plan.group, plan.offsets, plan.distances
    features = col_count * lax.axis_size("head")
    width = col_count // group
    blocks = lax.axis_size("block")
    r = lax.axis_index("place")
    place = jnp.reshape(r, (1,)).astype(jnp.int32)

    def swap(x, m):
        return lax.ppermute(x, "place", [(i, i ^ m) for i in range(group)]) if m else x

    def moved(x, by):
        if by == 0:
            return x
        return lax.ppermute(
            x, "block", [(i, i + by) for i in range(blocks) if 0 <= i + by < blocks]
        )

    def summed(x):
        step, count = 1, lax.axis_size("head")
        while step < count:
            x = x + lax.ppermute(x, "head", [(i, i ^ step) for i in range(count)])
            step *= 2
        return x

    query_gain = query_gain[None, :]
    key_gain = key_gain[None, :]

    def chunk(x, m):
        return lax.dynamic_slice_in_dim(x, (r ^ m) * width, width, axis=1)

    squares = summed(
        jnp.stack([jnp.sum(jnp.square(x.astype(f32)), axis=1) for x in (key_vectors, query_vectors)])
    )
    my_rstd = lax.rsqrt(squares / features + epsilon)

    def normed(x, rstd, gain):
        return (x.astype(f32) * rstd[:, None] * gain).astype(bf16)

    key_norm = normed(key_vectors, my_rstd[0], key_gain)
    kv = [jnp.stack([chunk(key_norm, m), chunk(value_vectors, m)]) for m in range(group)]
    query_norm = normed(query_vectors, my_rstd[1], query_gain)
    live = jnp.arange(block_pairs.shape[1], dtype=jnp.int32) < pair_counts[0]
    steps = block_pairs[0, :, 0] - block_pairs[0, :, 1]
    wanted = jnp.array(offsets, jnp.int32)
    flags = jnp.any(live[:, None] & (steps[:, None] == wanted[None, :]), axis=0)
    bias = jnp.pad(jnp.where(flags, 0.0, lowest), (0, TAIL - len(offsets)))
    allow = jnp.broadcast_to(bias[:, None], (TAIL, width)).astype(bf16)
    qd = [
        jnp.concatenate([chunk(query_norm, m), chunk(output_grad, m), allow]) for m in range(group)
    ]

    kv = [swap(x, m) for m, x in enumerate(kv)]
    near = jnp.stack(kv[: plan.pack])
    near = [moved(near, -by) for by in distances]
    kv, qd = lax.optimization_barrier((kv, qd))
    qd = [swap(x, m) for m, x in enumerate(qd)]
    packs = [jnp.stack(kv[i : i + plan.pack]) for i in range(plan.pack, group, plan.pack)]
    packs, near, qd[group // 2 % group] = lax.optimization_barrier((packs, near, qd[group // 2 % group]))
    kv = [[x] + [moved(y, -by) for y in packs] for x, by in zip(near, distances)]

    oq_back, kv_back = [], []
    for first, count in plan.chunks:
        oq_parts, kv_parts = attention(place, qd, kv, plan, first, count)
        oq_back.append([swap(x, m) for m, x in enumerate(oq_parts)])
        back = [moved(kv_parts[d], by) for d, by in enumerate(distances) if by]
        total = []
        for m in range(group):
            x = kv_parts[plan.home][m]
            for y in back:
                x = x + y[m].astype(f32)
            total.append(swap(x.astype(bf16), m))
        kv_back.append(total)

    attended, query_norm_grad, query_inner = joined(
        place, oq_back, query_vectors, my_rstd[1:2], query_gain, plan
    )
    value_grad, key_norm_grad, key_inner = joined(
        place, kv_back, key_vectors, my_rstd[0:1], key_gain, plan
    )

    def finished(raw, rstd, gain, grad, inner):
        inner = summed(inner[:, 0])[:, None] / features
        rstd_col = rstd[0][:, None]
        unit = raw.astype(f32) * rstd_col
        return (rstd_col * (gain * grad.astype(f32) - unit * inner)).astype(bf16)

    query_grad = finished(query_vectors, my_rstd[1:2], query_gain, query_norm_grad, query_inner)
    key_grad = finished(key_vectors, my_rstd[0:1], key_gain, key_norm_grad, key_inner)
    return (attended, query_grad, key_grad, value_grad)


def solution(mesh):
    spans, head_groups = mesh.devices.shape
    plan = Plan(spans, DIM // HEAD // head_groups)
    blocks = Mesh(
        mesh.devices.reshape(spans // plan.group, plan.group, head_groups),
        ("block", "place", "head"),
    )
    ctx = ("block", "place")
    placed = (
        P(ctx, "head"),
        P(ctx, "head"),
        P(ctx, "head"),
        P(ctx, "head"),
        P("head"),
        P("head"),
        P(ctx, None, None),
        P(ctx),
    )
    return jax.shard_map(
        functools.partial(local, plan=plan),
        mesh=blocks,
        in_specs=placed,
        out_specs=(P(ctx, "head"),) * 4,
        check_vma=False,
    )
```

time: 137 us -> 123 us (0.90)
  waiting for transfers between devices: 55.5 us -> 69.6 us
  starting transfers between devices: 42.7 us -> 30.5 us
  Pallas kernels: 23.6 us -> 13.6 us
  local copies, waits for them, and re-layouts: 5.52 us -> 0.53 us
    ppermute x12, waiting for transfers between devices: 35.4 us -> 53.7 us  [swap(): lax.ppermute(x, 'place', [(i, i ^ m) for i in range(group)])]
    ppermute x10 -> x6, starting transfers between devices: 28.6 us -> 17.6 us  [moved(): lax.ppermute(x, 'block', [(i, i + by) for i in range(blocks) if 0 <= i +...]
    pallas_call x3 -> x1, Pallas kernels: 20.9 us -> 10.9 us  [attention(): pl.pallas_call(functools.partial(attend, plan=plan, first=first, heads=he...]
    unnamed x50 -> x16, local copies, waits for them, and re-layouts: 5.07 us -> 0.04 us
    ppermute x10 -> x6, waiting for transfers between devices: 16.5 us -> 11.6 us  [moved(): lax.ppermute(x, 'block', [(i, i + by) for i in range(blocks) if 0 <= i +...]
    convert_element_type x1, other arithmetic: 2.28 us -> 0.56 us  [local(): total.append(swap(x.astype(bf16), m))]
  transfers between devices with their start and end apart: 25 -> 21, of which waited for: 14 -> 17; matrix products, arithmetic and copies ran while one was open for 1% -> 2% of each run, Pallas kernels for 1% -> 1%
where the time goes in v2:
time: 123 us
  waiting for transfers between devices  69.6 us (57%)
  starting transfers between devices  30.5 us (25%)
  Pallas kernels  13.6 us (11%)
  other arithmetic  6.99 us (6%)
  between operations  1.62 us (1%)
    ppermute x12, waiting for transfers between devices, swap(): lax.ppermute(x, 'place', [(i, i ^ m) for i in range(group)])  53.7 us
    ppermute x6, starting transfers between devices, moved(): lax.ppermute(x, 'block', [(i, i + by) for i in range(blocks) if 0 <= i +...  17.6 us
    ppermute x6, waiting for transfers between devices, moved(): lax.ppermute(x, 'block', [(i, i + by) for i in range(blocks) if 0 <= i +...  11.6 us
    pallas_call x1, Pallas kernels, attention(): pl.pallas_call(functools.partial(attend, plan=plan, first=first, heads=he...  10.9 us
    ppermute x12, starting transfers between devices, swap(): lax.ppermute(x, 'place', [(i, i ^ m) for i in range(group)])  7.59 us
    ppermute x3, starting transfers between devices, summed(): x = x + lax.ppermute(x, 'head', [(i, i ^ step) for i in range(count)])  5.39 us
    ppermute x3, waiting for transfers between devices, summed(): x = x + lax.ppermute(x, 'head', [(i, i ^ step) for i in range(count)])  4.29 us
    reduce_sum x2, other arithmetic, local(): jnp.sum(jnp.square(x.astype(f32)), axis=1)  2.7 us
  transfers between devices with their start and end apart: 21, of which 17 were waited for; matrix products, arithmetic and copies ran while one was open for 2% of the time, Pallas kernels for 1%

profile of v2, /device:TPU:0, one launch (start us, length us, event | category | flops | bytes accessed | tf_op | source)
XLA Modules:
  0.0 122.9 jit_solution(6762041708283516183)
XLA Ops:
  0.7 1.4 %fusion.12 = f32[128]{0:T(128)S(1)} fusion(bf16[128,2560]{1,0:T(8,128)(2,1)} %refs_4_.3), kind=kLoop, calls=%fused_computation.16 | loop fusion | flops 982912 | bytes 655872 | tf_op jit(solution)/shard_map/reduce_sum | solution.py:271
  2.1 1.3 %fusion.13 = f32[128]{0:T(128)S(1)} fusion(bf16[128,2560]{1,0:T(8,128)(2,1)} %refs_4_.2), kind=kLoop, calls=%fused_computation.17 | loop fusion | flops 982912 | bytes 655872 | tf_op jit(solution)/shard_map/reduce_sum | solution.py:271
  3.4 3.0 %collective-permute-start = (f32[2,128]{1,0:T(2,128)S(1)}, f32[2,128]{1,0:T(2,128)S(1)}, u32[]{:S(2)}, u32[]{:S(2)}) collective-permute-start(f32[2,128]{1,0:T(2,128)S(1)} %pad_maximum_fusion.6), channel_id=1, source_target_pairs={{0,1},{1,0},{2,3},{3,2},{4,5},{5,4},{6,7},{7,6},{8,9},{9,8},{10,11... | collective-permute-start | bytes 3080 | tf_op jit(solution)/shard_map/ppermute | solution.py:260
  8.9 1.8 %collective-permute-start.2 = (bf16[2,128,640]{2,1,0:T(8,128)(2,1)S(1)}, bf16[2,128,640]{2,1,0:T(8,128)(2,1)S(1)}, u32[]{:S(2)}, u32[]{:S(2)}) collective-permute-start(bf16[2,128,640]{2,1,0:T(8,128)(2,1)S(1)} %pad_maximum_fusion.4), channel_id=1, source_target_pairs={{0,4},{2,6},{4,0},{6,2},{1,5},{3,7},{5,1},{7,3},{8,12},{10,14},{12... | collective-permute-start | bytes 983048 | tf_op jit(solution)/shard_map/ppermute | solution.py:248
  12.5 3.5 %collective-permute-start.5 = (bf16[2,2,128,640]{3,2,1,0:T(8,128)(2,1)S(1)}, bf16[2,2,128,640]{3,2,1,0:T(8,128)(2,1)S(1)}, u32[]{:S(2)}, u32[]{:S(2)}) collective-permute-start(bf16[2,2,128,640]{3,2,1,0:T(8,128)(2,1)S(1)} %pad_maximum_fusion.1.refs_6_), channel_id=1, source_target_pairs={{0,8},{8,16},{16,24},{1,9},{9,17},{17,25},{2,10},{10,18},{18,26},{... | collective-permute-start | bytes 1966088 | tf_op jit(solution)/shard_map/ppermute | solution.py:253
  16.0 1.3 %collective-permute-start.6 = (bf16[2,2,128,640]{3,2,1,0:T(8,128)(2,1)S(1)}, bf16[2,2,128,640]{3,2,1,0:T(8,128)(2,1)S(1)}, u32[]{:S(2)}, u32[]{:S(2)}) collective-permute-start(bf16[2,2,128,640]{3,2,1,0:T(8,128)(2,1)S(1)} %pad_maximum_fusion.1.refs_6_), channel_id=1, source_target_pairs={{8,0},{16,8},{24,16},{9,1},{17,9},{25,17},{10,2},{18,10},{26,18},{... | collective-permute-start | bytes 1966088 | tf_op jit(solution)/shard_map/ppermute | solution.py:253
  18.1 7.5 %collective-permute-done.2 = bf16[2,128,640]{2,1,0:T(8,128)(2,1)S(1)} collective-permute-done((bf16[2,128,640]{2,1,0:T(8,128)(2,1)S(1)}, bf16[2,128,640]{2,1,0:T(8,128)(2,1)S(1)}, u32[]{:S(2)}, u32[]{:S(2)}) %collective-permute-start.2) | collective-permute-done | bytes 327712 | tf_op jit(solution)/shard_map/ppermute | solution.py:248
  25.6 9.6 %collective-permute-done.7.refs_2_ = bf16[272,640]{1,0:T(8,128)(2,1)S(1)} collective-permute-done((bf16[272,640]{1,0:T(8,128)(2,1)S(1)}, bf16[272,640]{1,0:T(8,128)(2,1)S(1)}, u32[]{:S(2)}, u32[]{:S(2)}) %collective-permute-start.7) | collective-permute-done | bytes 348192 | tf_op jit(solution)/shard_map/ppermute | solution.py:248
  36.5 5.1 %collective-permute-start.9 = (bf16[2,2,128,640]{3,2,1,0:T(8,128)(2,1)S(1)}, bf16[2,2,128,640]{3,2,1,0:T(8,128)(2,1)S(1)}, u32[]{:S(2)}, u32[]{:S(2)}) collective-permute-start(bf16[2,2,128,640]{3,2,1,0:T(8,128)(2,1)S(1)} %pad_maximum_fusion.refs_7_), channel_id=1, source_target_pairs={{0,8},{8,16},{16,24},{1,9},{9,17},{17,25},{2,10},{10,18},{18,26},{... | collective-permute-start | bytes 1966088 | tf_op jit(solution)/shard_map/ppermute | solution.py:253
  43.4 8.3 %collective-permute-done.8.refs_3_ = bf16[272,640]{1,0:T(8,128)(2,1)S(1)} collective-permute-done((bf16[272,640]{1,0:T(8,128)(2,1)S(1)}, bf16[272,640]{1,0:T(8,128)(2,1)S(1)}, u32[]{:S(2)}, u32[]{:S(2)}) %collective-permute-start.8) | collective-permute-done | bytes 348192 | tf_op jit(solution)/shard_map/ppermute | solution.py:248
  51.7 2.1 %collective-permute-done.10.refs_9_ = bf16[2,2,128,640]{3,2,1,0:T(8,128)(2,1)S(1)} collective-permute-done((bf16[2,2,128,640]{3,2,1,0:T(8,128)(2,1)S(1)}, bf16[2,2,128,640]{3,2,1,0:T(8,128)(2,1)S(1)}, u32[]{:S(2)}, u32[]{:S(2)}) %collective-permute-start.10) | collective-permute-done | bytes 655392 | tf_op jit(solution)/shard_map/ppermute | solution.py:253
  55.0 10.9 %attend.1 = (bf16[2,128,640]{2,1,0:T(8,128)(2,1)S(1)}, bf16[2,128,640]{2,1,0:T(8,128)(2,1)S(1)}, bf16[2,128,640]{2,1,0:T(8,128)(2,1)S(1)}, bf16[2,128,640]{2,1,0...) custom-call(s32[1]{0:T(128)} %bitcast.place, ...), custom_call_target="tpu_custom_call" | custom-call | flops 22000001024 | bytes 70000000 | tf_op jit(solution)/shard_map/attend/pallas_call | solution.py:158
  65.9 1.3 %collective-permute-start.15 = (bf16[4,2,128,640]{3,2,1,0:T(8,128)(2,1)S(1)}, bf16[4,2,128,640]{3,2,1,0:T(8,128)(2,1)S(1)}, u32[]{:S(2)}, u32[]{:S(2)}) collective-permute-start(bf16[4,2,128,640]{3,2,1,0:T(8,128)(2,1)S(1)} %get-tuple-element.47), channel_id=1, source_target_pairs={{8,0},{16,8},{24,16},{9,1},{17,9},{25,17},{10,2},{18,10},{26,18},{... | collective-permute-start | bytes 3932168 | tf_op jit(solution)/shard_map/ppermute | solution.py:253
  67.2 5.1 %collective-permute-start.16 = (bf16[4,2,128,640]{3,2,1,0:T(8,128)(2,1)S(1)}, bf16[4,2,128,640]{3,2,1,0:T(8,128)(2,1)S(1)}, u32[]{:S(2)}, u32[]{:S(2)}) collective-permute-start(bf16[4,2,128,640]{3,2,1,0:T(8,128)(2,1)S(1)} %get-tuple-element.48), channel_id=1, source_target_pairs={{0,8},{8,16},{16,24},{1,9},{9,17},{17,25},{2,10},{10,18},{18,26},{... | collective-permute-start | bytes 3932168 | tf_op jit(solution)/shard_map/ppermute | solution.py:253
  72.4 1.5 %collective-permute-start.12 = (bf16[2,128,640]{2,1,0:T(8,128)(2,1)S(1)}, bf16[2,128,640]{2,1,0:T(8,128)(2,1)S(1)}, u32[]{:S(2)}, u32[]{:S(2)}) collective-permute-start(bf16[2,128,640]{2,1,0:T(8,128)(2,1)S(1)} %get-tuple-element.41), channel_id=1, source_target_pairs={{0,4},{2,6},{4,0},{6,2},{1,5},{3,7},{5,1},{7,3},{8,12},{10,14},{12... | collective-permute-start | bytes 983048 | tf_op jit(solution)/shard_map/ppermute | solution.py:248
  74.3 8.7 %collective-permute-done.12.refs_2_ = bf16[2,128,640]{2,1,0:T(8,128)(2,1)S(1)} collective-permute-done((bf16[2,128,640]{2,1,0:T(8,128)(2,1)S(1)}, bf16[2,128,640]{2,1,0:T(8,128)(2,1)S(1)}, u32[]{:S(2)}, u32[]{:S(2)}) %collective-permute-start.12) | collective-permute-done | bytes 327712 | tf_op jit(solution)/shard_map/ppermute | solution.py:248
  83.0 6.1 %collective-permute-done.13.refs_3_ = bf16[2,128,640]{2,1,0:T(8,128)(2,1)S(1)} collective-permute-done((bf16[2,128,640]{2,1,0:T(8,128)(2,1)S(1)}, bf16[2,128,640]{2,1,0:T(8,128)(2,1)S(1)}, u32[]{:S(2)}, u32[]{:S(2)}) %collective-permute-start.13) | collective-permute-done | bytes 327712 | tf_op jit(solution)/shard_map/ppermute | solution.py:248
  89.1 1.3 %join.2 = (bf16[128,2560]{1,0:T(8,128)(2,1)}, bf16[128,2560]{1,0:T(8,128)(2,1)S(1)}, f32[128,128]{1,0:T(8,128)S(1)}) custom-call(s32[1]{0:T(128)} %bitcast.place, bf16[2,128,640]{2,1,0:T(8,128)(2,1)S(1)} %get-tuple-element.39.refs_0_, bf16[2,128,640]{2,1,0:T(8,128)(2,1)S(1)} %collective-permute-done.11.refs_1_, ...), custom_call_target="tpu_custom_call" | custom-call | flops 2200000000 | bytes 7000000 | tf_op jit(solution)/shard_map/join/pallas_call | solution.py:208
  90.4 7.1 %collective-permute-done.15 = bf16[4,2,128,640]{3,2,1,0:T(8,128)(2,1)S(1)} collective-permute-done((bf16[4,2,128,640]{3,2,1,0:T(8,128)(2,1)S(1)}, bf16[4,2,128,640]{3,2,1,0:T(8,128)(2,1)S(1)}, u32[]{:S(2)}, u32[]{:S(2)}) %collective-permute-start.15) | collective-permute-done | bytes 1310752 | tf_op jit(solution)/shard_map/ppermute | solution.py:253
  99.4 2.2 %collective-permute-start.18 = (bf16[2,128,640]{2,1,0:T(8,128)(2,1)S(1)}, bf16[2,128,640]{2,1,0:T(8,128)(2,1)S(1)}, u32[]{:S(2)}, u32[]{:S(2)}) collective-permute-start(bf16[2,128,640]{2,1,0:T(8,128)(2,1)S(1)} %get-tuple-element.53), channel_id=1, source_target_pairs={{0,4},{2,6},{4,0},{6,2},{1,5},{3,7},{5,1},{7,3},{8,12},{10,14},{12... | collective-permute-start | bytes 983048 | tf_op jit(solution)/shard_map/ppermute | solution.py:248
  102.9 2.4 %collective-permute-done.14 = f32[128]{0:T(128)S(1)} collective-permute-done((f32[128]{0:T(128)S(1)}, f32[128]{0:T(128)S(1)}, u32[]{:S(2)}, u32[]{:S(2)}) %collective-permute-start.14) | collective-permute-done | bytes 544 | tf_op jit(solution)/shard_map/ppermute | solution.py:260
  105.3 4.8 %collective-permute-done.18.refs_2_ = bf16[2,128,640]{2,1,0:T(8,128)(2,1)S(1)} collective-permute-done((bf16[2,128,640]{2,1,0:T(8,128)(2,1)S(1)}, bf16[2,128,640]{2,1,0:T(8,128)(2,1)S(1)}, u32[]{:S(2)}, u32[]{:S(2)}) %collective-permute-start.18) | collective-permute-done | bytes 327712 | tf_op jit(solution)/shard_map/ppermute | solution.py:248
  110.1 6.5 %collective-permute-done.19.refs_3_ = bf16[2,128,640]{2,1,0:T(8,128)(2,1)S(1)} collective-permute-done((bf16[2,128,640]{2,1,0:T(8,128)(2,1)S(1)}, bf16[2,128,640]{2,1,0:T(8,128)(2,1)S(1)}, u32[]{:S(2)}, u32[]{:S(2)}) %collective-permute-start.19) | collective-permute-done | bytes 327712 | tf_op jit(solution)/shard_map/ppermute | solution.py:248
  116.6 1.3 %join.3 = (bf16[128,2560]{1,0:T(8,128)(2,1)}, bf16[128,2560]{1,0:T(8,128)(2,1)S(1)}, f32[128,128]{1,0:T(8,128)S(1)}) custom-call(s32[1]{0:T(128)} %bitcast.place, bf16[2,128,640]{2,1,0:T(8,128)(2,1)S(1)} %get-tuple-element.55.refs_0_, bf16[2,128,640]{2,1,0:T(8,128)(2,1)S(1)} %collective-permute-done.17.refs_1_, ...), custom_call_target="tpu_custom_call" | custom-call | flops 2200000000 | bytes 7000000 | tf_op jit(solution)/shard_map/join/pallas_call | solution.py:208
  (67 shorter events, 17.1 us)
Async XLA Ops:
  0.6 7.4 %copy-start.1 = (bf16[128,2560]{1,0:T(8,128)(2,1)S(1)}, bf16[128,2560]{1,0:T(8,128)(2,1)}, u32[]{:S(2)}) copy-start(bf16[128,2560]{1,0:T(8,128)(2,1)} %refs_4_.3) | copy-start | bytes 1966084
  0.7 7.3 %copy-start.5 = (f32[2560]{0:T(1024)S(1)}, f32[2560]{0:T(1024)}, u32[]{:S(2)}) copy-start(f32[2560]{0:T(1024)} %param.14) | copy-start | bytes 30724
  0.7 7.6 %copy-start.2 = (bf16[128,2560]{1,0:T(8,128)(2,1)S(1)}, bf16[128,2560]{1,0:T(8,128)(2,1)}, u32[]{:S(2)}) copy-start(bf16[128,2560]{1,0:T(8,128)(2,1)} %param.11) | copy-start | bytes 1966084
  3.4 4.6 %collective-permute-start = (f32[2,128]{1,0:T(2,128)S(1)}, f32[2,128]{1,0:T(2,128)S(1)}, u32[]{:S(2)}, u32[]{:S(2)}) collective-permute-start(f32[2,128]{1,0:T(2,128)S(1)} %pad_maximum_fusion.6), channel_id=1, source_target_pairs={{0,1},{1,0},{2,3},{3,2},{4,5},{5,4},{6,7},{7,6},{8,9},{9,8},{10,11... | collective-permute-start | bytes 3080 | tf_op jit(solution)/shard_map/ppermute | solution.py:260
  8.5 9.6 %collective-permute-start.3 = (bf16[2,128,640]{2,1,0:T(8,128)(2,1)S(1)}, bf16[2,128,640]{2,1,0:T(8,128)(2,1)S(1)}, u32[]{:S(2)}, u32[]{:S(2)}) collective-permute-start(bf16[2,128,640]{2,1,0:T(8,128)(2,1)S(1)} %pad_maximum_fusion.5), channel_id=1, source_target_pairs={{0,6},{2,4},{4,2},{6,0},{1,7},{3,5},{5,3},{7,1},{8,14},{10,12},{12... | collective-permute-start | bytes 983048 | tf_op jit(solution)/shard_map/ppermute | solution.py:248
  8.9 16.7 %collective-permute-start.2 = (bf16[2,128,640]{2,1,0:T(8,128)(2,1)S(1)}, bf16[2,128,640]{2,1,0:T(8,128)(2,1)S(1)}, u32[]{:S(2)}, u32[]{:S(2)}) collective-permute-start(bf16[2,128,640]{2,1,0:T(8,128)(2,1)S(1)} %pad_maximum_fusion.4), channel_id=1, source_target_pairs={{0,4},{2,6},{4,0},{6,2},{1,5},{3,7},{5,1},{7,3},{8,12},{10,14},{12... | collective-permute-start | bytes 983048 | tf_op jit(solution)/shard_map/ppermute | solution.py:248
  10.7 1.7 %collective-permute-start.1 = (bf16[2,128,640]{2,1,0:T(8,128)(2,1)S(1)}, bf16[2,128,640]{2,1,0:T(8,128)(2,1)S(1)}, u32[]{:S(2)}, u32[]{:S(2)}) collective-permute-start(bf16[2,128,640]{2,1,0:T(8,128)(2,1)S(1)} %pad_maximum_fusion.3), channel_id=1, source_target_pairs={{0,2},{2,0},{4,6},{6,4},{1,3},{3,1},{5,7},{7,5},{8,10},{10,8},{12,... | collective-permute-start | bytes 983048 | tf_op jit(solution)/shard_map/ppermute | solution.py:248
  12.5 22.8 %collective-permute-start.5 = (bf16[2,2,128,640]{3,2,1,0:T(8,128)(2,1)S(1)}, bf16[2,2,128,640]{3,2,1,0:T(8,128)(2,1)S(1)}, u32[]{:S(2)}, u32[]{:S(2)}) collective-permute-start(bf16[2,2,128,640]{3,2,1,0:T(8,128)(2,1)S(1)} %pad_maximum_fusion.1.refs_6_), channel_id=1, source_target_pairs={{0,8},{8,16},{16,24},{1,9},{9,17},{17,25},{2,10},{10,18},{18,26},{... | collective-permute-start | bytes 1966088 | tf_op jit(solution)/shard_map/ppermute | solution.py:253
  16.0 19.3 %collective-permute-start.6 = (bf16[2,2,128,640]{3,2,1,0:T(8,128)(2,1)S(1)}, bf16[2,2,128,640]{3,2,1,0:T(8,128)(2,1)S(1)}, u32[]{:S(2)}, u32[]{:S(2)}) collective-permute-start(bf16[2,2,128,640]{3,2,1,0:T(8,128)(2,1)S(1)} %pad_maximum_fusion.1.refs_6_), channel_id=1, source_target_pairs={{8,0},{16,8},{24,16},{9,1},{17,9},{25,17},{10,2},{18,10},{26,18},{... | collective-permute-start | bytes 1966088 | tf_op jit(solution)/shard_map/ppermute | solution.py:253
  25.6 9.7 %collective-permute-start.7 = (bf16[272,640]{1,0:T(8,128)(2,1)S(1)}, bf16[272,640]{1,0:T(8,128)(2,1)S(1)}, u32[]{:S(2)}, u32[]{:S(2)}) collective-permute-start(bf16[272,640]{1,0:T(8,128)(2,1)S(1)} %get-tuple-element.32), channel_id=1, source_target_pairs={{0,4},{2,6},{4,0},{6,2},{1,5},{3,7},{5,1},{7,3},{8,12},{10,14},{12... | collective-permute-start | bytes 1044488 | tf_op jit(solution)/shard_map/ppermute | solution.py:248
  35.3 18.5 %collective-permute-start.10 = (bf16[2,2,128,640]{3,2,1,0:T(8,128)(2,1)S(1)}, bf16[2,2,128,640]{3,2,1,0:T(8,128)(2,1)S(1)}, u32[]{:S(2)}, u32[]{:S(2)}) collective-permute-start(bf16[2,2,128,640]{3,2,1,0:T(8,128)(2,1)S(1)} %pad_maximum_fusion.refs_7_), channel_id=1, source_target_pairs={{8,0},{16,8},{24,16},{9,1},{17,9},{25,17},{10,2},{18,10},{26,18},{... | collective-permute-start | bytes 1966088 | tf_op jit(solution)/shard_map/ppermute | solution.py:253
  36.5 18.4 %collective-permute-start.9 = (bf16[2,2,128,640]{3,2,1,0:T(8,128)(2,1)S(1)}, bf16[2,2,128,640]{3,2,1,0:T(8,128)(2,1)S(1)}, u32[]{:S(2)}, u32[]{:S(2)}) collective-permute-start(bf16[2,2,128,640]{3,2,1,0:T(8,128)(2,1)S(1)} %pad_maximum_fusion.refs_7_), channel_id=1, source_target_pairs={{0,8},{8,16},{16,24},{1,9},{9,17},{17,25},{2,10},{10,18},{18,26},{... | collective-permute-start | bytes 1966088 | tf_op jit(solution)/shard_map/ppermute | solution.py:253
  41.6 1.7 %collective-permute-start.4 = (bf16[272,640]{1,0:T(8,128)(2,1)S(1)}, bf16[272,640]{1,0:T(8,128)(2,1)S(1)}, u32[]{:S(2)}, u32[]{:S(2)}) collective-permute-start(bf16[272,640]{1,0:T(8,128)(2,1)S(1)} %get-tuple-element.29), channel_id=1, source_target_pairs={{0,2},{2,0},{4,6},{6,4},{1,3},{3,1},{5,7},{7,5},{8,10},{10,8},{12,... | collective-permute-start | bytes 1044488 | tf_op jit(solution)/shard_map/ppermute | solution.py:248
  41.7 9.9 %collective-permute-start.8 = (bf16[272,640]{1,0:T(8,128)(2,1)S(1)}, bf16[272,640]{1,0:T(8,128)(2,1)S(1)}, u32[]{:S(2)}, u32[]{:S(2)}) collective-permute-start(bf16[272,640]{1,0:T(8,128)(2,1)S(1)} %get-tuple-element.34), channel_id=1, source_target_pairs={{0,6},{2,4},{4,2},{6,0},{1,7},{3,5},{5,3},{7,1},{8,14},{10,12},{12... | collective-permute-start | bytes 1044488 | tf_op jit(solution)/shard_map/ppermute | solution.py:248
  65.9 31.6 %collective-permute-start.15 = (bf16[4,2,128,640]{3,2,1,0:T(8,128)(2,1)S(1)}, bf16[4,2,128,640]{3,2,1,0:T(8,128)(2,1)S(1)}, u32[]{:S(2)}, u32[]{:S(2)}) collective-permute-start(bf16[4,2,128,640]{3,2,1,0:T(8,128)(2,1)S(1)} %get-tuple-element.47), channel_id=1, source_target_pairs={{8,0},{16,8},{24,16},{9,1},{17,9},{25,17},{10,2},{18,10},{26,18},{... | collective-permute-start | bytes 3932168 | tf_op jit(solution)/shard_map/ppermute | solution.py:253
  67.2 31.5 %collective-permute-start.16 = (bf16[4,2,128,640]{3,2,1,0:T(8,128)(2,1)S(1)}, bf16[4,2,128,640]{3,2,1,0:T(8,128)(2,1)S(1)}, u32[]{:S(2)}, u32[]{:S(2)}) collective-permute-start(bf16[4,2,128,640]{3,2,1,0:T(8,128)(2,1)S(1)} %get-tuple-element.48), channel_id=1, source_target_pairs={{0,8},{8,16},{16,24},{1,9},{9,17},{17,25},{2,10},{10,18},{18,26},{... | collective-permute-start | bytes 3932168 | tf_op jit(solution)/shard_map/ppermute | solution.py:253
  72.3 2.0 %collective-permute-start.11 = (bf16[2,128,640]{2,1,0:T(8,128)(2,1)S(1)}, bf16[2,128,640]{2,1,0:T(8,128)(2,1)S(1)}, u32[]{:S(2)}, u32[]{:S(2)}) collective-permute-start(bf16[2,128,640]{2,1,0:T(8,128)(2,1)S(1)} %get-tuple-element.40), channel_id=1, source_target_pairs={{0,2},{2,0},{4,6},{6,4},{1,3},{3,1},{5,7},{7,5},{8,10},{10,8},{12,... | collective-permute-start | bytes 983048 | tf_op jit(solution)/shard_map/ppermute | solution.py:248
  72.4 10.6 %collective-permute-start.12 = (bf16[2,128,640]{2,1,0:T(8,128)(2,1)S(1)}, bf16[2,128,640]{2,1,0:T(8,128)(2,1)S(1)}, u32[]{:S(2)}, u32[]{:S(2)}) collective-permute-start(bf16[2,128,640]{2,1,0:T(8,128)(2,1)S(1)} %get-tuple-element.41), channel_id=1, source_target_pairs={{0,4},{2,6},{4,0},{6,2},{1,5},{3,7},{5,1},{7,3},{8,12},{10,14},{12... | collective-permute-start | bytes 983048 | tf_op jit(solution)/shard_map/ppermute | solution.py:248
  73.9 15.2 %collective-permute-start.13 = (bf16[2,128,640]{2,1,0:T(8,128)(2,1)S(1)}, bf16[2,128,640]{2,1,0:T(8,128)(2,1)S(1)}, u32[]{:S(2)}, u32[]{:S(2)}) collective-permute-start(bf16[2,128,640]{2,1,0:T(8,128)(2,1)S(1)} %get-tuple-element.42), channel_id=1, source_target_pairs={{0,6},{2,4},{4,2},{6,0},{1,7},{3,5},{5,3},{7,1},{8,14},{10,12},{12... | collective-permute-start | bytes 983048 | tf_op jit(solution)/shard_map/ppermute | solution.py:248
  99.3 6.0 %collective-permute-start.17 = (bf16[2,128,640]{2,1,0:T(8,128)(2,1)S(1)}, bf16[2,128,640]{2,1,0:T(8,128)(2,1)S(1)}, u32[]{:S(2)}, u32[]{:S(2)}) collective-permute-start(bf16[2,128,640]{2,1,0:T(8,128)(2,1)S(1)} %get-tuple-element.54), channel_id=1, source_target_pairs={{0,2},{2,0},{4,6},{6,4},{1,3},{3,1},{5,7},{7,5},{8,10},{10,8},{12,... | collective-permute-start | bytes 983048 | tf_op jit(solution)/shard_map/ppermute | solution.py:248
  99.4 10.7 %collective-permute-start.18 = (bf16[2,128,640]{2,1,0:T(8,128)(2,1)S(1)}, bf16[2,128,640]{2,1,0:T(8,128)(2,1)S(1)}, u32[]{:S(2)}, u32[]{:S(2)}) collective-permute-start(bf16[2,128,640]{2,1,0:T(8,128)(2,1)S(1)} %get-tuple-element.53), channel_id=1, source_target_pairs={{0,4},{2,6},{4,0},{6,2},{1,5},{3,7},{5,1},{7,3},{8,12},{10,14},{12... | collective-permute-start | bytes 983048 | tf_op jit(solution)/shard_map/ppermute | solution.py:248
  101.5 15.1 %collective-permute-start.19 = (bf16[2,128,640]{2,1,0:T(8,128)(2,1)S(1)}, bf16[2,128,640]{2,1,0:T(8,128)(2,1)S(1)}, u32[]{:S(2)}, u32[]{:S(2)}) collective-permute-start(bf16[2,128,640]{2,1,0:T(8,128)(2,1)S(1)} %get-tuple-element.52), channel_id=1, source_target_pairs={{0,6},{2,4},{4,2},{6,0},{1,7},{3,5},{5,3},{7,1},{8,14},{10,12},{12... | collective-permute-start | bytes 983048 | tf_op jit(solution)/shard_map/ppermute | solution.py:248
  101.7 3.6 %collective-permute-start.14 = (f32[128]{0:T(128)S(1)}, f32[128]{0:T(128)S(1)}, u32[]{:S(2)}, u32[]{:S(2)}) collective-permute-start(f32[128]{0:T(128)S(1)} %slice_reduce_fusion.1), channel_id=1, source_target_pairs={{0,1},{1,0},{2,3},{3,2},{4,5},{5,4},{6,7},{7,6},{8,9},{9,8},{10,11... | collective-permute-start | bytes 1544 | tf_op jit(solution)/shard_map/ppermute | solution.py:260
  118.0 3.6 %collective-permute-start.20 = (f32[128]{0:T(128)S(1)}, f32[128]{0:T(128)S(1)}, u32[]{:S(2)}, u32[]{:S(2)}) collective-permute-start(f32[128]{0:T(128)S(1)} %slice_reduce_fusion), channel_id=1, source_target_pairs={{0,1},{1,0},{2,3},{3,2},{4,5},{5,4},{6,7},{7,6},{8,9},{9,8},{10,11... | collective-permute-start | bytes 1544 | tf_op jit(solution)/shard_map/ppermute | solution.py:260
  (5 other events, 24.1 us)

commit v3 on v2

--- a/solution.py
+++ b/solution.py
@@ -47,7 +47,8 @@
 
 
 def chunks_of(heads):
-    return [(0, heads)]
+    first = (heads + 1) // 2
+    return [(0, first), (first, heads - first)] if heads > 1 else [(0, heads)]
 
 
 def busy(us):
@@ -58,7 +59,7 @@
     return lax.dot_general(a, b, (((ca,), (cb,)), ((), ())), preferred_element_type=f32)
 
 
-def attend(place, *refs, plan, first, heads):
+def attend(place, *refs, plan, first, heads, going_on):
     group, nd, noff = plan.group, len(plan.distances), len(plan.offsets)
     it = iter(refs)
     packs = group // plan.pack
@@ -68,6 +69,8 @@
 
     qd = [next(it) for _ in range(group)]
     kv = [unpacked() for _ in range(nd)]
+    for _ in range(group if going_on else 0):
+        next(it)
     out_oq = [next(it) for _ in range(group)]
     out_kv = [next(it) for _ in range(nd)]
     keys, vals, queries, grads, weights, scored, outs, dqs, allow = (next(it) for _ in range(9))
@@ -118,8 +121,8 @@
             dqs[rows(s), :] = dot(ds[s], k[s], 1, 0).astype(bf16)
 
         for m in range(group):
-            out_oq[m][0, :, target] = outs[rows(m ^ r), :]
-            out_oq[m][1, :, target] = dqs[rows(m ^ r), :]
+            out_oq[m][0, :, source] = outs[rows(m ^ r), :]
+            out_oq[m][1, :, source] = dqs[rows(m ^ r), :]
 
         for d in range(nd):
             for s in range(group):
@@ -142,7 +145,7 @@
     lax.fori_loop(0, heads, one_head, 0)
 
 
-def attention(place, qd, kv, plan, first, heads):
+def attention(place, qd, kv, oq, plan, first, heads):
     width = heads * HEAD
     group, nd, noff = plan.group, len(plan.distances), len(plan.offsets)
     ng = nd * group
@@ -151,16 +154,21 @@
     keyed = pl.BlockSpec((plan.pack, 2, HEAD, HEAD), lambda h, _: (0, 0, 0, h + first))
     packs = group // plan.pack
     whole = pl.BlockSpec(memory_space=pltpu.VMEM)
-    outs = [jax.ShapeDtypeStruct((2, HEAD, width), bf16)] * group + [
+    args = [place, *qd, *[pack for block in kv for pack in block]]
+    used = len(args)
+    args += [] if oq is None else oq
+    outs = [jax.ShapeDtypeStruct((2, HEAD, plan.heads * HEAD), bf16)] * group + [
         jax.ShapeDtypeStruct((group, 2, HEAD, width), f32 if by == 0 else bf16)
         for by in plan.distances
     ]
     result = pl.pallas_call(
-        functools.partial(attend, plan=plan, first=first, heads=heads),
+        functools.partial(
+            attend, plan=plan, first=first, heads=heads, going_on=oq is not None
+        ),
         grid_spec=pltpu.PrefetchScalarGridSpec(
             num_scalar_prefetch=1,
             grid=(),
-            in_specs=[whole] * (group + nd * packs),
+            in_specs=[whole] * (len(args) - 1),
             out_specs=[whole] * (group + nd),
             scratch_shapes=[pltpu.VMEM((ng * HEAD, HEAD), bf16)] * 2
             + [pltpu.VMEM((group * HEAD, HEAD), bf16)] * 2
@@ -170,22 +178,23 @@
         ),
         out_shape=outs,
         compiler_params=pltpu.CompilerParams(vmem_limit_bytes=36 * 2**20),
+        input_output_aliases={} if oq is None else {used + m: m for m in range(group)},
         cost_estimate=busy(4 * heads),
         name="attend",
-    )(place, *qd, *[pack for block in kv for pack in block])
+    )(*args)
     return result[:group], result[group:]
 
 
-def join(place, *refs, plan):
+def join(place, *refs, plan, chunks):
     group = plan.group
-    count = len(plan.chunks) * group
+    count = len(chunks) * group
     parts = refs[:count]
     raw_ref, rstd_ref, gain_ref, plain, normed, inner = refs[count:]
     r = place[0]
     column = jnp.transpose(jnp.broadcast_to(rstd_ref[...], (HEAD, HEAD)))[:, 0:1]
     width = plan.heads * HEAD
     total = jnp.zeros((HEAD, HEAD), f32)
-    for c, (first, heads) in enumerate(plan.chunks):
+    for c, (first, heads) in enumerate(chunks):
         for m in range(group):
             base = (m ^ r) * width + first * HEAD
             part = parts[c * group + m]
@@ -201,12 +210,12 @@
     )
 
 
-def joined(place, parts, raw, rstd, gain, plan):
+def joined(place, parts, raw, rstd, gain, plan, chunks):
     shape = raw.shape
     flat = [x for chunk in parts for x in chunk]
     whole = pl.BlockSpec(memory_space=pltpu.VMEM)
     return pl.pallas_call(
-        functools.partial(join, plan=plan),
+        functools.partial(join, plan=plan, chunks=chunks),
         grid_spec=pltpu.PrefetchScalarGridSpec(
             num_scalar_prefetch=1,
             grid=(),
@@ -297,24 +306,29 @@
     packs, near, qd[group // 2 % group] = lax.optimization_barrier((packs, near, qd[group // 2 % group]))
     kv = [[x] + [moved(y, -by) for y in packs] for x, by in zip(near, distances)]
 
-    oq_back, kv_back = [], []
+    oq = None
+    back = []
     for first, count in plan.chunks:
-        oq_parts, kv_parts = attention(place, qd, kv, plan, first, count)
-        oq_back.append([swap(x, m) for m, x in enumerate(oq_parts)])
-        back = [moved(kv_parts[d], by) for d, by in enumerate(distances) if by]
+        oq, kv_parts = attention(place, qd, kv, oq, plan, first, count)
+        sent = [moved(kv_parts[d], by) for d, by in enumerate(distances) if by]
+        back.append((kv_parts[plan.home], sent))
+    oq = [swap(x, m) for m, x in enumerate(oq)]
+    attended, query_norm_grad, query_inner = joined(
+        place, [oq], query_vectors, my_rstd[1:2], query_gain, plan, [(0, plan.heads)]
+    )
+    kv_back = []
+    for own, sent in back:
+        if kv_back:
+            sent, kv_back[-1] = lax.optimization_barrier((sent, kv_back[-1]))
         total = []
         for m in range(group):
-            x = kv_parts[plan.home][m]
-            for y in back:
+            x = own[m]
+            for y in sent:
                 x = x + y[m].astype(f32)
             total.append(swap(x.astype(bf16), m))
         kv_back.append(total)
-
-    attended, query_norm_grad, query_inner = joined(
-        place, oq_back, query_vectors, my_rstd[1:2], query_gain, plan
-    )
     value_grad, key_norm_grad, key_inner = joined(
-        place, kv_back, key_vectors, my_rstd[0:1], key_gain, plan
+        place, kv_back, key_vectors, my_rstd[0:1], key_gain, plan, plan.chunks
     )
 
     def finished(raw, rstd, gain, grad, inner):

time: 123 us -> 113 us (0.919)
  waiting for transfers between devices: 69.6 us -> 50.2 us
  starting transfers between devices: 30.5 us -> 39.8 us
    ppermute x12 -> x15, waiting for transfers between devices: 53.7 us -> 35.5 us  [swap(): lax.ppermute(x, 'place', [(i, i ^ m) for i in range(group)])]
    ppermute x6 -> x8, starting transfers between devices: 17.6 us -> 23.5 us  [moved(): lax.ppermute(x, 'block', [(i, i + by) for i in range(blocks) if 0 <= i +...]
    ppermute x12 -> x15, starting transfers between devices: 7.59 us -> 11.5 us  [swap(): lax.ppermute(x, 'place', [(i, i ^ m) for i in range(group)])]
    ppermute x3, waiting for transfers between devices: 4.29 us -> 2.09 us  [summed(): x = x + lax.ppermute(x, 'head', [(i, i ^ step) for i in range(count)])]
    ppermute x6 -> x8, waiting for transfers between devices: 11.6 us -> 12.6 us  [moved(): lax.ppermute(x, 'block', [(i, i + by) for i in range(blocks) if 0 <= i +...]
    pallas_call x1 -> x2, Pallas kernels: 10.9 us -> 11 us  [attention(): pl.pallas_call(functools.partial(attend, plan=plan, first=first, heads=he...]
  transfers between devices with their start and end apart: 21 -> 26, of which waited for: 17 -> 17; matrix products, arithmetic and copies ran while one was open for 2% -> 3% of each run, Pallas kernels for 1% -> 5%
where the time goes in v3:
time: 113 us
  waiting for transfers between devices  50.2 us (44%)
  starting transfers between devices  39.8 us (35%)
  Pallas kernels  13.6 us (12%)
  other arithmetic  6.99 us (6%)
  between operations  1.69 us (1%)
    ppermute x15, waiting for transfers between devices, swap(): lax.ppermute(x, 'place', [(i, i ^ m) for i in range(group)])  35.5 us
    ppermute x8, starting transfers between devices, moved(): lax.ppermute(x, 'block', [(i, i + by) for i in range(blocks) if 0 <= i +...  23.5 us
    ppermute x8, waiting for transfers between devices, moved(): lax.ppermute(x, 'block', [(i, i + by) for i in range(blocks) if 0 <= i +...  12.6 us
    ppermute x15, starting transfers between devices, swap(): lax.ppermute(x, 'place', [(i, i ^ m) for i in range(group)])  11.5 us
    pallas_call x2, Pallas kernels, attention(): pl.pallas_call(functools.partial(attend, plan=plan, first=first, heads=he...  11 us
    ppermute x3, starting transfers between devices, summed(): x = x + lax.ppermute(x, 'head', [(i, i ^ step) for i in range(count)])  4.77 us
    reduce_sum x2, other arithmetic, local(): jnp.sum(jnp.square(x.astype(f32)), axis=1)  2.7 us
    pallas_call x2, Pallas kernels, joined(): pl.pallas_call(functools.partial(join, plan=plan, chunks=chunks), grid_sp...  2.66 us
  transfers between devices with their start and end apart: 26, of which 17 were waited for; matrix products, arithmetic and copies ran while one was open for 3% of the time, Pallas kernels for 5%

profile of v3, /device:TPU:0, one launch (start us, length us, event | category | flops | bytes accessed | tf_op | source)
XLA Modules:
  0.0 112.9 jit_solution(6621935353249485111)
XLA Ops:
  0.7 1.4 %fusion.12 = f32[128]{0:T(128)S(1)} fusion(bf16[128,2560]{1,0:T(8,128)(2,1)} %refs_8_.1), kind=kLoop, calls=%fused_computation.16 | loop fusion | flops 982912 | bytes 655872 | tf_op jit(solution)/shard_map/reduce_sum | solution.py:280
  3.4 3.0 %collective-permute-start = (f32[2,128]{1,0:T(2,128)S(1)}, f32[2,128]{1,0:T(2,128)S(1)}, u32[]{:S(2)}, u32[]{:S(2)}) collective-permute-start(f32[2,128]{1,0:T(2,128)S(1)} %pad_maximum_fusion.6), channel_id=1, source_target_pairs={{0,1},{1,0},{2,3},{3,2},{4,5},{5,4},{6,7},{7,6},{8,9},{9,8},{10,11... | collective-permute-start | bytes 3080 | tf_op jit(solution)/shard_map/ppermute | solution.py:269
  8.6 2.2 %collective-permute-start.3 = (bf16[2,128,640]{2,1,0:T(8,128)(2,1)S(1)}, bf16[2,128,640]{2,1,0:T(8,128)(2,1)S(1)}, u32[]{:S(2)}, u32[]{:S(2)}) collective-permute-start(bf16[2,128,640]{2,1,0:T(8,128)(2,1)S(1)} %pad_maximum_fusion.5), channel_id=1, source_target_pairs={{0,6},{2,4},{4,2},{6,0},{1,7},{3,5},{5,3},{7,1},{8,14},{10,12},{12... | collective-permute-start | bytes 983048 | tf_op jit(solution)/shard_map/ppermute | solution.py:257
  11.3 4.1 %collective-permute-start.5 = (bf16[2,2,128,640]{3,2,1,0:T(8,128)(2,1)S(1)}, bf16[2,2,128,640]{3,2,1,0:T(8,128)(2,1)S(1)}, u32[]{:S(2)}, u32[]{:S(2)}) collective-permute-start(bf16[2,2,128,640]{3,2,1,0:T(8,128)(2,1)S(1)} %pad_maximum_fusion.1.refs_6_), channel_id=1, source_target_pairs={{0,8},{8,16},{16,24},{1,9},{9,17},{17,25},{2,10},{10,18},{18,26},{... | collective-permute-start | bytes 1966088 | tf_op jit(solution)/shard_map/ppermute | solution.py:262
  17.2 1.6 %collective-permute-done.3 = bf16[2,128,640]{2,1,0:T(8,128)(2,1)S(1)} collective-permute-done((bf16[2,128,640]{2,1,0:T(8,128)(2,1)S(1)}, bf16[2,128,640]{2,1,0:T(8,128)(2,1)S(1)}, u32[]{:S(2)}, u32[]{:S(2)}) %collective-permute-start.3) | collective-permute-done | bytes 327712 | tf_op jit(solution)/shard_map/ppermute | solution.py:257
  18.8 7.2 %collective-permute-done.2 = bf16[2,128,640]{2,1,0:T(8,128)(2,1)S(1)} collective-permute-done((bf16[2,128,640]{2,1,0:T(8,128)(2,1)S(1)}, bf16[2,128,640]{2,1,0:T(8,128)(2,1)S(1)}, u32[]{:S(2)}, u32[]{:S(2)}) %collective-permute-start.2) | collective-permute-done | bytes 327712 | tf_op jit(solution)/shard_map/ppermute | solution.py:257
  26.0 1.6 %collective-permute-start.7 = (bf16[272,640]{1,0:T(8,128)(2,1)S(1)}, bf16[272,640]{1,0:T(8,128)(2,1)S(1)}, u32[]{:S(2)}, u32[]{:S(2)}) collective-permute-start(bf16[272,640]{1,0:T(8,128)(2,1)S(1)} %get-tuple-element.45), channel_id=1, source_target_pairs={{0,4},{2,6},{4,0},{6,2},{1,5},{3,7},{5,1},{7,3},{8,12},{10,14},{12... | collective-permute-start | bytes 1044488 | tf_op jit(solution)/shard_map/ppermute | solution.py:257
  27.8 8.1 %collective-permute-done.7.refs_2_ = bf16[272,640]{1,0:T(8,128)(2,1)S(1)} collective-permute-done((bf16[272,640]{1,0:T(8,128)(2,1)S(1)}, bf16[272,640]{1,0:T(8,128)(2,1)S(1)}, u32[]{:S(2)}, u32[]{:S(2)}) %collective-permute-start.7) | collective-permute-done | bytes 348192 | tf_op jit(solution)/shard_map/ppermute | solution.py:257
  37.2 4.6 %collective-permute-start.9 = (bf16[2,2,128,640]{3,2,1,0:T(8,128)(2,1)S(1)}, bf16[2,2,128,640]{3,2,1,0:T(8,128)(2,1)S(1)}, u32[]{:S(2)}, u32[]{:S(2)}) collective-permute-start(bf16[2,2,128,640]{3,2,1,0:T(8,128)(2,1)S(1)} %pad_maximum_fusion.refs_7_), channel_id=1, source_target_pairs={{0,8},{8,16},{16,24},{1,9},{9,17},{17,25},{2,10},{10,18},{18,26},{... | collective-permute-start | bytes 1966088 | tf_op jit(solution)/shard_map/ppermute | solution.py:262
  41.9 1.5 %collective-permute-start.8 = (bf16[272,640]{1,0:T(8,128)(2,1)S(1)}, bf16[272,640]{1,0:T(8,128)(2,1)S(1)}, u32[]{:S(2)}, u32[]{:S(2)}) collective-permute-start(bf16[272,640]{1,0:T(8,128)(2,1)S(1)} %get-tuple-element.47), channel_id=1, source_target_pairs={{0,6},{2,4},{4,2},{6,0},{1,7},{3,5},{5,3},{7,1},{8,14},{10,12},{12... | collective-permute-start | bytes 1044488 | tf_op jit(solution)/shard_map/ppermute | solution.py:257
  43.5 8.3 %collective-permute-done.8.refs_3_ = bf16[272,640]{1,0:T(8,128)(2,1)S(1)} collective-permute-done((bf16[272,640]{1,0:T(8,128)(2,1)S(1)}, bf16[272,640]{1,0:T(8,128)(2,1)S(1)}, u32[]{:S(2)}, u32[]{:S(2)}) %collective-permute-start.8) | collective-permute-done | bytes 348192 | tf_op jit(solution)/shard_map/ppermute | solution.py:257
  51.8 1.5 %collective-permute-done.10.refs_9_ = bf16[2,2,128,640]{3,2,1,0:T(8,128)(2,1)S(1)} collective-permute-done((bf16[2,2,128,640]{3,2,1,0:T(8,128)(2,1)S(1)}, bf16[2,2,128,640]{3,2,1,0:T(8,128)(2,1)S(1)}, u32[]{:S(2)}, u32[]{:S(2)}) %collective-permute-start.10) | collective-permute-done | bytes 655392 | tf_op jit(solution)/shard_map/ppermute | solution.py:262
  54.5 6.6 %attend.2 = (bf16[2,128,640]{2,1,0:T(8,128)(2,1)S(1)}, bf16[2,128,640]{2,1,0:T(8,128)(2,1)S(1)}, bf16[2,128,640]{2,1,0:T(8,128)(2,1)S(1)}, bf16[2,128,640]{2,1,0...) custom-call(s32[1]{0:T(128)} %bitcast.place, ...), custom_call_target="tpu_custom_call" | custom-call | flops 13200000000 | bytes 42000000 | tf_op jit(solution)/shard_map/attend/pallas_call | solution.py:164
  62.4 5.1 %collective-permute-start.18 = (bf16[4,2,128,384]{3,2,1,0:T(8,128)(2,1)S(1)}, bf16[4,2,128,384]{3,2,1,0:T(8,128)(2,1)S(1)}, u32[]{:S(2)}, u32[]{:S(2)}) collective-permute-start(bf16[4,2,128,384]{3,2,1,0:T(8,128)(2,1)S(1)} %get-tuple-element.67), channel_id=1, source_target_pairs={{0,8},{8,16},{16,24},{1,9},{9,17},{17,25},{2,10},{10,18},{18,26},{... | collective-permute-start | bytes 2359304 | tf_op jit(solution)/shard_map/ppermute | solution.py:262
  67.5 4.4 %attend.3 = (bf16[2,128,640]{2,1,0:T(8,128)(2,1)S(1)}, bf16[2,128,640]{2,1,0:T(8,128)(2,1)S(1)}, bf16[2,128,640]{2,1,0:T(8,128)(2,1)S(1)}, bf16[2,128,640]{2,1,0...) custom-call(s32[1]{0:T(128)} %bitcast.place, ...), custom_call_target="tpu_custom_call", output_to_operand_aliasing={{0}: (11, {}), {1}: (12, {}), {2}: (13, {}), {3}: (14, {})} | custom-call | flops 8800000000 | bytes 28000000 | tf_op jit(solution)/shard_map/attend/pallas_call | solution.py:164
  73.8 7.0 %collective-permute-done.17 = bf16[4,2,128,384]{3,2,1,0:T(8,128)(2,1)S(1)} collective-permute-done((bf16[4,2,128,384]{3,2,1,0:T(8,128)(2,1)S(1)}, bf16[4,2,128,384]{3,2,1,0:T(8,128)(2,1)S(1)}, u32[]{:S(2)}, u32[]{:S(2)}) %collective-permute-start.17) | collective-permute-done | bytes 786464 | tf_op jit(solution)/shard_map/ppermute | solution.py:262
  82.2 4.6 %collective-permute-start.16 = (bf16[4,2,128,256]{3,2,1,0:T(8,128)(2,1)S(1)}, bf16[4,2,128,256]{3,2,1,0:T(8,128)(2,1)S(1)}, u32[]{:S(2)}, u32[]{:S(2)}) collective-permute-start(bf16[4,2,128,256]{3,2,1,0:T(8,128)(2,1)S(1)} %get-tuple-element.64), channel_id=1, source_target_pairs={{0,8},{8,16},{16,24},{1,9},{9,17},{17,25},{2,10},{10,18},{18,26},{... | collective-permute-start | bytes 1572872 | tf_op jit(solution)/shard_map/ppermute | solution.py:262
  89.8 1.3 %join.2 = (bf16[128,2560]{1,0:T(8,128)(2,1)}, bf16[128,2560]{1,0:T(8,128)(2,1)S(1)}, f32[128,128]{1,0:T(8,128)S(1)}) custom-call(s32[1]{0:T(128)} %bitcast.place, bf16[2,128,640]{2,1,0:T(8,128)(2,1)S(1)} %get-tuple-element.56.refs_0_, bf16[2,128,640]{2,1,0:T(8,128)(2,1)S(1)} %collective-permute-done.11.refs_1_, ...), custom_call_target="tpu_custom_call" | custom-call | flops 2200000000 | bytes 7000000 | tf_op jit(solution)/shard_map/join/pallas_call | solution.py:217
  91.2 2.4 %collective-permute-done.15 = bf16[4,2,128,256]{3,2,1,0:T(8,128)(2,1)S(1)} collective-permute-done((bf16[4,2,128,256]{3,2,1,0:T(8,128)(2,1)S(1)}, bf16[4,2,128,256]{3,2,1,0:T(8,128)(2,1)S(1)}, u32[]{:S(2)}, u32[]{:S(2)}) %collective-permute-start.15) | collective-permute-done | bytes 524320 | tf_op jit(solution)/shard_map/ppermute | solution.py:262
  94.9 3.3 %collective-permute-done.21.refs_3_ = bf16[2,128,384]{2,1,0:T(8,128)(2,1)S(1)} collective-permute-done((bf16[2,128,384]{2,1,0:T(8,128)(2,1)S(1)}, bf16[2,128,384]{2,1,0:T(8,128)(2,1)S(1)}, u32[]{:S(2)}, u32[]{:S(2)}) %collective-permute-start.21) | collective-permute-done | bytes 196640 | tf_op jit(solution)/shard_map/ppermute | solution.py:257
  100.4 4.7 %collective-permute-done.23.refs_6_ = bf16[2,128,256]{2,1,0:T(8,128)(2,1)S(1)} collective-permute-done((bf16[2,128,256]{2,1,0:T(8,128)(2,1)S(1)}, bf16[2,128,256]{2,1,0:T(8,128)(2,1)S(1)}, u32[]{:S(2)}, u32[]{:S(2)}) %collective-permute-start.23) | collective-permute-done | bytes 131104 | tf_op jit(solution)/shard_map/ppermute | solution.py:257
  105.2 1.4 %collective-permute-done.24.refs_7_ = bf16[2,128,256]{2,1,0:T(8,128)(2,1)S(1)} collective-permute-done((bf16[2,128,256]{2,1,0:T(8,128)(2,1)S(1)}, bf16[2,128,256]{2,1,0:T(8,128)(2,1)S(1)}, u32[]{:S(2)}, u32[]{:S(2)}) %collective-permute-start.24) | collective-permute-done | bytes 131104 | tf_op jit(solution)/shard_map/ppermute | solution.py:257
  106.5 1.3 %join.3 = (bf16[128,2560]{1,0:T(8,128)(2,1)}, bf16[128,2560]{1,0:T(8,128)(2,1)S(1)}, f32[128,128]{1,0:T(8,128)S(1)}) custom-call(s32[1]{0:T(128)} %bitcast.place, bf16[2,128,384]{2,1,0:T(8,128)(2,1)S(1)} %get-tuple-element.68.refs_0_, bf16[2,128,384]{2,1,0:T(8,128)(2,1)S(1)} %collective-permute-done.19.refs_1_, ...), custom_call_target="tpu_custom_call" | custom-call | flops 2200000000 | bytes 7000000 | tf_op jit(solution)/shard_map/join/pallas_call | solution.py:217
  110.2 1.4 %collective-permute-done.25 = f32[128]{0:T(128)S(1)} collective-permute-done((f32[128]{0:T(128)S(1)}, f32[128]{0:T(128)S(1)}, u32[]{:S(2)}, u32[]{:S(2)}) %collective-permute-start.25) | collective-permute-done | bytes 544 | tf_op jit(solution)/shard_map/ppermute | solution.py:269
  (79 shorter events, 22.4 us)
Async XLA Ops:
  3.4 4.6 %collective-permute-start = (f32[2,128]{1,0:T(2,128)S(1)}, f32[2,128]{1,0:T(2,128)S(1)}, u32[]{:S(2)}, u32[]{:S(2)}) collective-permute-start(f32[2,128]{1,0:T(2,128)S(1)} %pad_maximum_fusion.6), channel_id=1, source_target_pairs={{0,1},{1,0},{2,3},{3,2},{4,5},{5,4},{6,7},{7,6},{8,9},{9,8},{10,11... | collective-permute-start | bytes 3080 | tf_op jit(solution)/shard_map/ppermute | solution.py:269
  8.5 2.7 %collective-permute-start.1 = (bf16[2,128,640]{2,1,0:T(8,128)(2,1)S(1)}, bf16[2,128,640]{2,1,0:T(8,128)(2,1)S(1)}, u32[]{:S(2)}, u32[]{:S(2)}) collective-permute-start(bf16[2,128,640]{2,1,0:T(8,128)(2,1)S(1)} %pad_maximum_fusion.3), channel_id=1, source_target_pairs={{0,2},{2,0},{4,6},{6,4},{1,3},{3,1},{5,7},{7,5},{8,10},{10,8},{12,... | collective-permute-start | bytes 983048 | tf_op jit(solution)/shard_map/ppermute | solution.py:257
  8.6 10.2 %collective-permute-start.3 = (bf16[2,128,640]{2,1,0:T(8,128)(2,1)S(1)}, bf16[2,128,640]{2,1,0:T(8,128)(2,1)S(1)}, u32[]{:S(2)}, u32[]{:S(2)}) collective-permute-start(bf16[2,128,640]{2,1,0:T(8,128)(2,1)S(1)} %pad_maximum_fusion.5), channel_id=1, source_target_pairs={{0,6},{2,4},{4,2},{6,0},{1,7},{3,5},{5,3},{7,1},{8,14},{10,12},{12... | collective-permute-start | bytes 983048 | tf_op jit(solution)/shard_map/ppermute | solution.py:257
  10.8 15.3 %collective-permute-start.2 = (bf16[2,128,640]{2,1,0:T(8,128)(2,1)S(1)}, bf16[2,128,640]{2,1,0:T(8,128)(2,1)S(1)}, u32[]{:S(2)}, u32[]{:S(2)}) collective-permute-start(bf16[2,128,640]{2,1,0:T(8,128)(2,1)S(1)} %pad_maximum_fusion.4), channel_id=1, source_target_pairs={{0,4},{2,6},{4,0},{6,2},{1,5},{3,7},{5,1},{7,3},{8,12},{10,14},{12... | collective-permute-start | bytes 983048 | tf_op jit(solution)/shard_map/ppermute | solution.py:257
  11.3 24.6 %collective-permute-start.5 = (bf16[2,2,128,640]{3,2,1,0:T(8,128)(2,1)S(1)}, bf16[2,2,128,640]{3,2,1,0:T(8,128)(2,1)S(1)}, u32[]{:S(2)}, u32[]{:S(2)}) collective-permute-start(bf16[2,2,128,640]{3,2,1,0:T(8,128)(2,1)S(1)} %pad_maximum_fusion.1.refs_6_), channel_id=1, source_target_pairs={{0,8},{8,16},{16,24},{1,9},{9,17},{17,25},{2,10},{10,18},{18,26},{... | collective-permute-start | bytes 1966088 | tf_op jit(solution)/shard_map/ppermute | solution.py:262
  15.4 20.5 %collective-permute-start.6 = (bf16[2,2,128,640]{3,2,1,0:T(8,128)(2,1)S(1)}, bf16[2,2,128,640]{3,2,1,0:T(8,128)(2,1)S(1)}, u32[]{:S(2)}, u32[]{:S(2)}) collective-permute-start(bf16[2,2,128,640]{3,2,1,0:T(8,128)(2,1)S(1)} %pad_maximum_fusion.1.refs_6_), channel_id=1, source_target_pairs={{8,0},{16,8},{24,16},{9,1},{17,9},{25,17},{10,2},{18,10},{26,18},{... | collective-permute-start | bytes 1966088 | tf_op jit(solution)/shard_map/ppermute | solution.py:262
  26.0 9.8 %collective-permute-start.7 = (bf16[272,640]{1,0:T(8,128)(2,1)S(1)}, bf16[272,640]{1,0:T(8,128)(2,1)S(1)}, u32[]{:S(2)}, u32[]{:S(2)}) collective-permute-start(bf16[272,640]{1,0:T(8,128)(2,1)S(1)} %get-tuple-element.45), channel_id=1, source_target_pairs={{0,4},{2,6},{4,0},{6,2},{1,5},{3,7},{5,1},{7,3},{8,12},{10,14},{12... | collective-permute-start | bytes 1044488 | tf_op jit(solution)/shard_map/ppermute | solution.py:257
  35.9 17.4 %collective-permute-start.10 = (bf16[2,2,128,640]{3,2,1,0:T(8,128)(2,1)S(1)}, bf16[2,2,128,640]{3,2,1,0:T(8,128)(2,1)S(1)}, u32[]{:S(2)}, u32[]{:S(2)}) collective-permute-start(bf16[2,2,128,640]{3,2,1,0:T(8,128)(2,1)S(1)} %pad_maximum_fusion.refs_7_), channel_id=1, source_target_pairs={{8,0},{16,8},{24,16},{9,1},{17,9},{25,17},{10,2},{18,10},{26,18},{... | collective-permute-start | bytes 1966088 | tf_op jit(solution)/shard_map/ppermute | solution.py:262
  37.2 17.3 %collective-permute-start.9 = (bf16[2,2,128,640]{3,2,1,0:T(8,128)(2,1)S(1)}, bf16[2,2,128,640]{3,2,1,0:T(8,128)(2,1)S(1)}, u32[]{:S(2)}, u32[]{:S(2)}) collective-permute-start(bf16[2,2,128,640]{3,2,1,0:T(8,128)(2,1)S(1)} %pad_maximum_fusion.refs_7_), channel_id=1, source_target_pairs={{0,8},{8,16},{16,24},{1,9},{9,17},{17,25},{2,10},{10,18},{18,26},{... | collective-permute-start | bytes 1966088 | tf_op jit(solution)/shard_map/ppermute | solution.py:262
  41.9 9.9 %collective-permute-start.8 = (bf16[272,640]{1,0:T(8,128)(2,1)S(1)}, bf16[272,640]{1,0:T(8,128)(2,1)S(1)}, u32[]{:S(2)}, u32[]{:S(2)}) collective-permute-start(bf16[272,640]{1,0:T(8,128)(2,1)S(1)} %get-tuple-element.47), channel_id=1, source_target_pairs={{0,6},{2,4},{4,2},{6,0},{1,7},{3,5},{5,3},{7,1},{8,14},{10,12},{12... | collective-permute-start | bytes 1044488 | tf_op jit(solution)/shard_map/ppermute | solution.py:257
  61.1 19.8 %collective-permute-start.17 = (bf16[4,2,128,384]{3,2,1,0:T(8,128)(2,1)S(1)}, bf16[4,2,128,384]{3,2,1,0:T(8,128)(2,1)S(1)}, u32[]{:S(2)}, u32[]{:S(2)}) collective-permute-start(bf16[4,2,128,384]{3,2,1,0:T(8,128)(2,1)S(1)} %get-tuple-element.66), channel_id=1, source_target_pairs={{8,0},{16,8},{24,16},{9,1},{17,9},{25,17},{10,2},{18,10},{26,18},{... | collective-permute-start | bytes 2359304 | tf_op jit(solution)/shard_map/ppermute | solution.py:262
  62.4 19.8 %collective-permute-start.18 = (bf16[4,2,128,384]{3,2,1,0:T(8,128)(2,1)S(1)}, bf16[4,2,128,384]{3,2,1,0:T(8,128)(2,1)S(1)}, u32[]{:S(2)}, u32[]{:S(2)}) collective-permute-start(bf16[4,2,128,384]{3,2,1,0:T(8,128)(2,1)S(1)} %get-tuple-element.67), channel_id=1, source_target_pairs={{0,8},{8,16},{16,24},{1,9},{9,17},{17,25},{2,10},{10,18},{18,26},{... | collective-permute-start | bytes 2359304 | tf_op jit(solution)/shard_map/ppermute | solution.py:262
  71.9 15.2 %collective-permute-start.11 = (bf16[2,128,640]{2,1,0:T(8,128)(2,1)S(1)}, bf16[2,128,640]{2,1,0:T(8,128)(2,1)S(1)}, u32[]{:S(2)}, u32[]{:S(2)}) collective-permute-start(bf16[2,128,640]{2,1,0:T(8,128)(2,1)S(1)} %get-tuple-element.57), channel_id=1, source_target_pairs={{0,2},{2,0},{4,6},{6,4},{1,3},{3,1},{5,7},{7,5},{8,10},{10,8},{12,... | collective-permute-start | bytes 983048 | tf_op jit(solution)/shard_map/ppermute | solution.py:257
  71.9 15.2 %collective-permute-start.12 = (bf16[2,128,640]{2,1,0:T(8,128)(2,1)S(1)}, bf16[2,128,640]{2,1,0:T(8,128)(2,1)S(1)}, u32[]{:S(2)}, u32[]{:S(2)}) collective-permute-start(bf16[2,128,640]{2,1,0:T(8,128)(2,1)S(1)} %get-tuple-element.58), channel_id=1, source_target_pairs={{0,4},{2,6},{4,0},{6,2},{1,5},{3,7},{5,1},{7,3},{8,12},{10,14},{12... | collective-permute-start | bytes 983048 | tf_op jit(solution)/shard_map/ppermute | solution.py:257
  73.0 15.6 %collective-permute-start.13 = (bf16[2,128,640]{2,1,0:T(8,128)(2,1)S(1)}, bf16[2,128,640]{2,1,0:T(8,128)(2,1)S(1)}, u32[]{:S(2)}, u32[]{:S(2)}) collective-permute-start(bf16[2,128,640]{2,1,0:T(8,128)(2,1)S(1)} %get-tuple-element.59), channel_id=1, source_target_pairs={{0,6},{2,4},{4,2},{6,0},{1,7},{3,5},{5,3},{7,1},{8,14},{10,12},{12... | collective-permute-start | bytes 983048 | tf_op jit(solution)/shard_map/ppermute | solution.py:257
  80.9 12.8 %collective-permute-start.15 = (bf16[4,2,128,256]{3,2,1,0:T(8,128)(2,1)S(1)}, bf16[4,2,128,256]{3,2,1,0:T(8,128)(2,1)S(1)}, u32[]{:S(2)}, u32[]{:S(2)}) collective-permute-start(bf16[4,2,128,256]{3,2,1,0:T(8,128)(2,1)S(1)} %get-tuple-element.63), channel_id=1, source_target_pairs={{8,0},{16,8},{24,16},{9,1},{17,9},{25,17},{10,2},{18,10},{26,18},{... | collective-permute-start | bytes 1572872 | tf_op jit(solution)/shard_map/ppermute | solution.py:262
  82.2 12.7 %collective-permute-start.16 = (bf16[4,2,128,256]{3,2,1,0:T(8,128)(2,1)S(1)}, bf16[4,2,128,256]{3,2,1,0:T(8,128)(2,1)S(1)}, u32[]{:S(2)}, u32[]{:S(2)}) collective-permute-start(bf16[4,2,128,256]{3,2,1,0:T(8,128)(2,1)S(1)} %get-tuple-element.64), channel_id=1, source_target_pairs={{0,8},{8,16},{16,24},{1,9},{9,17},{17,25},{2,10},{10,18},{18,26},{... | collective-permute-start | bytes 1572872 | tf_op jit(solution)/shard_map/ppermute | solution.py:262
  87.1 7.8 %collective-permute-start.19 = (bf16[2,128,384]{2,1,0:T(8,128)(2,1)S(1)}, bf16[2,128,384]{2,1,0:T(8,128)(2,1)S(1)}, u32[]{:S(2)}, u32[]{:S(2)}) collective-permute-start(bf16[2,128,384]{2,1,0:T(8,128)(2,1)S(1)} %get-tuple-element.80), channel_id=1, source_target_pairs={{0,2},{2,0},{4,6},{6,4},{1,3},{3,1},{5,7},{7,5},{8,10},{10,8},{12,... | collective-permute-start | bytes 589832 | tf_op jit(solution)/shard_map/ppermute | solution.py:257
  87.2 7.8 %collective-permute-start.20 = (bf16[2,128,384]{2,1,0:T(8,128)(2,1)S(1)}, bf16[2,128,384]{2,1,0:T(8,128)(2,1)S(1)}, u32[]{:S(2)}, u32[]{:S(2)}) collective-permute-start(bf16[2,128,384]{2,1,0:T(8,128)(2,1)S(1)} %get-tuple-element.79), channel_id=1, source_target_pairs={{0,4},{2,6},{4,0},{6,2},{1,5},{3,7},{5,1},{7,3},{8,12},{10,14},{12... | collective-permute-start | bytes 589832 | tf_op jit(solution)/shard_map/ppermute | solution.py:257
  88.6 9.6 %collective-permute-start.21 = (bf16[2,128,384]{2,1,0:T(8,128)(2,1)S(1)}, bf16[2,128,384]{2,1,0:T(8,128)(2,1)S(1)}, u32[]{:S(2)}, u32[]{:S(2)}) collective-permute-start(bf16[2,128,384]{2,1,0:T(8,128)(2,1)S(1)} %get-tuple-element.78), channel_id=1, source_target_pairs={{0,6},{2,4},{4,2},{6,0},{1,7},{3,5},{5,3},{7,1},{8,14},{10,12},{12... | collective-permute-start | bytes 589832 | tf_op jit(solution)/shard_map/ppermute | solution.py:257
  93.7 6.7 %collective-permute-start.14 = (f32[128]{0:T(128)S(1)}, f32[128]{0:T(128)S(1)}, u32[]{:S(2)}, u32[]{:S(2)}) collective-permute-start(f32[128]{0:T(128)S(1)} %slice_reduce_fusion.1), channel_id=1, source_target_pairs={{0,1},{1,0},{2,3},{3,2},{4,5},{5,4},{6,7},{7,6},{8,9},{9,8},{10,11... | collective-permute-start | bytes 1544 | tf_op jit(solution)/shard_map/ppermute | solution.py:269
  98.8 6.3 %collective-permute-start.23 = (bf16[2,128,256]{2,1,0:T(8,128)(2,1)S(1)}, bf16[2,128,256]{2,1,0:T(8,128)(2,1)S(1)}, u32[]{:S(2)}, u32[]{:S(2)}) collective-permute-start(bf16[2,128,256]{2,1,0:T(8,128)(2,1)S(1)} %get-tuple-element.83), channel_id=1, source_target_pairs={{0,4},{2,6},{4,0},{6,2},{1,5},{3,7},{5,1},{7,3},{8,12},{10,14},{12... | collective-permute-start | bytes 393224 | tf_op jit(solution)/shard_map/ppermute | solution.py:257
  99.7 6.8 %collective-permute-start.24 = (bf16[2,128,256]{2,1,0:T(8,128)(2,1)S(1)}, bf16[2,128,256]{2,1,0:T(8,128)(2,1)S(1)}, u32[]{:S(2)}, u32[]{:S(2)}) collective-permute-start(bf16[2,128,256]{2,1,0:T(8,128)(2,1)S(1)} %get-tuple-element.82), channel_id=1, source_target_pairs={{0,6},{2,4},{4,2},{6,0},{1,7},{3,5},{5,3},{7,1},{8,14},{10,12},{12... | collective-permute-start | bytes 393224 | tf_op jit(solution)/shard_map/ppermute | solution.py:257
  108.0 3.6 %collective-permute-start.25 = (f32[128]{0:T(128)S(1)}, f32[128]{0:T(128)S(1)}, u32[]{:S(2)}, u32[]{:S(2)}) collective-permute-start(f32[128]{0:T(128)S(1)} %slice_reduce_fusion), channel_id=1, source_target_pairs={{0,1},{1,0},{2,3},{3,2},{4,5},{5,4},{6,7},{7,6},{8,9},{9,8},{10,11... | collective-permute-start | bytes 1544 | tf_op jit(solution)/shard_map/ppermute | solution.py:269
  (10 other events, 49.5 us)

commit v4 on v2

--- a/solution.py
+++ b/solution.py
@@ -39,7 +39,6 @@
         self.home = self.distances.index(0)
         self.heads = heads_here // self.group
         self.chunks = chunks_of(self.heads)
-        self.pack = min(self.group, 2)
         if self.group > 1:
             self.slots = [[self.group + s - o for o in self.offsets] for s in range(self.group)]
         else:
@@ -47,7 +46,8 @@
 
 
 def chunks_of(heads):
-    return [(0, heads)]
+    first = (heads + 1) // 2
+    return [(0, first), (first, heads - first)] if heads > 1 else [(0, heads)]
 
 
 def busy(us):
@@ -61,13 +61,8 @@
 def attend(place, *refs, plan, first, heads):
     group, nd, noff = plan.group, len(plan.distances), len(plan.offsets)
     it = iter(refs)
-    packs = group // plan.pack
-
-    def unpacked():
-        return [ref.at[i] for ref in [next(it) for _ in range(packs)] for i in range(plan.pack)]
-
     qd = [next(it) for _ in range(group)]
-    kv = [unpacked() for _ in range(nd)]
+    kv = [[ref.at[m] for m in range(group)] for ref in [next(it) for _ in range(nd)]]
     out_oq = [next(it) for _ in range(group)]
     out_kv = [next(it) for _ in range(nd)]
     keys, vals, queries, grads, weights, scored, outs, dqs, allow = (next(it) for _ in range(9))
@@ -79,8 +74,8 @@
         return pl.ds(pl.multiple_of(slot * HEAD, HEAD), HEAD)
 
     def one_head(h, _):
-        source = pl.ds(pl.multiple_of((first + h) * HEAD, HEAD), HEAD)
-        target = pl.ds(pl.multiple_of(h * HEAD, HEAD), HEAD)
+        source = pl.ds(pl.multiple_of(h * HEAD, HEAD), HEAD)
+        target = source
         for m in range(group):
             at = rows(m ^ r)
             queries[at, :] = qd[m][0:HEAD, source]
@@ -146,11 +141,8 @@
     width = heads * HEAD
     group, nd, noff = plan.group, len(plan.distances), len(plan.offsets)
     ng = nd * group
-    packs = group // plan.pack
-    query = pl.BlockSpec((2 * HEAD + TAIL, HEAD), lambda h, _: (0, h + first))
-    keyed = pl.BlockSpec((plan.pack, 2, HEAD, HEAD), lambda h, _: (0, 0, 0, h + first))
-    packs = group // plan.pack
     whole = pl.BlockSpec(memory_space=pltpu.VMEM)
+    args = [place, *qd, *kv]
     outs = [jax.ShapeDtypeStruct((2, HEAD, width), bf16)] * group + [
         jax.ShapeDtypeStruct((group, 2, HEAD, width), f32 if by == 0 else bf16)
         for by in plan.distances
@@ -160,7 +152,7 @@
         grid_spec=pltpu.PrefetchScalarGridSpec(
             num_scalar_prefetch=1,
             grid=(),
-            in_specs=[whole] * (group + nd * packs),
+            in_specs=[whole] * (len(args) - 1),
             out_specs=[whole] * (group + nd),
             scratch_shapes=[pltpu.VMEM((ng * HEAD, HEAD), bf16)] * 2
             + [pltpu.VMEM((group * HEAD, HEAD), bf16)] * 2
@@ -172,7 +164,7 @@
         compiler_params=pltpu.CompilerParams(vmem_limit_bytes=36 * 2**20),
         cost_estimate=busy(4 * heads),
         name="attend",
-    )(place, *qd, *[pack for block in kv for pack in block])
+    )(*args)
     return result[:group], result[group:]
 
 
@@ -276,7 +268,6 @@
         return (x.astype(f32) * rstd[:, None] * gain).astype(bf16)
 
     key_norm = normed(key_vectors, my_rstd[0], key_gain)
-    kv = [jnp.stack([chunk(key_norm, m), chunk(value_vectors, m)]) for m in range(group)]
     query_norm = normed(query_vectors, my_rstd[1], query_gain)
     live = jnp.arange(block_pairs.shape[1], dtype=jnp.int32) < pair_counts[0]
     steps = block_pairs[0, :, 0] - block_pairs[0, :, 1]
@@ -284,35 +275,69 @@
     flags = jnp.any(live[:, None] & (steps[:, None] == wanted[None, :]), axis=0)
     bias = jnp.pad(jnp.where(flags, 0.0, lowest), (0, TAIL - len(offsets)))
     allow = jnp.broadcast_to(bias[:, None], (TAIL, width)).astype(bf16)
-    qd = [
-        jnp.concatenate([chunk(query_norm, m), chunk(output_grad, m), allow]) for m in range(group)
+
+    def cut(x, m, first, count):
+        return lax.dynamic_slice_in_dim(x, (r ^ m) * width + first * HEAD, count * HEAD, axis=1)
+
+    kv_cut = [
+        [jnp.stack([cut(key_norm, m, *c), cut(value_vectors, m, *c)]) for m in range(group)]
+        for c in plan.chunks
     ]
-
-    kv = [swap(x, m) for m, x in enumerate(kv)]
-    near = jnp.stack(kv[: plan.pack])
-    near = [moved(near, -by) for by in distances]
-    kv, qd = lax.optimization_barrier((kv, qd))
-    qd = [swap(x, m) for m, x in enumerate(qd)]
-    packs = [jnp.stack(kv[i : i + plan.pack]) for i in range(plan.pack, group, plan.pack)]
-    packs, near, qd[group // 2 % group] = lax.optimization_barrier((packs, near, qd[group // 2 % group]))
-    kv = [[x] + [moved(y, -by) for y in packs] for x, by in zip(near, distances)]
-
-    oq_back, kv_back = [], []
-    for first, count in plan.chunks:
-        oq_parts, kv_parts = attention(place, qd, kv, plan, first, count)
-        oq_back.append([swap(x, m) for m, x in enumerate(oq_parts)])
-        back = [moved(kv_parts[d], by) for d, by in enumerate(distances) if by]
+    qd_cut = [
+        [
+            jnp.concatenate(
+                [cut(query_norm, m, *c), cut(output_grad, m, *c), allow[:, : c[1] * HEAD]]
+            )
+            for m in range(group)
+        ]
+        for c in plan.chunks
+    ]
+
+    def after(x, *earlier):
+        return lax.optimization_barrier((x, earlier))[0]
+
+    def swaps(xs):
+        return [swap(x, m) for m, x in enumerate(xs)]
+
+    half, last = group // 2, group - 1
+    kv, qd = [], []
+    arrived = None
+    for c in range(len(plan.chunks)):
+        mine = kv_cut[c] if arrived is None else after(kv_cut[c], arrived[half])
+        arrived = swaps(mine)
+        kv.append(arrived)
+    for c in range(len(plan.chunks)):
+        arrived = swaps(after(qd_cut[c], arrived[half]))
+        qd.append(arrived)
+    halo = []
+    for c in range(len(plan.chunks)):
+        pack = jnp.stack(kv[c])
+        if halo:
+            pack = after(pack, qd[0][last])
+        halo.append([moved(pack, -by) for by in distances])
+    kv = halo
+
+    back = []
+    oq_back = []
+    for c, (first, count) in enumerate(plan.chunks):
+        oq, kv_parts = attention(place, qd[c], kv[c], plan, first, count)
+        sent = [moved(kv_parts[d], by) for d, by in enumerate(distances) if by]
+        back.append((kv_parts[plan.home], sent))
+        oq_back.append([swap(x, m) for m, x in enumerate(oq)])
+    attended, query_norm_grad, query_inner = joined(
+        place, oq_back, query_vectors, my_rstd[1:2], query_gain, plan
+    )
+    kv_back = []
+    for own, sent in back:
+        if kv_back:
+            sent, kv_back[-1] = lax.optimization_barrier((sent, kv_back[-1]))
         total = []
         for m in range(group):
-            x = kv_parts[plan.home][m]
-            for y in back:
+            x = own[m]
+            for y in sent:
                 x = x + y[m].astype(f32)
             total.append(swap(x.astype(bf16), m))
         kv_back.append(total)
-
-    attended, query_norm_grad, query_inner = joined(
-        place, oq_back, query_vectors, my_rstd[1:2], query_gain, plan
-    )
     value_grad, key_norm_grad, key_inner = joined(
         place, kv_back, key_vectors, my_rstd[0:1], key_gain, plan
     )

time: 123 us -> 109 us (0.89)
  waiting for transfers between devices: 69.6 us -> 39.7 us
  starting transfers between devices: 30.5 us -> 45.4 us
    ppermute x12 -> x24, waiting for transfers between devices: 53.7 us -> 32.2 us  [swap(): lax.ppermute(x, 'place', [(i, i ^ m) for i in range(group)])]
    ppermute x12 -> x24, starting transfers between devices: 7.59 us -> 16.2 us  [swap(): lax.ppermute(x, 'place', [(i, i ^ m) for i in range(group)])]
    ppermute x6 -> x8, starting transfers between devices: 17.6 us -> 23 us  [moved(): lax.ppermute(x, 'block', [(i, i + by) for i in range(blocks) if 0 <= i +...]
    ppermute x6 -> x8, waiting for transfers between devices: 11.6 us -> 6.2 us  [moved(): lax.ppermute(x, 'block', [(i, i + by) for i in range(blocks) if 0 <= i +...]
    ppermute x3, waiting for transfers between devices: 4.29 us -> 1.33 us  [summed(): x = x + lax.ppermute(x, 'head', [(i, i ^ step) for i in range(count)])]
    pallas_call x1 -> x2, Pallas kernels: 10.9 us -> 10.9 us  [attention(): pl.pallas_call(functools.partial(attend, plan=plan, first=first, heads=he...]
  transfers between devices with their start and end apart: 21 -> 35, of which waited for: 17 -> 17; matrix products, arithmetic and copies ran while one was open for 2% -> 3% of each run, Pallas kernels for 1% -> 11%
where the time goes in v4:
time: 109 us
  starting transfers between devices  45.4 us (42%)
  waiting for transfers between devices  39.7 us (36%)
  Pallas kernels  13.6 us (12%)
  other arithmetic  7.09 us (7%)
  between operations  1.8 us (2%)
  local copies, waits for them, and re-layouts  1.13 us (1%)
    ppermute x24, waiting for transfers between devices, swap(): lax.ppermute(x, 'place', [(i, i ^ m) for i in range(group)])  32.2 us
    ppermute x8, starting transfers between devices, moved(): lax.ppermute(x, 'block', [(i, i + by) for i in range(blocks) if 0 <= i +...  23 us
    ppermute x24, starting transfers between devices, swap(): lax.ppermute(x, 'place', [(i, i ^ m) for i in range(group)])  16.2 us
    pallas_call x2, Pallas kernels, attention(): pl.pallas_call(functools.partial(attend, plan=plan, first=first, heads=he...  10.9 us
    ppermute x8, waiting for transfers between devices, moved(): lax.ppermute(x, 'block', [(i, i + by) for i in range(blocks) if 0 <= i +...  6.2 us
    ppermute x3, starting transfers between devices, summed(): x = x + lax.ppermute(x, 'head', [(i, i ^ step) for i in range(count)])  6.13 us
    reduce_sum x2, other arithmetic, local(): jnp.sum(jnp.square(x.astype(f32)), axis=1)  2.7 us
    pallas_call x2, Pallas kernels, joined(): pl.pallas_call(functools.partial(join, plan=plan), grid_spec=pltpu.Prefet...  2.65 us
  transfers between devices with their start and end apart: 35, of which 17 were waited for; matrix products, arithmetic and copies ran while one was open for 3% of the time, Pallas kernels for 11%

profile of v4, /device:TPU:0, one launch (start us, length us, event | category | flops | bytes accessed | tf_op | source)
XLA Modules:
  0.0 108.7 jit_solution(2489658633630990774)
XLA Ops:
  0.7 1.4 %fusion.13 = f32[128]{0:T(128)S(1)} fusion(bf16[128,2560]{1,0:T(8,128)(2,1)} %refs_8_.3), kind=kLoop, calls=%fused_computation.17 | loop fusion | flops 982912 | bytes 655872 | tf_op jit(solution)/shard_map/reduce_sum | solution.py:263
  2.1 1.3 %fusion.12 = f32[128]{0:T(128)S(1)} fusion(bf16[128,2560]{1,0:T(8,128)(2,1)} %refs_8_.2), kind=kLoop, calls=%fused_computation.16 | loop fusion | flops 982912 | bytes 655872 | tf_op jit(solution)/shard_map/reduce_sum | solution.py:263
  3.4 3.0 %collective-permute-start = (f32[2,128]{1,0:T(2,128)S(1)}, f32[2,128]{1,0:T(2,128)S(1)}, u32[]{:S(2)}, u32[]{:S(2)}) collective-permute-start(f32[2,128]{1,0:T(2,128)S(1)} %pad_maximum_fusion.9), channel_id=1, source_target_pairs={{0,1},{1,0},{2,3},{3,2},{4,5},{5,4},{6,7},{7,6},{8,9},{9,8},{10,11... | collective-permute-start | bytes 3080 | tf_op jit(solution)/shard_map/ppermute | solution.py:252
  8.4 2.1 %collective-permute-start.1 = (bf16[2,128,384]{2,1,0:T(8,128)(2,1)S(1)}, bf16[2,128,384]{2,1,0:T(8,128)(2,1)S(1)}, u32[]{:S(2)}, u32[]{:S(2)}) collective-permute-start(bf16[2,128,384]{2,1,0:T(8,128)(2,1)S(1)} %pad_maximum_fusion.2), channel_id=1, source_target_pairs={{0,4},{2,6},{4,0},{6,2},{1,5},{3,7},{5,1},{7,3},{8,12},{10,14},{12... | collective-permute-start | bytes 589832 | tf_op jit(solution)/shard_map/ppermute | solution.py:240
  11.8 4.0 %collective-permute-done.1 = bf16[2,128,384]{2,1,0:T(8,128)(2,1)S(1)} collective-permute-done((bf16[2,128,384]{2,1,0:T(8,128)(2,1)S(1)}, bf16[2,128,384]{2,1,0:T(8,128)(2,1)S(1)}, u32[]{:S(2)}, u32[]{:S(2)}) %collective-permute-start.1) | collective-permute-done | bytes 196640 | tf_op jit(solution)/shard_map/ppermute | solution.py:240
  15.8 2.2 %collective-permute-done.7 = bf16[2,128,384]{2,1,0:T(8,128)(2,1)S(1)} collective-permute-done((bf16[2,128,384]{2,1,0:T(8,128)(2,1)S(1)}, bf16[2,128,384]{2,1,0:T(8,128)(2,1)S(1)}, u32[]{:S(2)}, u32[]{:S(2)}) %collective-permute-start.7) | collective-permute-done | bytes 196640 | tf_op jit(solution)/shard_map/ppermute | solution.py:240
  18.1 3.5 %collective-permute-start.8 = (bf16[4,2,128,384]{3,2,1,0:T(8,128)(2,1)S(1)}, bf16[4,2,128,384]{3,2,1,0:T(8,128)(2,1)S(1)}, u32[]{:S(2)}, u32[]{:S(2)}) collective-permute-start(bf16[4,2,128,384]{3,2,1,0:T(8,128)(2,1)S(1)} %pad_maximum_fusion.refs_5_), channel_id=1, source_target_pairs={{0,8},{8,16},{16,24},{1,9},{9,17},{17,25},{2,10},{10,18},{18,26},{... | collective-permute-start | bytes 2359304 | tf_op jit(solution)/shard_map/ppermute | solution.py:245
  25.4 3.9 %collective-permute-done.2 = bf16[2,128,256]{2,1,0:T(8,128)(2,1)S(1)} collective-permute-done((bf16[2,128,256]{2,1,0:T(8,128)(2,1)S(1)}, bf16[2,128,256]{2,1,0:T(8,128)(2,1)S(1)}, u32[]{:S(2)}, u32[]{:S(2)}) %collective-permute-start.2) | collective-permute-done | bytes 131104 | tf_op jit(solution)/shard_map/ppermute | solution.py:240
  32.2 8.7 %collective-permute-done.5.refs_3_ = bf16[272,384]{1,0:T(8,128)(2,1)S(1)} collective-permute-done((bf16[272,384]{1,0:T(8,128)(2,1)S(1)}, bf16[272,384]{1,0:T(8,128)(2,1)S(1)}, u32[]{:S(2)}, u32[]{:S(2)}) %collective-permute-start.5) | collective-permute-done | bytes 208928 | tf_op jit(solution)/shard_map/ppermute | solution.py:240
  41.0 4.6 %collective-permute-start.18 = (bf16[4,2,128,256]{3,2,1,0:T(8,128)(2,1)S(1)}, bf16[4,2,128,256]{3,2,1,0:T(8,128)(2,1)S(1)}, u32[]{:S(2)}, u32[]{:S(2)}) collective-permute-start(bf16[4,2,128,256]{3,2,1,0:T(8,128)(2,1)S(1)} %pad_maximum_fusion.1.refs_5_), channel_id=1, source_target_pairs={{0,8},{8,16},{16,24},{1,9},{9,17},{17,25},{2,10},{10,18},{18,26},{... | collective-permute-start | bytes 1572872 | tf_op jit(solution)/shard_map/ppermute | solution.py:245
  48.8 6.6 %attend.2 = (bf16[2,128,384]{2,1,0:T(8,128)(2,1)S(1)}, bf16[2,128,384]{2,1,0:T(8,128)(2,1)S(1)}, bf16[2,128,384]{2,1,0:T(8,128)(2,1)S(1)}, bf16[2,128,384]{2,1,0...) custom-call(s32[1]{0:T(128)} %bitcast.place, ...), custom_call_target="tpu_custom_call" | custom-call | flops 13200000000 | bytes 42000000 | tf_op jit(solution)/shard_map/attend/pallas_call | solution.py:150
  56.7 5.2 %collective-permute-start.27 = (bf16[4,2,128,384]{3,2,1,0:T(8,128)(2,1)S(1)}, bf16[4,2,128,384]{3,2,1,0:T(8,128)(2,1)S(1)}, u32[]{:S(2)}, u32[]{:S(2)}) collective-permute-start(bf16[4,2,128,384]{3,2,1,0:T(8,128)(2,1)S(1)} %get-tuple-element.71), channel_id=1, source_target_pairs={{0,8},{8,16},{16,24},{1,9},{9,17},{17,25},{2,10},{10,18},{18,26},{... | collective-permute-start | bytes 2359304 | tf_op jit(solution)/shard_map/ppermute | solution.py:245
  62.5 1.5 %collective-permute-start.12 = (bf16[2,128,384]{2,1,0:T(8,128)(2,1)S(1)}, bf16[2,128,384]{2,1,0:T(8,128)(2,1)S(1)}, u32[]{:S(2)}, u32[]{:S(2)}) collective-permute-start(bf16[2,128,384]{2,1,0:T(8,128)(2,1)S(1)} %get-tuple-element.51), channel_id=1, source_target_pairs={{0,6},{2,4},{4,2},{6,0},{1,7},{3,5},{5,3},{7,1},{8,14},{10,12},{12... | collective-permute-start | bytes 589832 | tf_op jit(solution)/shard_map/ppermute | solution.py:240
  63.9 4.4 %attend.3 = (bf16[2,128,256]{2,1,0:T(8,128)(2,1)S(1)}, bf16[2,128,256]{2,1,0:T(8,128)(2,1)S(1)}, bf16[2,128,256]{2,1,0:T(8,128)(2,1)S(1)}, bf16[2,128,256]{2,1,0...) custom-call(s32[1]{0:T(128)} %bitcast.place, ...), custom_call_target="tpu_custom_call" | custom-call | flops 8800000000 | bytes 28000000 | tf_op jit(solution)/shard_map/attend/pallas_call | solution.py:150
  69.8 4.5 %collective-permute-start.25 = (bf16[4,2,128,256]{3,2,1,0:T(8,128)(2,1)S(1)}, bf16[4,2,128,256]{3,2,1,0:T(8,128)(2,1)S(1)}, u32[]{:S(2)}, u32[]{:S(2)}) collective-permute-start(bf16[4,2,128,256]{3,2,1,0:T(8,128)(2,1)S(1)} %get-tuple-element.68), channel_id=1, source_target_pairs={{0,8},{8,16},{16,24},{1,9},{9,17},{17,25},{2,10},{10,18},{18,26},{... | collective-permute-start | bytes 1572872 | tf_op jit(solution)/shard_map/ppermute | solution.py:245
  74.5 4.2 %collective-permute-done.26 = bf16[4,2,128,384]{3,2,1,0:T(8,128)(2,1)S(1)} collective-permute-done((bf16[4,2,128,384]{3,2,1,0:T(8,128)(2,1)S(1)}, bf16[4,2,128,384]{3,2,1,0:T(8,128)(2,1)S(1)}, u32[]{:S(2)}, u32[]{:S(2)}) %collective-permute-start.26) | collective-permute-done | bytes 786464 | tf_op jit(solution)/shard_map/ppermute | solution.py:245
  81.2 3.3 %collective-permute-done.21.refs_6_ = bf16[2,128,256]{2,1,0:T(8,128)(2,1)S(1)} collective-permute-done((bf16[2,128,256]{2,1,0:T(8,128)(2,1)S(1)}, bf16[2,128,256]{2,1,0:T(8,128)(2,1)S(1)}, u32[]{:S(2)}, u32[]{:S(2)}) %collective-permute-start.21) | collective-permute-done | bytes 131104 | tf_op jit(solution)/shard_map/ppermute | solution.py:240
  85.5 1.4 %collective-permute-start.30 = (bf16[2,128,384]{2,1,0:T(8,128)(2,1)S(1)}, bf16[2,128,384]{2,1,0:T(8,128)(2,1)S(1)}, u32[]{:S(2)}, u32[]{:S(2)}) collective-permute-start(bf16[2,128,384]{2,1,0:T(8,128)(2,1)S(1)} %get-tuple-element.82), channel_id=1, source_target_pairs={{0,6},{2,4},{4,2},{6,0},{1,7},{3,5},{5,3},{7,1},{8,14},{10,12},{12... | collective-permute-start | bytes 589832 | tf_op jit(solution)/shard_map/ppermute | solution.py:240
  86.9 1.3 %join.2 = (bf16[128,2560]{1,0:T(8,128)(2,1)}, bf16[128,2560]{1,0:T(8,128)(2,1)S(1)}, f32[128,128]{1,0:T(8,128)S(1)}) custom-call(s32[1]{0:T(128)} %bitcast.place, bf16[2,128,384]{2,1,0:T(8,128)(2,1)S(1)} %get-tuple-element.48.refs_0_, bf16[2,128,384]{2,1,0:T(8,128)(2,1)S(1)} %collective-permute-done.10.refs_1_, ...), custom_call_target="tpu_custom_call" | custom-call | flops 2200000000 | bytes 7000000 | tf_op jit(solution)/shard_map/join/pallas_call | solution.py:200
  89.6 1.5 %collective-permute-start.23 = (f32[128]{0:T(128)S(1)}, f32[128]{0:T(128)S(1)}, u32[]{:S(2)}, u32[]{:S(2)}) collective-permute-start(f32[128]{0:T(128)S(1)} %slice_reduce_fusion.1), channel_id=1, source_target_pairs={{0,1},{1,0},{2,3},{3,2},{4,5},{5,4},{6,7},{7,6},{8,9},{9,8},{10,11... | collective-permute-start | bytes 1544 | tf_op jit(solution)/shard_map/ppermute | solution.py:252
  93.3 1.6 %collective-permute-start.31 = (bf16[2,128,256]{2,1,0:T(8,128)(2,1)S(1)}, bf16[2,128,256]{2,1,0:T(8,128)(2,1)S(1)}, u32[]{:S(2)}, u32[]{:S(2)}) collective-permute-start(bf16[2,128,256]{2,1,0:T(8,128)(2,1)S(1)} %get-tuple-element.88), channel_id=1, source_target_pairs={{0,2},{2,0},{4,6},{6,4},{1,3},{3,1},{5,7},{7,5},{8,10},{10,8},{12,... | collective-permute-start | bytes 393224 | tf_op jit(solution)/shard_map/ppermute | solution.py:240
  96.4 4.9 %collective-permute-done.32.refs_6_ = bf16[2,128,256]{2,1,0:T(8,128)(2,1)S(1)} collective-permute-done((bf16[2,128,256]{2,1,0:T(8,128)(2,1)S(1)}, bf16[2,128,256]{2,1,0:T(8,128)(2,1)S(1)}, u32[]{:S(2)}, u32[]{:S(2)}) %collective-permute-start.32) | collective-permute-done | bytes 131104 | tf_op jit(solution)/shard_map/ppermute | solution.py:240
  102.4 1.3 %join.3 = (bf16[128,2560]{1,0:T(8,128)(2,1)}, bf16[128,2560]{1,0:T(8,128)(2,1)S(1)}, f32[128,128]{1,0:T(8,128)S(1)}) custom-call(s32[1]{0:T(128)} %bitcast.place, bf16[2,128,384]{2,1,0:T(8,128)(2,1)S(1)} %get-tuple-element.72.refs_0_, bf16[2,128,384]{2,1,0:T(8,128)(2,1)S(1)} %collective-permute-done.28.refs_1_, ...), custom_call_target="tpu_custom_call" | custom-call | flops 2200000000 | bytes 7000000 | tf_op jit(solution)/shard_map/join/pallas_call | solution.py:200
  103.8 1.6 %collective-permute-start.34 = (f32[128]{0:T(128)S(1)}, f32[128]{0:T(128)S(1)}, u32[]{:S(2)}, u32[]{:S(2)}) collective-permute-start(f32[128]{0:T(128)S(1)} %slice_reduce_fusion), channel_id=1, source_target_pairs={{0,1},{1,0},{2,3},{3,2},{4,5},{5,4},{6,7},{7,6},{8,9},{9,8},{10,11... | collective-permute-start | bytes 1544 | tf_op jit(solution)/shard_map/ppermute | solution.py:252
  (104 shorter events, 28.9 us)
Async XLA Ops:
  8.4 7.3 %collective-permute-start.1 = (bf16[2,128,384]{2,1,0:T(8,128)(2,1)S(1)}, bf16[2,128,384]{2,1,0:T(8,128)(2,1)S(1)}, u32[]{:S(2)}, u32[]{:S(2)}) collective-permute-start(bf16[2,128,384]{2,1,0:T(8,128)(2,1)S(1)} %pad_maximum_fusion.2), channel_id=1, source_target_pairs={{0,4},{2,6},{4,0},{6,2},{1,5},{3,7},{5,1},{7,3},{8,12},{10,14},{12... | collective-permute-start | bytes 589832 | tf_op jit(solution)/shard_map/ppermute | solution.py:240
  10.6 7.3 %collective-permute-start.7 = (bf16[2,128,384]{2,1,0:T(8,128)(2,1)S(1)}, bf16[2,128,384]{2,1,0:T(8,128)(2,1)S(1)}, u32[]{:S(2)}, u32[]{:S(2)}) collective-permute-start(bf16[2,128,384]{2,1,0:T(8,128)(2,1)S(1)} %pad_maximum_fusion.4), channel_id=1, source_target_pairs={{0,6},{2,4},{4,2},{6,0},{1,7},{3,5},{5,3},{7,1},{8,14},{10,12},{12... | collective-permute-start | bytes 589832 | tf_op jit(solution)/shard_map/ppermute | solution.py:240
  18.1 29.1 %collective-permute-start.8 = (bf16[4,2,128,384]{3,2,1,0:T(8,128)(2,1)S(1)}, bf16[4,2,128,384]{3,2,1,0:T(8,128)(2,1)S(1)}, u32[]{:S(2)}, u32[]{:S(2)}) collective-permute-start(bf16[4,2,128,384]{3,2,1,0:T(8,128)(2,1)S(1)} %pad_maximum_fusion.refs_5_), channel_id=1, source_target_pairs={{0,8},{8,16},{16,24},{1,9},{9,17},{17,25},{2,10},{10,18},{18,26},{... | collective-permute-start | bytes 2359304 | tf_op jit(solution)/shard_map/ppermute | solution.py:245
  21.6 26.0 %collective-permute-start.9 = (bf16[4,2,128,384]{3,2,1,0:T(8,128)(2,1)S(1)}, bf16[4,2,128,384]{3,2,1,0:T(8,128)(2,1)S(1)}, u32[]{:S(2)}, u32[]{:S(2)}) collective-permute-start(bf16[4,2,128,384]{3,2,1,0:T(8,128)(2,1)S(1)} %pad_maximum_fusion.refs_5_), channel_id=1, source_target_pairs={{8,0},{16,8},{24,16},{9,1},{17,9},{25,17},{10,2},{18,10},{26,18},{... | collective-permute-start | bytes 2359304 | tf_op jit(solution)/shard_map/ppermute | solution.py:245
  24.7 6.6 %collective-permute-start.17 = (bf16[2,128,256]{2,1,0:T(8,128)(2,1)S(1)}, bf16[2,128,256]{2,1,0:T(8,128)(2,1)S(1)}, u32[]{:S(2)}, u32[]{:S(2)}) collective-permute-start(bf16[2,128,256]{2,1,0:T(8,128)(2,1)S(1)} %get-tuple-element.58), channel_id=1, source_target_pairs={{0,6},{2,4},{4,2},{6,0},{1,7},{3,5},{5,3},{7,1},{8,14},{10,12},{12... | collective-permute-start | bytes 393224 | tf_op jit(solution)/shard_map/ppermute | solution.py:240
  29.3 17.6 %collective-permute-start.3 = (bf16[272,384]{1,0:T(8,128)(2,1)S(1)}, bf16[272,384]{1,0:T(8,128)(2,1)S(1)}, u32[]{:S(2)}, u32[]{:S(2)}) collective-permute-start(bf16[272,384]{1,0:T(8,128)(2,1)S(1)} %get-tuple-element.45), channel_id=1, source_target_pairs={{0,2},{2,0},{4,6},{6,4},{1,3},{3,1},{5,7},{7,5},{8,10},{10,8},{12,... | collective-permute-start | bytes 626696 | tf_op jit(solution)/shard_map/ppermute | solution.py:240
  29.3 16.3 %collective-permute-start.4 = (bf16[272,384]{1,0:T(8,128)(2,1)S(1)}, bf16[272,384]{1,0:T(8,128)(2,1)S(1)}, u32[]{:S(2)}, u32[]{:S(2)}) collective-permute-start(bf16[272,384]{1,0:T(8,128)(2,1)S(1)} %get-tuple-element.46), channel_id=1, source_target_pairs={{0,4},{2,6},{4,0},{6,2},{1,5},{3,7},{5,1},{7,3},{8,12},{10,14},{12... | collective-permute-start | bytes 626696 | tf_op jit(solution)/shard_map/ppermute | solution.py:240
  31.3 9.7 %collective-permute-start.5 = (bf16[272,384]{1,0:T(8,128)(2,1)S(1)}, bf16[272,384]{1,0:T(8,128)(2,1)S(1)}, u32[]{:S(2)}, u32[]{:S(2)}) collective-permute-start(bf16[272,384]{1,0:T(8,128)(2,1)S(1)} %get-tuple-element.47), channel_id=1, source_target_pairs={{0,6},{2,4},{4,2},{6,0},{1,7},{3,5},{5,3},{7,1},{8,14},{10,12},{12... | collective-permute-start | bytes 626696 | tf_op jit(solution)/shard_map/ppermute | solution.py:240
  41.0 21.2 %collective-permute-start.18 = (bf16[4,2,128,256]{3,2,1,0:T(8,128)(2,1)S(1)}, bf16[4,2,128,256]{3,2,1,0:T(8,128)(2,1)S(1)}, u32[]{:S(2)}, u32[]{:S(2)}) collective-permute-start(bf16[4,2,128,256]{3,2,1,0:T(8,128)(2,1)S(1)} %pad_maximum_fusion.1.refs_5_), channel_id=1, source_target_pairs={{0,8},{8,16},{16,24},{1,9},{9,17},{17,25},{2,10},{10,18},{18,26},{... | collective-permute-start | bytes 1572872 | tf_op jit(solution)/shard_map/ppermute | solution.py:245
  45.6 16.9 %collective-permute-start.19 = (bf16[4,2,128,256]{3,2,1,0:T(8,128)(2,1)S(1)}, bf16[4,2,128,256]{3,2,1,0:T(8,128)(2,1)S(1)}, u32[]{:S(2)}, u32[]{:S(2)}) collective-permute-start(bf16[4,2,128,256]{3,2,1,0:T(8,128)(2,1)S(1)} %pad_maximum_fusion.1.refs_5_), channel_id=1, source_target_pairs={{8,0},{16,8},{24,16},{9,1},{17,9},{25,17},{10,2},{18,10},{26,18},{... | collective-permute-start | bytes 1572872 | tf_op jit(solution)/shard_map/ppermute | solution.py:245
  46.9 8.5 %collective-permute-start.13 = (bf16[272,256]{1,0:T(8,128)(2,1)S(1)}, bf16[272,256]{1,0:T(8,128)(2,1)S(1)}, u32[]{:S(2)}, u32[]{:S(2)}) collective-permute-start(bf16[272,256]{1,0:T(8,128)(2,1)S(1)} %get-tuple-element.53), channel_id=1, source_target_pairs={{0,2},{2,0},{4,6},{6,4},{1,3},{3,1},{5,7},{7,5},{8,10},{10,8},{12,... | collective-permute-start | bytes 417800 | tf_op jit(solution)/shard_map/ppermute | solution.py:240
  47.2 9.5 %collective-permute-start.14 = (bf16[272,256]{1,0:T(8,128)(2,1)S(1)}, bf16[272,256]{1,0:T(8,128)(2,1)S(1)}, u32[]{:S(2)}, u32[]{:S(2)}) collective-permute-start(bf16[272,256]{1,0:T(8,128)(2,1)S(1)} %get-tuple-element.54), channel_id=1, source_target_pairs={{0,4},{2,6},{4,0},{6,2},{1,5},{3,7},{5,1},{7,3},{8,12},{10,14},{12... | collective-permute-start | bytes 417800 | tf_op jit(solution)/shard_map/ppermute | solution.py:240
  47.6 14.4 %collective-permute-start.15 = (bf16[272,256]{1,0:T(8,128)(2,1)S(1)}, bf16[272,256]{1,0:T(8,128)(2,1)S(1)}, u32[]{:S(2)}, u32[]{:S(2)}) collective-permute-start(bf16[272,256]{1,0:T(8,128)(2,1)S(1)} %get-tuple-element.55), channel_id=1, source_target_pairs={{0,6},{2,4},{4,2},{6,0},{1,7},{3,5},{5,3},{7,1},{8,14},{10,12},{12... | collective-permute-start | bytes 417800 | tf_op jit(solution)/shard_map/ppermute | solution.py:240
  55.4 23.2 %collective-permute-start.26 = (bf16[4,2,128,384]{3,2,1,0:T(8,128)(2,1)S(1)}, bf16[4,2,128,384]{3,2,1,0:T(8,128)(2,1)S(1)}, u32[]{:S(2)}, u32[]{:S(2)}) collective-permute-start(bf16[4,2,128,384]{3,2,1,0:T(8,128)(2,1)S(1)} %get-tuple-element.70), channel_id=1, source_target_pairs={{8,0},{16,8},{24,16},{9,1},{17,9},{25,17},{10,2},{18,10},{26,18},{... | collective-permute-start | bytes 2359304 | tf_op jit(solution)/shard_map/ppermute | solution.py:245
  56.7 23.1 %collective-permute-start.27 = (bf16[4,2,128,384]{3,2,1,0:T(8,128)(2,1)S(1)}, bf16[4,2,128,384]{3,2,1,0:T(8,128)(2,1)S(1)}, u32[]{:S(2)}, u32[]{:S(2)}) collective-permute-start(bf16[4,2,128,384]{3,2,1,0:T(8,128)(2,1)S(1)} %get-tuple-element.71), channel_id=1, source_target_pairs={{0,8},{8,16},{16,24},{1,9},{9,17},{17,25},{2,10},{10,18},{18,26},{... | collective-permute-start | bytes 2359304 | tf_op jit(solution)/shard_map/ppermute | solution.py:245
  62.1 7.7 %collective-permute-start.11 = (bf16[2,128,384]{2,1,0:T(8,128)(2,1)S(1)}, bf16[2,128,384]{2,1,0:T(8,128)(2,1)S(1)}, u32[]{:S(2)}, u32[]{:S(2)}) collective-permute-start(bf16[2,128,384]{2,1,0:T(8,128)(2,1)S(1)} %get-tuple-element.50), channel_id=1, source_target_pairs={{0,4},{2,6},{4,0},{6,2},{1,5},{3,7},{5,1},{7,3},{8,12},{10,14},{12... | collective-permute-start | bytes 589832 | tf_op jit(solution)/shard_map/ppermute | solution.py:240
  62.5 11.9 %collective-permute-start.12 = (bf16[2,128,384]{2,1,0:T(8,128)(2,1)S(1)}, bf16[2,128,384]{2,1,0:T(8,128)(2,1)S(1)}, u32[]{:S(2)}, u32[]{:S(2)}) collective-permute-start(bf16[2,128,384]{2,1,0:T(8,128)(2,1)S(1)} %get-tuple-element.51), channel_id=1, source_target_pairs={{0,6},{2,4},{4,2},{6,0},{1,7},{3,5},{5,3},{7,1},{8,14},{10,12},{12... | collective-permute-start | bytes 589832 | tf_op jit(solution)/shard_map/ppermute | solution.py:240
  68.3 21.3 %collective-permute-start.24 = (bf16[4,2,128,256]{3,2,1,0:T(8,128)(2,1)S(1)}, bf16[4,2,128,256]{3,2,1,0:T(8,128)(2,1)S(1)}, u32[]{:S(2)}, u32[]{:S(2)}) collective-permute-start(bf16[4,2,128,256]{3,2,1,0:T(8,128)(2,1)S(1)} %get-tuple-element.67), channel_id=1, source_target_pairs={{8,0},{16,8},{24,16},{9,1},{17,9},{25,17},{10,2},{18,10},{26,18},{... | collective-permute-start | bytes 1572872 | tf_op jit(solution)/shard_map/ppermute | solution.py:245
  69.8 21.3 %collective-permute-start.25 = (bf16[4,2,128,256]{3,2,1,0:T(8,128)(2,1)S(1)}, bf16[4,2,128,256]{3,2,1,0:T(8,128)(2,1)S(1)}, u32[]{:S(2)}, u32[]{:S(2)}) collective-permute-start(bf16[4,2,128,256]{3,2,1,0:T(8,128)(2,1)S(1)} %get-tuple-element.68), channel_id=1, source_target_pairs={{0,8},{8,16},{16,24},{1,9},{9,17},{17,25},{2,10},{10,18},{18,26},{... | collective-permute-start | bytes 1572872 | tf_op jit(solution)/shard_map/ppermute | solution.py:245
  80.2 11.0 %collective-permute-start.28 = (bf16[2,128,384]{2,1,0:T(8,128)(2,1)S(1)}, bf16[2,128,384]{2,1,0:T(8,128)(2,1)S(1)}, u32[]{:S(2)}, u32[]{:S(2)}) collective-permute-start(bf16[2,128,384]{2,1,0:T(8,128)(2,1)S(1)} %get-tuple-element.84), channel_id=1, source_target_pairs={{0,2},{2,0},{4,6},{6,4},{1,3},{3,1},{5,7},{7,5},{8,10},{10,8},{12,... | collective-permute-start | bytes 589832 | tf_op jit(solution)/shard_map/ppermute | solution.py:240
  84.5 7.8 %collective-permute-start.29 = (bf16[2,128,384]{2,1,0:T(8,128)(2,1)S(1)}, bf16[2,128,384]{2,1,0:T(8,128)(2,1)S(1)}, u32[]{:S(2)}, u32[]{:S(2)}) collective-permute-start(bf16[2,128,384]{2,1,0:T(8,128)(2,1)S(1)} %get-tuple-element.83), channel_id=1, source_target_pairs={{0,4},{2,6},{4,0},{6,2},{1,5},{3,7},{5,1},{7,3},{8,12},{10,14},{12... | collective-permute-start | bytes 589832 | tf_op jit(solution)/shard_map/ppermute | solution.py:240
  85.5 7.6 %collective-permute-start.30 = (bf16[2,128,384]{2,1,0:T(8,128)(2,1)S(1)}, bf16[2,128,384]{2,1,0:T(8,128)(2,1)S(1)}, u32[]{:S(2)}, u32[]{:S(2)}) collective-permute-start(bf16[2,128,384]{2,1,0:T(8,128)(2,1)S(1)} %get-tuple-element.82), channel_id=1, source_target_pairs={{0,6},{2,4},{4,2},{6,0},{1,7},{3,5},{5,3},{7,1},{8,14},{10,12},{12... | collective-permute-start | bytes 589832 | tf_op jit(solution)/shard_map/ppermute | solution.py:240
  89.6 6.8 %collective-permute-start.23 = (f32[128]{0:T(128)S(1)}, f32[128]{0:T(128)S(1)}, u32[]{:S(2)}, u32[]{:S(2)}) collective-permute-start(f32[128]{0:T(128)S(1)} %slice_reduce_fusion.1), channel_id=1, source_target_pairs={{0,1},{1,0},{2,3},{3,2},{4,5},{5,4},{6,7},{7,6},{8,9},{9,8},{10,11... | collective-permute-start | bytes 1544 | tf_op jit(solution)/shard_map/ppermute | solution.py:252
  95.4 7.0 %collective-permute-start.33 = (bf16[2,128,256]{2,1,0:T(8,128)(2,1)S(1)}, bf16[2,128,256]{2,1,0:T(8,128)(2,1)S(1)}, u32[]{:S(2)}, u32[]{:S(2)}) collective-permute-start(bf16[2,128,256]{2,1,0:T(8,128)(2,1)S(1)} %get-tuple-element.86), channel_id=1, source_target_pairs={{0,6},{2,4},{4,2},{6,0},{1,7},{3,5},{5,3},{7,1},{8,14},{10,12},{12... | collective-permute-start | bytes 393224 | tf_op jit(solution)/shard_map/ppermute | solution.py:240
  (19 other events, 102.5 us)

commit v5 on v4

--- a/solution.py
+++ b/solution.py
@@ -313,7 +313,7 @@
     for c in range(len(plan.chunks)):
         pack = jnp.stack(kv[c])
         if halo:
-            pack = after(pack, qd[0][last])
+            pack = after(pack, qd[0][1 % group])
         halo.append([moved(pack, -by) for by in distances])
     kv = halo
 

time: 109 us -> 103 us (0.945)
  waiting for transfers between devices: 39.7 us -> 33.9 us
    ppermute x24, waiting for transfers between devices: 32.2 us -> 26 us  [swap(): lax.ppermute(x, 'place', [(i, i ^ m) for i in range(group)])]
  transfers between devices with their start and end apart: 35 -> 35, of which waited for: 17 -> 18; matrix products, arithmetic and copies ran while one was open for 3% -> 3% of each run, Pallas kernels for 11% -> 12%
where the time goes in v5:
time: 103 us
  starting transfers between devices  45.5 us (44%)
  waiting for transfers between devices  33.9 us (33%)
  Pallas kernels  13.6 us (13%)
  other arithmetic  7.09 us (7%)
  between operations  1.82 us (2%)
  local copies, waits for them, and re-layouts  1.13 us (1%)
    ppermute x24, waiting for transfers between devices, swap(): lax.ppermute(x, 'place', [(i, i ^ m) for i in range(group)])  26 us
    ppermute x8, starting transfers between devices, moved(): lax.ppermute(x, 'block', [(i, i + by) for i in range(blocks) if 0 <= i +...  22.6 us
    ppermute x24, starting transfers between devices, swap(): lax.ppermute(x, 'place', [(i, i ^ m) for i in range(group)])  16.7 us
    pallas_call x2, Pallas kernels, attention(): pl.pallas_call(functools.partial(attend, plan=plan, first=first, heads=he...  10.9 us
    ppermute x8, waiting for transfers between devices, moved(): lax.ppermute(x, 'block', [(i, i + by) for i in range(blocks) if 0 <= i +...  6.63 us
    ppermute x3, starting transfers between devices, summed(): x = x + lax.ppermute(x, 'head', [(i, i ^ step) for i in range(count)])  6.16 us
    reduce_sum x2, other arithmetic, local(): jnp.sum(jnp.square(x.astype(f32)), axis=1)  2.7 us
    pallas_call x2, Pallas kernels, joined(): pl.pallas_call(functools.partial(join, plan=plan), grid_spec=pltpu.Prefet...  2.65 us
  transfers between devices with their start and end apart: 35, of which 18 were waited for; matrix products, arithmetic and copies ran while one was open for 3% of the time, Pallas kernels for 12%

profile of v5, /device:TPU:0, one launch (start us, length us, event | category | flops | bytes accessed | tf_op | source)
XLA Modules:
  0.0 103.0 jit_solution(301737394482247575)
XLA Ops:
  0.7 1.4 %fusion.13 = f32[128]{0:T(128)S(1)} fusion(bf16[128,2560]{1,0:T(8,128)(2,1)} %refs_8_.3), kind=kLoop, calls=%fused_computation.17 | loop fusion | flops 982912 | bytes 655872 | tf_op jit(solution)/shard_map/reduce_sum | solution.py:263
  3.4 3.0 %collective-permute-start = (f32[2,128]{1,0:T(2,128)S(1)}, f32[2,128]{1,0:T(2,128)S(1)}, u32[]{:S(2)}, u32[]{:S(2)}) collective-permute-start(f32[2,128]{1,0:T(2,128)S(1)} %pad_maximum_fusion.9), channel_id=1, source_target_pairs={{0,1},{1,0},{2,3},{3,2},{4,5},{5,4},{6,7},{7,6},{8,9},{9,8},{10,11... | collective-permute-start | bytes 3080 | tf_op jit(solution)/shard_map/ppermute | solution.py:252
  8.4 2.1 %collective-permute-start.1 = (bf16[2,128,384]{2,1,0:T(8,128)(2,1)S(1)}, bf16[2,128,384]{2,1,0:T(8,128)(2,1)S(1)}, u32[]{:S(2)}, u32[]{:S(2)}) collective-permute-start(bf16[2,128,384]{2,1,0:T(8,128)(2,1)S(1)} %pad_maximum_fusion.2), channel_id=1, source_target_pairs={{0,4},{2,6},{4,0},{6,2},{1,5},{3,7},{5,1},{7,3},{8,12},{10,14},{12... | collective-permute-start | bytes 589832 | tf_op jit(solution)/shard_map/ppermute | solution.py:240
  11.8 4.0 %collective-permute-done.1 = bf16[2,128,384]{2,1,0:T(8,128)(2,1)S(1)} collective-permute-done((bf16[2,128,384]{2,1,0:T(8,128)(2,1)S(1)}, bf16[2,128,384]{2,1,0:T(8,128)(2,1)S(1)}, u32[]{:S(2)}, u32[]{:S(2)}) %collective-permute-start.1) | collective-permute-done | bytes 196640 | tf_op jit(solution)/shard_map/ppermute | solution.py:240
  15.8 2.2 %collective-permute-done.7 = bf16[2,128,384]{2,1,0:T(8,128)(2,1)S(1)} collective-permute-done((bf16[2,128,384]{2,1,0:T(8,128)(2,1)S(1)}, bf16[2,128,384]{2,1,0:T(8,128)(2,1)S(1)}, u32[]{:S(2)}, u32[]{:S(2)}) %collective-permute-start.7) | collective-permute-done | bytes 196640 | tf_op jit(solution)/shard_map/ppermute | solution.py:240
  18.1 3.5 %collective-permute-start.8 = (bf16[4,2,128,384]{3,2,1,0:T(8,128)(2,1)S(1)}, bf16[4,2,128,384]{3,2,1,0:T(8,128)(2,1)S(1)}, u32[]{:S(2)}, u32[]{:S(2)}) collective-permute-start(bf16[4,2,128,384]{3,2,1,0:T(8,128)(2,1)S(1)} %pad_maximum_fusion.refs_5_), channel_id=1, source_target_pairs={{0,8},{8,16},{16,24},{1,9},{9,17},{17,25},{2,10},{10,18},{18,26},{... | collective-permute-start | bytes 2359304 | tf_op jit(solution)/shard_map/ppermute | solution.py:245
  25.4 3.9 %collective-permute-done.2 = bf16[2,128,256]{2,1,0:T(8,128)(2,1)S(1)} collective-permute-done((bf16[2,128,256]{2,1,0:T(8,128)(2,1)S(1)}, bf16[2,128,256]{2,1,0:T(8,128)(2,1)S(1)}, u32[]{:S(2)}, u32[]{:S(2)}) %collective-permute-start.2) | collective-permute-done | bytes 131104 | tf_op jit(solution)/shard_map/ppermute | solution.py:240
  32.2 4.8 %collective-permute-start.18 = (bf16[4,2,128,256]{3,2,1,0:T(8,128)(2,1)S(1)}, bf16[4,2,128,256]{3,2,1,0:T(8,128)(2,1)S(1)}, u32[]{:S(2)}, u32[]{:S(2)}) collective-permute-start(bf16[4,2,128,256]{3,2,1,0:T(8,128)(2,1)S(1)} %pad_maximum_fusion.1.refs_5_), channel_id=1, source_target_pairs={{0,8},{8,16},{16,24},{1,9},{9,17},{17,25},{2,10},{10,18},{18,26},{... | collective-permute-start | bytes 1572872 | tf_op jit(solution)/shard_map/ppermute | solution.py:245
  38.5 2.4 %collective-permute-done.5.refs_3_ = bf16[272,384]{1,0:T(8,128)(2,1)S(1)} collective-permute-done((bf16[272,384]{1,0:T(8,128)(2,1)S(1)}, bf16[272,384]{1,0:T(8,128)(2,1)S(1)}, u32[]{:S(2)}, u32[]{:S(2)}) %collective-permute-start.5) | collective-permute-done | bytes 208928 | tf_op jit(solution)/shard_map/ppermute | solution.py:240
  42.1 1.7 %collective-permute-done.9.refs_6_ = bf16[4,2,128,384]{3,2,1,0:T(8,128)(2,1)S(1)} collective-permute-done((bf16[4,2,128,384]{3,2,1,0:T(8,128)(2,1)S(1)}, bf16[4,2,128,384]{3,2,1,0:T(8,128)(2,1)S(1)}, u32[]{:S(2)}, u32[]{:S(2)}) %collective-permute-start.9) | collective-permute-done | bytes 786464 | tf_op jit(solution)/shard_map/ppermute | solution.py:245
  44.2 6.6 %attend.2 = (bf16[2,128,384]{2,1,0:T(8,128)(2,1)S(1)}, bf16[2,128,384]{2,1,0:T(8,128)(2,1)S(1)}, bf16[2,128,384]{2,1,0:T(8,128)(2,1)S(1)}, bf16[2,128,384]{2,1,0...) custom-call(s32[1]{0:T(128)} %bitcast.place, ...), custom_call_target="tpu_custom_call" | custom-call | flops 13200000000 | bytes 42000000 | tf_op jit(solution)/shard_map/attend/pallas_call | solution.py:150
  52.1 4.6 %collective-permute-start.27 = (bf16[4,2,128,384]{3,2,1,0:T(8,128)(2,1)S(1)}, bf16[4,2,128,384]{3,2,1,0:T(8,128)(2,1)S(1)}, u32[]{:S(2)}, u32[]{:S(2)}) collective-permute-start(bf16[4,2,128,384]{3,2,1,0:T(8,128)(2,1)S(1)} %get-tuple-element.71), channel_id=1, source_target_pairs={{0,8},{8,16},{16,24},{1,9},{9,17},{17,25},{2,10},{10,18},{18,26},{... | collective-permute-start | bytes 2359304 | tf_op jit(solution)/shard_map/ppermute | solution.py:245
  58.6 4.4 %attend.3 = (bf16[2,128,256]{2,1,0:T(8,128)(2,1)S(1)}, bf16[2,128,256]{2,1,0:T(8,128)(2,1)S(1)}, bf16[2,128,256]{2,1,0:T(8,128)(2,1)S(1)}, bf16[2,128,256]{2,1,0...) custom-call(s32[1]{0:T(128)} %bitcast.place, ...), custom_call_target="tpu_custom_call" | custom-call | flops 8800000000 | bytes 28000000 | tf_op jit(solution)/shard_map/attend/pallas_call | solution.py:150
  64.5 4.6 %collective-permute-start.25 = (bf16[4,2,128,256]{3,2,1,0:T(8,128)(2,1)S(1)}, bf16[4,2,128,256]{3,2,1,0:T(8,128)(2,1)S(1)}, u32[]{:S(2)}, u32[]{:S(2)}) collective-permute-start(bf16[4,2,128,256]{3,2,1,0:T(8,128)(2,1)S(1)} %get-tuple-element.68), channel_id=1, source_target_pairs={{0,8},{8,16},{16,24},{1,9},{9,17},{17,25},{2,10},{10,18},{18,26},{... | collective-permute-start | bytes 1572872 | tf_op jit(solution)/shard_map/ppermute | solution.py:245
  69.2 3.8 %collective-permute-done.26 = bf16[4,2,128,384]{3,2,1,0:T(8,128)(2,1)S(1)} collective-permute-done((bf16[4,2,128,384]{3,2,1,0:T(8,128)(2,1)S(1)}, bf16[4,2,128,384]{3,2,1,0:T(8,128)(2,1)S(1)}, u32[]{:S(2)}, u32[]{:S(2)}) %collective-permute-start.26) | collective-permute-done | bytes 786464 | tf_op jit(solution)/shard_map/ppermute | solution.py:245
  75.7 2.8 %collective-permute-done.21.refs_6_ = bf16[2,128,256]{2,1,0:T(8,128)(2,1)S(1)} collective-permute-done((bf16[2,128,256]{2,1,0:T(8,128)(2,1)S(1)}, bf16[2,128,256]{2,1,0:T(8,128)(2,1)S(1)}, u32[]{:S(2)}, u32[]{:S(2)}) %collective-permute-start.21) | collective-permute-done | bytes 131104 | tf_op jit(solution)/shard_map/ppermute | solution.py:240
  80.3 2.0 %collective-permute-start.30 = (bf16[2,128,384]{2,1,0:T(8,128)(2,1)S(1)}, bf16[2,128,384]{2,1,0:T(8,128)(2,1)S(1)}, u32[]{:S(2)}, u32[]{:S(2)}) collective-permute-start(bf16[2,128,384]{2,1,0:T(8,128)(2,1)S(1)} %get-tuple-element.82), channel_id=1, source_target_pairs={{0,6},{2,4},{4,2},{6,0},{1,7},{3,5},{5,3},{7,1},{8,14},{10,12},{12... | collective-permute-start | bytes 589832 | tf_op jit(solution)/shard_map/ppermute | solution.py:240
  82.3 1.3 %join.2 = (bf16[128,2560]{1,0:T(8,128)(2,1)}, bf16[128,2560]{1,0:T(8,128)(2,1)S(1)}, f32[128,128]{1,0:T(8,128)S(1)}) custom-call(s32[1]{0:T(128)} %bitcast.place, bf16[2,128,384]{2,1,0:T(8,128)(2,1)S(1)} %get-tuple-element.48.refs_0_, bf16[2,128,384]{2,1,0:T(8,128)(2,1)S(1)} %collective-permute-done.10.refs_1_, ...), custom_call_target="tpu_custom_call" | custom-call | flops 2200000000 | bytes 7000000 | tf_op jit(solution)/shard_map/join/pallas_call | solution.py:200
  83.7 1.5 %collective-permute-start.23 = (f32[128]{0:T(128)S(1)}, f32[128]{0:T(128)S(1)}, u32[]{:S(2)}, u32[]{:S(2)}) collective-permute-start(f32[128]{0:T(128)S(1)} %slice_reduce_fusion.1), channel_id=1, source_target_pairs={{0,1},{1,0},{2,3},{3,2},{4,5},{5,4},{6,7},{7,6},{8,9},{9,8},{10,11... | collective-permute-start | bytes 1544 | tf_op jit(solution)/shard_map/ppermute | solution.py:252
  86.3 1.9 %collective-permute-done.30.refs_3_ = bf16[2,128,384]{2,1,0:T(8,128)(2,1)S(1)} collective-permute-done((bf16[2,128,384]{2,1,0:T(8,128)(2,1)S(1)}, bf16[2,128,384]{2,1,0:T(8,128)(2,1)S(1)}, u32[]{:S(2)}, u32[]{:S(2)}) %collective-permute-start.30) | collective-permute-done | bytes 196640 | tf_op jit(solution)/shard_map/ppermute | solution.py:240
  89.3 1.5 %collective-permute-start.32 = (bf16[2,128,256]{2,1,0:T(8,128)(2,1)S(1)}, bf16[2,128,256]{2,1,0:T(8,128)(2,1)S(1)}, u32[]{:S(2)}, u32[]{:S(2)}) collective-permute-start(bf16[2,128,256]{2,1,0:T(8,128)(2,1)S(1)} %get-tuple-element.87), channel_id=1, source_target_pairs={{0,4},{2,6},{4,0},{6,2},{1,5},{3,7},{5,1},{7,3},{8,12},{10,14},{12... | collective-permute-start | bytes 393224 | tf_op jit(solution)/shard_map/ppermute | solution.py:240
  90.8 4.9 %collective-permute-done.32.refs_6_ = bf16[2,128,256]{2,1,0:T(8,128)(2,1)S(1)} collective-permute-done((bf16[2,128,256]{2,1,0:T(8,128)(2,1)S(1)}, bf16[2,128,256]{2,1,0:T(8,128)(2,1)S(1)}, u32[]{:S(2)}, u32[]{:S(2)}) %collective-permute-start.32) | collective-permute-done | bytes 131104 | tf_op jit(solution)/shard_map/ppermute | solution.py:240
  96.7 1.3 %join.3 = (bf16[128,2560]{1,0:T(8,128)(2,1)}, bf16[128,2560]{1,0:T(8,128)(2,1)S(1)}, f32[128,128]{1,0:T(8,128)S(1)}) custom-call(s32[1]{0:T(128)} %bitcast.place, bf16[2,128,384]{2,1,0:T(8,128)(2,1)S(1)} %get-tuple-element.72.refs_0_, bf16[2,128,384]{2,1,0:T(8,128)(2,1)S(1)} %collective-permute-done.28.refs_1_, ...), custom_call_target="tpu_custom_call" | custom-call | flops 2200000000 | bytes 7000000 | tf_op jit(solution)/shard_map/join/pallas_call | solution.py:200
  98.1 1.6 %collective-permute-start.34 = (f32[128]{0:T(128)S(1)}, f32[128]{0:T(128)S(1)}, u32[]{:S(2)}, u32[]{:S(2)}) collective-permute-start(f32[128]{0:T(128)S(1)} %slice_reduce_fusion), channel_id=1, source_target_pairs={{0,1},{1,0},{2,3},{3,2},{4,5},{5,4},{6,7},{7,6},{8,9},{9,8},{10,11... | collective-permute-start | bytes 1544 | tf_op jit(solution)/shard_map/ppermute | solution.py:252
  (104 shorter events, 29.6 us)
Async XLA Ops:
  8.4 7.3 %collective-permute-start.1 = (bf16[2,128,384]{2,1,0:T(8,128)(2,1)S(1)}, bf16[2,128,384]{2,1,0:T(8,128)(2,1)S(1)}, u32[]{:S(2)}, u32[]{:S(2)}) collective-permute-start(bf16[2,128,384]{2,1,0:T(8,128)(2,1)S(1)} %pad_maximum_fusion.2), channel_id=1, source_target_pairs={{0,4},{2,6},{4,0},{6,2},{1,5},{3,7},{5,1},{7,3},{8,12},{10,14},{12... | collective-permute-start | bytes 589832 | tf_op jit(solution)/shard_map/ppermute | solution.py:240
  10.6 7.3 %collective-permute-start.7 = (bf16[2,128,384]{2,1,0:T(8,128)(2,1)S(1)}, bf16[2,128,384]{2,1,0:T(8,128)(2,1)S(1)}, u32[]{:S(2)}, u32[]{:S(2)}) collective-permute-start(bf16[2,128,384]{2,1,0:T(8,128)(2,1)S(1)} %pad_maximum_fusion.4), channel_id=1, source_target_pairs={{0,6},{2,4},{4,2},{6,0},{1,7},{3,5},{5,3},{7,1},{8,14},{10,12},{12... | collective-permute-start | bytes 589832 | tf_op jit(solution)/shard_map/ppermute | solution.py:240
  18.1 23.4 %collective-permute-start.8 = (bf16[4,2,128,384]{3,2,1,0:T(8,128)(2,1)S(1)}, bf16[4,2,128,384]{3,2,1,0:T(8,128)(2,1)S(1)}, u32[]{:S(2)}, u32[]{:S(2)}) collective-permute-start(bf16[4,2,128,384]{3,2,1,0:T(8,128)(2,1)S(1)} %pad_maximum_fusion.refs_5_), channel_id=1, source_target_pairs={{0,8},{8,16},{16,24},{1,9},{9,17},{17,25},{2,10},{10,18},{18,26},{... | collective-permute-start | bytes 2359304 | tf_op jit(solution)/shard_map/ppermute | solution.py:245
  21.6 22.2 %collective-permute-start.9 = (bf16[4,2,128,384]{3,2,1,0:T(8,128)(2,1)S(1)}, bf16[4,2,128,384]{3,2,1,0:T(8,128)(2,1)S(1)}, u32[]{:S(2)}, u32[]{:S(2)}) collective-permute-start(bf16[4,2,128,384]{3,2,1,0:T(8,128)(2,1)S(1)} %pad_maximum_fusion.refs_5_), channel_id=1, source_target_pairs={{8,0},{16,8},{24,16},{9,1},{17,9},{25,17},{10,2},{18,10},{26,18},{... | collective-permute-start | bytes 2359304 | tf_op jit(solution)/shard_map/ppermute | solution.py:245
  22.9 6.4 %collective-permute-start.2 = (bf16[2,128,256]{2,1,0:T(8,128)(2,1)S(1)}, bf16[2,128,256]{2,1,0:T(8,128)(2,1)S(1)}, u32[]{:S(2)}, u32[]{:S(2)}) collective-permute-start(bf16[2,128,256]{2,1,0:T(8,128)(2,1)S(1)} %get-tuple-element.43), channel_id=1, source_target_pairs={{0,4},{2,6},{4,0},{6,2},{1,5},{3,7},{5,1},{7,3},{8,12},{10,14},{12... | collective-permute-start | bytes 393224 | tf_op jit(solution)/shard_map/ppermute | solution.py:240
  24.7 6.6 %collective-permute-start.17 = (bf16[2,128,256]{2,1,0:T(8,128)(2,1)S(1)}, bf16[2,128,256]{2,1,0:T(8,128)(2,1)S(1)}, u32[]{:S(2)}, u32[]{:S(2)}) collective-permute-start(bf16[2,128,256]{2,1,0:T(8,128)(2,1)S(1)} %get-tuple-element.58), channel_id=1, source_target_pairs={{0,6},{2,4},{4,2},{6,0},{1,7},{3,5},{5,3},{7,1},{8,14},{10,12},{12... | collective-permute-start | bytes 393224 | tf_op jit(solution)/shard_map/ppermute | solution.py:240
  29.3 8.0 %collective-permute-start.4 = (bf16[272,384]{1,0:T(8,128)(2,1)S(1)}, bf16[272,384]{1,0:T(8,128)(2,1)S(1)}, u32[]{:S(2)}, u32[]{:S(2)}) collective-permute-start(bf16[272,384]{1,0:T(8,128)(2,1)S(1)} %get-tuple-element.46), channel_id=1, source_target_pairs={{0,4},{2,6},{4,0},{6,2},{1,5},{3,7},{5,1},{7,3},{8,12},{10,14},{12... | collective-permute-start | bytes 626696 | tf_op jit(solution)/shard_map/ppermute | solution.py:240
  31.3 9.7 %collective-permute-start.5 = (bf16[272,384]{1,0:T(8,128)(2,1)S(1)}, bf16[272,384]{1,0:T(8,128)(2,1)S(1)}, u32[]{:S(2)}, u32[]{:S(2)}) collective-permute-start(bf16[272,384]{1,0:T(8,128)(2,1)S(1)} %get-tuple-element.47), channel_id=1, source_target_pairs={{0,6},{2,4},{4,2},{6,0},{1,7},{3,5},{5,3},{7,1},{8,14},{10,12},{12... | collective-permute-start | bytes 626696 | tf_op jit(solution)/shard_map/ppermute | solution.py:240
  32.2 24.5 %collective-permute-start.18 = (bf16[4,2,128,256]{3,2,1,0:T(8,128)(2,1)S(1)}, bf16[4,2,128,256]{3,2,1,0:T(8,128)(2,1)S(1)}, u32[]{:S(2)}, u32[]{:S(2)}) collective-permute-start(bf16[4,2,128,256]{3,2,1,0:T(8,128)(2,1)S(1)} %pad_maximum_fusion.1.refs_5_), channel_id=1, source_target_pairs={{0,8},{8,16},{16,24},{1,9},{9,17},{17,25},{2,10},{10,18},{18,26},{... | collective-permute-start | bytes 1572872 | tf_op jit(solution)/shard_map/ppermute | solution.py:245
  37.3 20.7 %collective-permute-start.19 = (bf16[4,2,128,256]{3,2,1,0:T(8,128)(2,1)S(1)}, bf16[4,2,128,256]{3,2,1,0:T(8,128)(2,1)S(1)}, u32[]{:S(2)}, u32[]{:S(2)}) collective-permute-start(bf16[4,2,128,256]{3,2,1,0:T(8,128)(2,1)S(1)} %pad_maximum_fusion.1.refs_5_), channel_id=1, source_target_pairs={{8,0},{16,8},{24,16},{9,1},{17,9},{25,17},{10,2},{18,10},{26,18},{... | collective-permute-start | bytes 1572872 | tf_op jit(solution)/shard_map/ppermute | solution.py:245
  41.0 9.8 %collective-permute-start.13 = (bf16[272,256]{1,0:T(8,128)(2,1)S(1)}, bf16[272,256]{1,0:T(8,128)(2,1)S(1)}, u32[]{:S(2)}, u32[]{:S(2)}) collective-permute-start(bf16[272,256]{1,0:T(8,128)(2,1)S(1)} %get-tuple-element.53), channel_id=1, source_target_pairs={{0,2},{2,0},{4,6},{6,4},{1,3},{3,1},{5,7},{7,5},{8,10},{10,8},{12,... | collective-permute-start | bytes 417800 | tf_op jit(solution)/shard_map/ppermute | solution.py:240
  41.5 10.6 %collective-permute-start.14 = (bf16[272,256]{1,0:T(8,128)(2,1)S(1)}, bf16[272,256]{1,0:T(8,128)(2,1)S(1)}, u32[]{:S(2)}, u32[]{:S(2)}) collective-permute-start(bf16[272,256]{1,0:T(8,128)(2,1)S(1)} %get-tuple-element.54), channel_id=1, source_target_pairs={{0,4},{2,6},{4,0},{6,2},{1,5},{3,7},{5,1},{7,3},{8,12},{10,14},{12... | collective-permute-start | bytes 417800 | tf_op jit(solution)/shard_map/ppermute | solution.py:240
  43.8 12.8 %collective-permute-start.15 = (bf16[272,256]{1,0:T(8,128)(2,1)S(1)}, bf16[272,256]{1,0:T(8,128)(2,1)S(1)}, u32[]{:S(2)}, u32[]{:S(2)}) collective-permute-start(bf16[272,256]{1,0:T(8,128)(2,1)S(1)} %get-tuple-element.55), channel_id=1, source_target_pairs={{0,6},{2,4},{4,2},{6,0},{1,7},{3,5},{5,3},{7,1},{8,14},{10,12},{12... | collective-permute-start | bytes 417800 | tf_op jit(solution)/shard_map/ppermute | solution.py:240
  50.8 22.2 %collective-permute-start.26 = (bf16[4,2,128,384]{3,2,1,0:T(8,128)(2,1)S(1)}, bf16[4,2,128,384]{3,2,1,0:T(8,128)(2,1)S(1)}, u32[]{:S(2)}, u32[]{:S(2)}) collective-permute-start(bf16[4,2,128,384]{3,2,1,0:T(8,128)(2,1)S(1)} %get-tuple-element.70), channel_id=1, source_target_pairs={{8,0},{16,8},{24,16},{9,1},{17,9},{25,17},{10,2},{18,10},{26,18},{... | collective-permute-start | bytes 2359304 | tf_op jit(solution)/shard_map/ppermute | solution.py:245
  52.1 22.4 %collective-permute-start.27 = (bf16[4,2,128,384]{3,2,1,0:T(8,128)(2,1)S(1)}, bf16[4,2,128,384]{3,2,1,0:T(8,128)(2,1)S(1)}, u32[]{:S(2)}, u32[]{:S(2)}) collective-permute-start(bf16[4,2,128,384]{3,2,1,0:T(8,128)(2,1)S(1)} %get-tuple-element.71), channel_id=1, source_target_pairs={{0,8},{8,16},{16,24},{1,9},{9,17},{17,25},{2,10},{10,18},{18,26},{... | collective-permute-start | bytes 2359304 | tf_op jit(solution)/shard_map/ppermute | solution.py:245
  56.8 7.8 %collective-permute-start.11 = (bf16[2,128,384]{2,1,0:T(8,128)(2,1)S(1)}, bf16[2,128,384]{2,1,0:T(8,128)(2,1)S(1)}, u32[]{:S(2)}, u32[]{:S(2)}) collective-permute-start(bf16[2,128,384]{2,1,0:T(8,128)(2,1)S(1)} %get-tuple-element.50), channel_id=1, source_target_pairs={{0,4},{2,6},{4,0},{6,2},{1,5},{3,7},{5,1},{7,3},{8,12},{10,14},{12... | collective-permute-start | bytes 589832 | tf_op jit(solution)/shard_map/ppermute | solution.py:240
  58.0 11.1 %collective-permute-start.12 = (bf16[2,128,384]{2,1,0:T(8,128)(2,1)S(1)}, bf16[2,128,384]{2,1,0:T(8,128)(2,1)S(1)}, u32[]{:S(2)}, u32[]{:S(2)}) collective-permute-start(bf16[2,128,384]{2,1,0:T(8,128)(2,1)S(1)} %get-tuple-element.51), channel_id=1, source_target_pairs={{0,6},{2,4},{4,2},{6,0},{1,7},{3,5},{5,3},{7,1},{8,14},{10,12},{12... | collective-permute-start | bytes 589832 | tf_op jit(solution)/shard_map/ppermute | solution.py:240
  63.0 20.7 %collective-permute-start.24 = (bf16[4,2,128,256]{3,2,1,0:T(8,128)(2,1)S(1)}, bf16[4,2,128,256]{3,2,1,0:T(8,128)(2,1)S(1)}, u32[]{:S(2)}, u32[]{:S(2)}) collective-permute-start(bf16[4,2,128,256]{3,2,1,0:T(8,128)(2,1)S(1)} %get-tuple-element.67), channel_id=1, source_target_pairs={{8,0},{16,8},{24,16},{9,1},{17,9},{25,17},{10,2},{18,10},{26,18},{... | collective-permute-start | bytes 1572872 | tf_op jit(solution)/shard_map/ppermute | solution.py:245
  64.5 20.7 %collective-permute-start.25 = (bf16[4,2,128,256]{3,2,1,0:T(8,128)(2,1)S(1)}, bf16[4,2,128,256]{3,2,1,0:T(8,128)(2,1)S(1)}, u32[]{:S(2)}, u32[]{:S(2)}) collective-permute-start(bf16[4,2,128,256]{3,2,1,0:T(8,128)(2,1)S(1)} %get-tuple-element.68), channel_id=1, source_target_pairs={{0,8},{8,16},{16,24},{1,9},{9,17},{17,25},{2,10},{10,18},{18,26},{... | collective-permute-start | bytes 1572872 | tf_op jit(solution)/shard_map/ppermute | solution.py:245
  75.1 10.2 %collective-permute-start.28 = (bf16[2,128,384]{2,1,0:T(8,128)(2,1)S(1)}, bf16[2,128,384]{2,1,0:T(8,128)(2,1)S(1)}, u32[]{:S(2)}, u32[]{:S(2)}) collective-permute-start(bf16[2,128,384]{2,1,0:T(8,128)(2,1)S(1)} %get-tuple-element.84), channel_id=1, source_target_pairs={{0,2},{2,0},{4,6},{6,4},{1,3},{3,1},{5,7},{7,5},{8,10},{10,8},{12,... | collective-permute-start | bytes 589832 | tf_op jit(solution)/shard_map/ppermute | solution.py:240
  78.4 7.8 %collective-permute-start.29 = (bf16[2,128,384]{2,1,0:T(8,128)(2,1)S(1)}, bf16[2,128,384]{2,1,0:T(8,128)(2,1)S(1)}, u32[]{:S(2)}, u32[]{:S(2)}) collective-permute-start(bf16[2,128,384]{2,1,0:T(8,128)(2,1)S(1)} %get-tuple-element.83), channel_id=1, source_target_pairs={{0,4},{2,6},{4,0},{6,2},{1,5},{3,7},{5,1},{7,3},{8,12},{10,14},{12... | collective-permute-start | bytes 589832 | tf_op jit(solution)/shard_map/ppermute | solution.py:240
  80.3 7.9 %collective-permute-start.30 = (bf16[2,128,384]{2,1,0:T(8,128)(2,1)S(1)}, bf16[2,128,384]{2,1,0:T(8,128)(2,1)S(1)}, u32[]{:S(2)}, u32[]{:S(2)}) collective-permute-start(bf16[2,128,384]{2,1,0:T(8,128)(2,1)S(1)} %get-tuple-element.82), channel_id=1, source_target_pairs={{0,6},{2,4},{4,2},{6,0},{1,7},{3,5},{5,3},{7,1},{8,14},{10,12},{12... | collective-permute-start | bytes 589832 | tf_op jit(solution)/shard_map/ppermute | solution.py:240
  83.7 7.0 %collective-permute-start.23 = (f32[128]{0:T(128)S(1)}, f32[128]{0:T(128)S(1)}, u32[]{:S(2)}, u32[]{:S(2)}) collective-permute-start(f32[128]{0:T(128)S(1)} %slice_reduce_fusion.1), channel_id=1, source_target_pairs={{0,1},{1,0},{2,3},{3,2},{4,5},{5,4},{6,7},{7,6},{8,9},{9,8},{10,11... | collective-permute-start | bytes 1544 | tf_op jit(solution)/shard_map/ppermute | solution.py:252
  89.3 6.4 %collective-permute-start.32 = (bf16[2,128,256]{2,1,0:T(8,128)(2,1)S(1)}, bf16[2,128,256]{2,1,0:T(8,128)(2,1)S(1)}, u32[]{:S(2)}, u32[]{:S(2)}) collective-permute-start(bf16[2,128,256]{2,1,0:T(8,128)(2,1)S(1)} %get-tuple-element.87), channel_id=1, source_target_pairs={{0,4},{2,6},{4,0},{6,2},{1,5},{3,7},{5,1},{7,3},{8,12},{10,14},{12... | collective-permute-start | bytes 393224 | tf_op jit(solution)/shard_map/ppermute | solution.py:240
  (19 other events, 97.9 us)

commit v6 on v5

--- a/solution.py
+++ b/solution.py
@@ -162,7 +162,7 @@
         ),
         out_shape=outs,
         compiler_params=pltpu.CompilerParams(vmem_limit_bytes=36 * 2**20),
-        cost_estimate=busy(4 * heads),
+        cost_estimate=busy(10 * heads),
         name="attend",
     )(*args)
     return result[:group], result[group:]
@@ -307,7 +307,7 @@
         arrived = swaps(mine)
         kv.append(arrived)
     for c in range(len(plan.chunks)):
-        arrived = swaps(after(qd_cut[c], arrived[half]))
+        arrived = swaps(after(qd_cut[c], arrived[1 % group]))
         qd.append(arrived)
     halo = []
     for c in range(len(plan.chunks)):

time: 103 us -> 103 us (level)
  waiting for transfers between devices: 33.9 us -> 29.5 us
  starting transfers between devices: 45.5 us -> 49.7 us
    ppermute x24, starting transfers between devices: 16.7 us -> 21.4 us  [swap(): lax.ppermute(x, 'place', [(i, i ^ m) for i in range(group)])]
    ppermute x24, waiting for transfers between devices: 26 us -> 22.1 us  [swap(): lax.ppermute(x, 'place', [(i, i ^ m) for i in range(group)])]
  transfers between devices with their start and end apart: 35 -> 35, of which waited for: 18 -> 16; matrix products, arithmetic and copies ran while one was open for 3% -> 3% of each run, Pallas kernels for 12% -> 12%
where the time goes in v6:
time: 103 us
  starting transfers between devices  49.7 us (48%)
  waiting for transfers between devices  29.5 us (29%)
  Pallas kernels  13.6 us (13%)
  other arithmetic  7.09 us (7%)
  between operations  1.84 us (2%)
  local copies, waits for them, and re-layouts  1.13 us (1%)
    ppermute x24, waiting for transfers between devices, swap(): lax.ppermute(x, 'place', [(i, i ^ m) for i in range(group)])  22.1 us
    ppermute x8, starting transfers between devices, moved(): lax.ppermute(x, 'block', [(i, i + by) for i in range(blocks) if 0 <= i +...  22.1 us
    ppermute x24, starting transfers between devices, swap(): lax.ppermute(x, 'place', [(i, i ^ m) for i in range(group)])  21.4 us
    pallas_call x2, Pallas kernels, attention(): pl.pallas_call(functools.partial(attend, plan=plan, first=first, heads=he...  10.9 us
    ppermute x3, starting transfers between devices, summed(): x = x + lax.ppermute(x, 'head', [(i, i ^ step) for i in range(count)])  6.19 us
    ppermute x8, waiting for transfers between devices, moved(): lax.ppermute(x, 'block', [(i, i + by) for i in range(blocks) if 0 <= i +...  6.07 us
    reduce_sum x2, other arithmetic, local(): jnp.sum(jnp.square(x.astype(f32)), axis=1)  2.7 us
    pallas_call x2, Pallas kernels, joined(): pl.pallas_call(functools.partial(join, plan=plan), grid_spec=pltpu.Prefet...  2.65 us
  transfers between devices with their start and end apart: 35, of which 16 were waited for; matrix products, arithmetic and copies ran while one was open for 3% of the time, Pallas kernels for 12%

profile of v6, /device:TPU:0, one launch (start us, length us, event | category | flops | bytes accessed | tf_op | source)
XLA Modules:
  0.0 102.9 jit_solution(3529413614839030999)
XLA Ops:
  3.4 3.0 %collective-permute-start = (f32[2,128]{1,0:T(2,128)S(1)}, f32[2,128]{1,0:T(2,128)S(1)}, u32[]{:S(2)}, u32[]{:S(2)}) collective-permute-start(f32[2,128]{1,0:T(2,128)S(1)} %pad_maximum_fusion.9), channel_id=1, source_target_pairs={{0,1},{1,0},{2,3},{3,2},{4,5},{5,4},{6,7},{7,6},{8,9},{9,8},{10,11... | collective-permute-start | bytes 3080 | tf_op jit(solution)/shard_map/ppermute | solution.py:252
  8.4 2.1 %collective-permute-start.1 = (bf16[2,128,384]{2,1,0:T(8,128)(2,1)S(1)}, bf16[2,128,384]{2,1,0:T(8,128)(2,1)S(1)}, u32[]{:S(2)}, u32[]{:S(2)}) collective-permute-start(bf16[2,128,384]{2,1,0:T(8,128)(2,1)S(1)} %pad_maximum_fusion.2), channel_id=1, source_target_pairs={{0,4},{2,6},{4,0},{6,2},{1,5},{3,7},{5,1},{7,3},{8,12},{10,14},{12... | collective-permute-start | bytes 589832 | tf_op jit(solution)/shard_map/ppermute | solution.py:240
  11.8 4.0 %collective-permute-done.1 = bf16[2,128,384]{2,1,0:T(8,128)(2,1)S(1)} collective-permute-done((bf16[2,128,384]{2,1,0:T(8,128)(2,1)S(1)}, bf16[2,128,384]{2,1,0:T(8,128)(2,1)S(1)}, u32[]{:S(2)}, u32[]{:S(2)}) %collective-permute-start.1) | collective-permute-done | bytes 196640 | tf_op jit(solution)/shard_map/ppermute | solution.py:240
  15.8 2.2 %collective-permute-done.7 = bf16[2,128,384]{2,1,0:T(8,128)(2,1)S(1)} collective-permute-done((bf16[2,128,384]{2,1,0:T(8,128)(2,1)S(1)}, bf16[2,128,384]{2,1,0:T(8,128)(2,1)S(1)}, u32[]{:S(2)}, u32[]{:S(2)}) %collective-permute-start.7) | collective-permute-done | bytes 196640 | tf_op jit(solution)/shard_map/ppermute | solution.py:240
  18.1 3.5 %collective-permute-start.8 = (bf16[4,2,128,384]{3,2,1,0:T(8,128)(2,1)S(1)}, bf16[4,2,128,384]{3,2,1,0:T(8,128)(2,1)S(1)}, u32[]{:S(2)}, u32[]{:S(2)}) collective-permute-start(bf16[4,2,128,384]{3,2,1,0:T(8,128)(2,1)S(1)} %pad_maximum_fusion.refs_5_), channel_id=1, source_target_pairs={{0,8},{8,16},{16,24},{1,9},{9,17},{17,25},{2,10},{10,18},{18,26},{... | collective-permute-start | bytes 2359304 | tf_op jit(solution)/shard_map/ppermute | solution.py:245
  23.5 1.5 %collective-permute-start.16 = (bf16[2,128,256]{2,1,0:T(8,128)(2,1)S(1)}, bf16[2,128,256]{2,1,0:T(8,128)(2,1)S(1)}, u32[]{:S(2)}, u32[]{:S(2)}) collective-permute-start(bf16[2,128,256]{2,1,0:T(8,128)(2,1)S(1)} %get-tuple-element.57), channel_id=1, source_target_pairs={{0,4},{2,6},{4,0},{6,2},{1,5},{3,7},{5,1},{7,3},{8,12},{10,14},{12... | collective-permute-start | bytes 393224 | tf_op jit(solution)/shard_map/ppermute | solution.py:240
  26.0 3.9 %collective-permute-done.16 = bf16[2,128,256]{2,1,0:T(8,128)(2,1)S(1)} collective-permute-done((bf16[2,128,256]{2,1,0:T(8,128)(2,1)S(1)}, bf16[2,128,256]{2,1,0:T(8,128)(2,1)S(1)}, u32[]{:S(2)}, u32[]{:S(2)}) %collective-permute-start.16) | collective-permute-done | bytes 131104 | tf_op jit(solution)/shard_map/ppermute | solution.py:240
  31.7 2.2 %collective-permute-start.5 = (bf16[272,384]{1,0:T(8,128)(2,1)S(1)}, bf16[272,384]{1,0:T(8,128)(2,1)S(1)}, u32[]{:S(2)}, u32[]{:S(2)}) collective-permute-start(bf16[272,384]{1,0:T(8,128)(2,1)S(1)} %get-tuple-element.47), channel_id=1, source_target_pairs={{0,6},{2,4},{4,2},{6,0},{1,7},{3,5},{5,3},{7,1},{8,14},{10,12},{12... | collective-permute-start | bytes 626696 | tf_op jit(solution)/shard_map/ppermute | solution.py:240
  34.1 4.3 %collective-permute-start.18 = (bf16[4,2,128,256]{3,2,1,0:T(8,128)(2,1)S(1)}, bf16[4,2,128,256]{3,2,1,0:T(8,128)(2,1)S(1)}, u32[]{:S(2)}, u32[]{:S(2)}) collective-permute-start(bf16[4,2,128,256]{3,2,1,0:T(8,128)(2,1)S(1)} %pad_maximum_fusion.1.refs_5_), channel_id=1, source_target_pairs={{0,8},{8,16},{16,24},{1,9},{9,17},{17,25},{2,10},{10,18},{18,26},{... | collective-permute-start | bytes 1572872 | tf_op jit(solution)/shard_map/ppermute | solution.py:245
  40.9 1.5 %collective-permute-start.14 = (bf16[272,256]{1,0:T(8,128)(2,1)S(1)}, bf16[272,256]{1,0:T(8,128)(2,1)S(1)}, u32[]{:S(2)}, u32[]{:S(2)}) collective-permute-start(bf16[272,256]{1,0:T(8,128)(2,1)S(1)} %get-tuple-element.54), channel_id=1, source_target_pairs={{0,4},{2,6},{4,0},{6,2},{1,5},{3,7},{5,1},{7,3},{8,12},{10,14},{12... | collective-permute-start | bytes 417800 | tf_op jit(solution)/shard_map/ppermute | solution.py:240
  43.8 6.6 %attend.2 = (bf16[2,128,384]{2,1,0:T(8,128)(2,1)S(1)}, bf16[2,128,384]{2,1,0:T(8,128)(2,1)S(1)}, bf16[2,128,384]{2,1,0:T(8,128)(2,1)S(1)}, bf16[2,128,384]{2,1,0...) custom-call(s32[1]{0:T(128)} %bitcast.place, ...), custom_call_target="tpu_custom_call" | custom-call | flops 32999999488 | bytes 105000000 | tf_op jit(solution)/shard_map/attend/pallas_call | solution.py:150
  51.7 4.6 %collective-permute-start.27 = (bf16[4,2,128,384]{3,2,1,0:T(8,128)(2,1)S(1)}, bf16[4,2,128,384]{3,2,1,0:T(8,128)(2,1)S(1)}, u32[]{:S(2)}, u32[]{:S(2)}) collective-permute-start(bf16[4,2,128,384]{3,2,1,0:T(8,128)(2,1)S(1)} %get-tuple-element.71), channel_id=1, source_target_pairs={{0,8},{8,16},{16,24},{1,9},{9,17},{17,25},{2,10},{10,18},{18,26},{... | collective-permute-start | bytes 2359304 | tf_op jit(solution)/shard_map/ppermute | solution.py:245
  56.5 1.5 %collective-permute-start.11 = (bf16[2,128,384]{2,1,0:T(8,128)(2,1)S(1)}, bf16[2,128,384]{2,1,0:T(8,128)(2,1)S(1)}, u32[]{:S(2)}, u32[]{:S(2)}) collective-permute-start(bf16[2,128,384]{2,1,0:T(8,128)(2,1)S(1)} %get-tuple-element.50), channel_id=1, source_target_pairs={{0,4},{2,6},{4,0},{6,2},{1,5},{3,7},{5,1},{7,3},{8,12},{10,14},{12... | collective-permute-start | bytes 589832 | tf_op jit(solution)/shard_map/ppermute | solution.py:240
  58.3 4.4 %attend.3 = (bf16[2,128,256]{2,1,0:T(8,128)(2,1)S(1)}, bf16[2,128,256]{2,1,0:T(8,128)(2,1)S(1)}, bf16[2,128,256]{2,1,0:T(8,128)(2,1)S(1)}, bf16[2,128,256]{2,1,0...) custom-call(s32[1]{0:T(128)} %bitcast.place, ...), custom_call_target="tpu_custom_call" | custom-call | flops 22000001024 | bytes 70000000 | tf_op jit(solution)/shard_map/attend/pallas_call | solution.py:150
  64.2 4.6 %collective-permute-start.25 = (bf16[4,2,128,256]{3,2,1,0:T(8,128)(2,1)S(1)}, bf16[4,2,128,256]{3,2,1,0:T(8,128)(2,1)S(1)}, u32[]{:S(2)}, u32[]{:S(2)}) collective-permute-start(bf16[4,2,128,256]{3,2,1,0:T(8,128)(2,1)S(1)} %get-tuple-element.68), channel_id=1, source_target_pairs={{0,8},{8,16},{16,24},{1,9},{9,17},{17,25},{2,10},{10,18},{18,26},{... | collective-permute-start | bytes 1572872 | tf_op jit(solution)/shard_map/ppermute | solution.py:245
  68.9 3.8 %collective-permute-done.26 = bf16[4,2,128,384]{3,2,1,0:T(8,128)(2,1)S(1)} collective-permute-done((bf16[4,2,128,384]{3,2,1,0:T(8,128)(2,1)S(1)}, bf16[4,2,128,384]{3,2,1,0:T(8,128)(2,1)S(1)}, u32[]{:S(2)}, u32[]{:S(2)}) %collective-permute-start.26) | collective-permute-done | bytes 786464 | tf_op jit(solution)/shard_map/ppermute | solution.py:245
  75.7 2.5 %collective-permute-done.21.refs_6_ = bf16[2,128,256]{2,1,0:T(8,128)(2,1)S(1)} collective-permute-done((bf16[2,128,256]{2,1,0:T(8,128)(2,1)S(1)}, bf16[2,128,256]{2,1,0:T(8,128)(2,1)S(1)}, u32[]{:S(2)}, u32[]{:S(2)}) %collective-permute-start.21) | collective-permute-done | bytes 131104 | tf_op jit(solution)/shard_map/ppermute | solution.py:240
  78.2 1.6 %collective-permute-start.29 = (bf16[2,128,384]{2,1,0:T(8,128)(2,1)S(1)}, bf16[2,128,384]{2,1,0:T(8,128)(2,1)S(1)}, u32[]{:S(2)}, u32[]{:S(2)}) collective-permute-start(bf16[2,128,384]{2,1,0:T(8,128)(2,1)S(1)} %get-tuple-element.83), channel_id=1, source_target_pairs={{0,4},{2,6},{4,0},{6,2},{1,5},{3,7},{5,1},{7,3},{8,12},{10,14},{12... | collective-permute-start | bytes 589832 | tf_op jit(solution)/shard_map/ppermute | solution.py:240
  80.1 2.2 %collective-permute-start.30 = (bf16[2,128,384]{2,1,0:T(8,128)(2,1)S(1)}, bf16[2,128,384]{2,1,0:T(8,128)(2,1)S(1)}, u32[]{:S(2)}, u32[]{:S(2)}) collective-permute-start(bf16[2,128,384]{2,1,0:T(8,128)(2,1)S(1)} %get-tuple-element.82), channel_id=1, source_target_pairs={{0,6},{2,4},{4,2},{6,0},{1,7},{3,5},{5,3},{7,1},{8,14},{10,12},{12... | collective-permute-start | bytes 589832 | tf_op jit(solution)/shard_map/ppermute | solution.py:240
  83.7 1.6 %collective-permute-start.23 = (f32[128]{0:T(128)S(1)}, f32[128]{0:T(128)S(1)}, u32[]{:S(2)}, u32[]{:S(2)}) collective-permute-start(f32[128]{0:T(128)S(1)} %slice_reduce_fusion.1), channel_id=1, source_target_pairs={{0,1},{1,0},{2,3},{3,2},{4,5},{5,4},{6,7},{7,6},{8,9},{9,8},{10,11... | collective-permute-start | bytes 1544 | tf_op jit(solution)/shard_map/ppermute | solution.py:252
  85.8 2.4 %collective-permute-done.30.refs_3_ = bf16[2,128,384]{2,1,0:T(8,128)(2,1)S(1)} collective-permute-done((bf16[2,128,384]{2,1,0:T(8,128)(2,1)S(1)}, bf16[2,128,384]{2,1,0:T(8,128)(2,1)S(1)}, u32[]{:S(2)}, u32[]{:S(2)}) %collective-permute-start.30) | collective-permute-done | bytes 196640 | tf_op jit(solution)/shard_map/ppermute | solution.py:240
  89.0 1.7 %collective-permute-start.32 = (bf16[2,128,256]{2,1,0:T(8,128)(2,1)S(1)}, bf16[2,128,256]{2,1,0:T(8,128)(2,1)S(1)}, u32[]{:S(2)}, u32[]{:S(2)}) collective-permute-start(bf16[2,128,256]{2,1,0:T(8,128)(2,1)S(1)} %get-tuple-element.87), channel_id=1, source_target_pairs={{0,4},{2,6},{4,0},{6,2},{1,5},{3,7},{5,1},{7,3},{8,12},{10,14},{12... | collective-permute-start | bytes 393224 | tf_op jit(solution)/shard_map/ppermute | solution.py:240
  90.8 4.4 %collective-permute-done.32.refs_6_ = bf16[2,128,256]{2,1,0:T(8,128)(2,1)S(1)} collective-permute-done((bf16[2,128,256]{2,1,0:T(8,128)(2,1)S(1)}, bf16[2,128,256]{2,1,0:T(8,128)(2,1)S(1)}, u32[]{:S(2)}, u32[]{:S(2)}) %collective-permute-start.32) | collective-permute-done | bytes 131104 | tf_op jit(solution)/shard_map/ppermute | solution.py:240
  98.0 1.6 %collective-permute-start.34 = (f32[128]{0:T(128)S(1)}, f32[128]{0:T(128)S(1)}, u32[]{:S(2)}, u32[]{:S(2)}) collective-permute-start(f32[128]{0:T(128)S(1)} %slice_reduce_fusion), channel_id=1, source_target_pairs={{0,1},{1,0},{2,3},{3,2},{4,5},{5,4},{6,7},{7,6},{8,9},{9,8},{10,11... | collective-permute-start | bytes 1544 | tf_op jit(solution)/shard_map/ppermute | solution.py:252
  (104 shorter events, 29.5 us)
Async XLA Ops:
  8.4 7.3 %collective-permute-start.1 = (bf16[2,128,384]{2,1,0:T(8,128)(2,1)S(1)}, bf16[2,128,384]{2,1,0:T(8,128)(2,1)S(1)}, u32[]{:S(2)}, u32[]{:S(2)}) collective-permute-start(bf16[2,128,384]{2,1,0:T(8,128)(2,1)S(1)} %pad_maximum_fusion.2), channel_id=1, source_target_pairs={{0,4},{2,6},{4,0},{6,2},{1,5},{3,7},{5,1},{7,3},{8,12},{10,14},{12... | collective-permute-start | bytes 589832 | tf_op jit(solution)/shard_map/ppermute | solution.py:240
  10.6 7.3 %collective-permute-start.7 = (bf16[2,128,384]{2,1,0:T(8,128)(2,1)S(1)}, bf16[2,128,384]{2,1,0:T(8,128)(2,1)S(1)}, u32[]{:S(2)}, u32[]{:S(2)}) collective-permute-start(bf16[2,128,384]{2,1,0:T(8,128)(2,1)S(1)} %pad_maximum_fusion.4), channel_id=1, source_target_pairs={{0,6},{2,4},{4,2},{6,0},{1,7},{3,5},{5,3},{7,1},{8,14},{10,12},{12... | collective-permute-start | bytes 589832 | tf_op jit(solution)/shard_map/ppermute | solution.py:240
  18.1 22.8 %collective-permute-start.8 = (bf16[4,2,128,384]{3,2,1,0:T(8,128)(2,1)S(1)}, bf16[4,2,128,384]{3,2,1,0:T(8,128)(2,1)S(1)}, u32[]{:S(2)}, u32[]{:S(2)}) collective-permute-start(bf16[4,2,128,384]{3,2,1,0:T(8,128)(2,1)S(1)} %pad_maximum_fusion.refs_5_), channel_id=1, source_target_pairs={{0,8},{8,16},{16,24},{1,9},{9,17},{17,25},{2,10},{10,18},{18,26},{... | collective-permute-start | bytes 2359304 | tf_op jit(solution)/shard_map/ppermute | solution.py:245
  21.6 22.2 %collective-permute-start.9 = (bf16[4,2,128,384]{3,2,1,0:T(8,128)(2,1)S(1)}, bf16[4,2,128,384]{3,2,1,0:T(8,128)(2,1)S(1)}, u32[]{:S(2)}, u32[]{:S(2)}) collective-permute-start(bf16[4,2,128,384]{3,2,1,0:T(8,128)(2,1)S(1)} %pad_maximum_fusion.refs_5_), channel_id=1, source_target_pairs={{8,0},{16,8},{24,16},{9,1},{17,9},{25,17},{10,2},{18,10},{26,18},{... | collective-permute-start | bytes 2359304 | tf_op jit(solution)/shard_map/ppermute | solution.py:245
  23.5 6.4 %collective-permute-start.16 = (bf16[2,128,256]{2,1,0:T(8,128)(2,1)S(1)}, bf16[2,128,256]{2,1,0:T(8,128)(2,1)S(1)}, u32[]{:S(2)}, u32[]{:S(2)}) collective-permute-start(bf16[2,128,256]{2,1,0:T(8,128)(2,1)S(1)} %get-tuple-element.57), channel_id=1, source_target_pairs={{0,4},{2,6},{4,0},{6,2},{1,5},{3,7},{5,1},{7,3},{8,12},{10,14},{12... | collective-permute-start | bytes 393224 | tf_op jit(solution)/shard_map/ppermute | solution.py:240
  25.0 6.7 %collective-permute-start.17 = (bf16[2,128,256]{2,1,0:T(8,128)(2,1)S(1)}, bf16[2,128,256]{2,1,0:T(8,128)(2,1)S(1)}, u32[]{:S(2)}, u32[]{:S(2)}) collective-permute-start(bf16[2,128,256]{2,1,0:T(8,128)(2,1)S(1)} %get-tuple-element.58), channel_id=1, source_target_pairs={{0,6},{2,4},{4,2},{6,0},{1,7},{3,5},{5,3},{7,1},{8,14},{10,12},{12... | collective-permute-start | bytes 393224 | tf_op jit(solution)/shard_map/ppermute | solution.py:240
  25.3 8.8 %collective-permute-start.3 = (bf16[272,384]{1,0:T(8,128)(2,1)S(1)}, bf16[272,384]{1,0:T(8,128)(2,1)S(1)}, u32[]{:S(2)}, u32[]{:S(2)}) collective-permute-start(bf16[272,384]{1,0:T(8,128)(2,1)S(1)} %get-tuple-element.45), channel_id=1, source_target_pairs={{0,2},{2,0},{4,6},{6,4},{1,3},{3,1},{5,7},{7,5},{8,10},{10,8},{12,... | collective-permute-start | bytes 626696 | tf_op jit(solution)/shard_map/ppermute | solution.py:240
  29.8 8.6 %collective-permute-start.4 = (bf16[272,384]{1,0:T(8,128)(2,1)S(1)}, bf16[272,384]{1,0:T(8,128)(2,1)S(1)}, u32[]{:S(2)}, u32[]{:S(2)}) collective-permute-start(bf16[272,384]{1,0:T(8,128)(2,1)S(1)} %get-tuple-element.46), channel_id=1, source_target_pairs={{0,4},{2,6},{4,0},{6,2},{1,5},{3,7},{5,1},{7,3},{8,12},{10,14},{12... | collective-permute-start | bytes 626696 | tf_op jit(solution)/shard_map/ppermute | solution.py:240
  31.7 8.1 %collective-permute-start.5 = (bf16[272,384]{1,0:T(8,128)(2,1)S(1)}, bf16[272,384]{1,0:T(8,128)(2,1)S(1)}, u32[]{:S(2)}, u32[]{:S(2)}) collective-permute-start(bf16[272,384]{1,0:T(8,128)(2,1)S(1)} %get-tuple-element.47), channel_id=1, source_target_pairs={{0,6},{2,4},{4,2},{6,0},{1,7},{3,5},{5,3},{7,1},{8,14},{10,12},{12... | collective-permute-start | bytes 626696 | tf_op jit(solution)/shard_map/ppermute | solution.py:240
  34.1 22.3 %collective-permute-start.18 = (bf16[4,2,128,256]{3,2,1,0:T(8,128)(2,1)S(1)}, bf16[4,2,128,256]{3,2,1,0:T(8,128)(2,1)S(1)}, u32[]{:S(2)}, u32[]{:S(2)}) collective-permute-start(bf16[4,2,128,256]{3,2,1,0:T(8,128)(2,1)S(1)} %pad_maximum_fusion.1.refs_5_), channel_id=1, source_target_pairs={{0,8},{8,16},{16,24},{1,9},{9,17},{17,25},{2,10},{10,18},{18,26},{... | collective-permute-start | bytes 1572872 | tf_op jit(solution)/shard_map/ppermute | solution.py:245
  38.4 19.6 %collective-permute-start.19 = (bf16[4,2,128,256]{3,2,1,0:T(8,128)(2,1)S(1)}, bf16[4,2,128,256]{3,2,1,0:T(8,128)(2,1)S(1)}, u32[]{:S(2)}, u32[]{:S(2)}) collective-permute-start(bf16[4,2,128,256]{3,2,1,0:T(8,128)(2,1)S(1)} %pad_maximum_fusion.1.refs_5_), channel_id=1, source_target_pairs={{8,0},{16,8},{24,16},{9,1},{17,9},{25,17},{10,2},{18,10},{26,18},{... | collective-permute-start | bytes 1572872 | tf_op jit(solution)/shard_map/ppermute | solution.py:245
  39.7 10.7 %collective-permute-start.13 = (bf16[272,256]{1,0:T(8,128)(2,1)S(1)}, bf16[272,256]{1,0:T(8,128)(2,1)S(1)}, u32[]{:S(2)}, u32[]{:S(2)}) collective-permute-start(bf16[272,256]{1,0:T(8,128)(2,1)S(1)} %get-tuple-element.53), channel_id=1, source_target_pairs={{0,2},{2,0},{4,6},{6,4},{1,3},{3,1},{5,7},{7,5},{8,10},{10,8},{12,... | collective-permute-start | bytes 417800 | tf_op jit(solution)/shard_map/ppermute | solution.py:240
  40.9 10.9 %collective-permute-start.14 = (bf16[272,256]{1,0:T(8,128)(2,1)S(1)}, bf16[272,256]{1,0:T(8,128)(2,1)S(1)}, u32[]{:S(2)}, u32[]{:S(2)}) collective-permute-start(bf16[272,256]{1,0:T(8,128)(2,1)S(1)} %get-tuple-element.54), channel_id=1, source_target_pairs={{0,4},{2,6},{4,0},{6,2},{1,5},{3,7},{5,1},{7,3},{8,12},{10,14},{12... | collective-permute-start | bytes 417800 | tf_op jit(solution)/shard_map/ppermute | solution.py:240
  43.8 12.5 %collective-permute-start.15 = (bf16[272,256]{1,0:T(8,128)(2,1)S(1)}, bf16[272,256]{1,0:T(8,128)(2,1)S(1)}, u32[]{:S(2)}, u32[]{:S(2)}) collective-permute-start(bf16[272,256]{1,0:T(8,128)(2,1)S(1)} %get-tuple-element.55), channel_id=1, source_target_pairs={{0,6},{2,4},{4,2},{6,0},{1,7},{3,5},{5,3},{7,1},{8,14},{10,12},{12... | collective-permute-start | bytes 417800 | tf_op jit(solution)/shard_map/ppermute | solution.py:240
  50.4 22.3 %collective-permute-start.26 = (bf16[4,2,128,384]{3,2,1,0:T(8,128)(2,1)S(1)}, bf16[4,2,128,384]{3,2,1,0:T(8,128)(2,1)S(1)}, u32[]{:S(2)}, u32[]{:S(2)}) collective-permute-start(bf16[4,2,128,384]{3,2,1,0:T(8,128)(2,1)S(1)} %get-tuple-element.70), channel_id=1, source_target_pairs={{8,0},{16,8},{24,16},{9,1},{17,9},{25,17},{10,2},{18,10},{26,18},{... | collective-permute-start | bytes 2359304 | tf_op jit(solution)/shard_map/ppermute | solution.py:245
  51.7 22.5 %collective-permute-start.27 = (bf16[4,2,128,384]{3,2,1,0:T(8,128)(2,1)S(1)}, bf16[4,2,128,384]{3,2,1,0:T(8,128)(2,1)S(1)}, u32[]{:S(2)}, u32[]{:S(2)}) collective-permute-start(bf16[4,2,128,384]{3,2,1,0:T(8,128)(2,1)S(1)} %get-tuple-element.71), channel_id=1, source_target_pairs={{0,8},{8,16},{16,24},{1,9},{9,17},{17,25},{2,10},{10,18},{18,26},{... | collective-permute-start | bytes 2359304 | tf_op jit(solution)/shard_map/ppermute | solution.py:245
  56.5 7.8 %collective-permute-start.11 = (bf16[2,128,384]{2,1,0:T(8,128)(2,1)S(1)}, bf16[2,128,384]{2,1,0:T(8,128)(2,1)S(1)}, u32[]{:S(2)}, u32[]{:S(2)}) collective-permute-start(bf16[2,128,384]{2,1,0:T(8,128)(2,1)S(1)} %get-tuple-element.50), channel_id=1, source_target_pairs={{0,4},{2,6},{4,0},{6,2},{1,5},{3,7},{5,1},{7,3},{8,12},{10,14},{12... | collective-permute-start | bytes 589832 | tf_op jit(solution)/shard_map/ppermute | solution.py:240
  58.0 10.8 %collective-permute-start.12 = (bf16[2,128,384]{2,1,0:T(8,128)(2,1)S(1)}, bf16[2,128,384]{2,1,0:T(8,128)(2,1)S(1)}, u32[]{:S(2)}, u32[]{:S(2)}) collective-permute-start(bf16[2,128,384]{2,1,0:T(8,128)(2,1)S(1)} %get-tuple-element.51), channel_id=1, source_target_pairs={{0,6},{2,4},{4,2},{6,0},{1,7},{3,5},{5,3},{7,1},{8,14},{10,12},{12... | collective-permute-start | bytes 589832 | tf_op jit(solution)/shard_map/ppermute | solution.py:240
  62.7 21.0 %collective-permute-start.24 = (bf16[4,2,128,256]{3,2,1,0:T(8,128)(2,1)S(1)}, bf16[4,2,128,256]{3,2,1,0:T(8,128)(2,1)S(1)}, u32[]{:S(2)}, u32[]{:S(2)}) collective-permute-start(bf16[4,2,128,256]{3,2,1,0:T(8,128)(2,1)S(1)} %get-tuple-element.67), channel_id=1, source_target_pairs={{8,0},{16,8},{24,16},{9,1},{17,9},{25,17},{10,2},{18,10},{26,18},{... | collective-permute-start | bytes 1572872 | tf_op jit(solution)/shard_map/ppermute | solution.py:245
  64.2 21.1 %collective-permute-start.25 = (bf16[4,2,128,256]{3,2,1,0:T(8,128)(2,1)S(1)}, bf16[4,2,128,256]{3,2,1,0:T(8,128)(2,1)S(1)}, u32[]{:S(2)}, u32[]{:S(2)}) collective-permute-start(bf16[4,2,128,256]{3,2,1,0:T(8,128)(2,1)S(1)} %get-tuple-element.68), channel_id=1, source_target_pairs={{0,8},{8,16},{16,24},{1,9},{9,17},{17,25},{2,10},{10,18},{18,26},{... | collective-permute-start | bytes 1572872 | tf_op jit(solution)/shard_map/ppermute | solution.py:245
  75.1 10.2 %collective-permute-start.28 = (bf16[2,128,384]{2,1,0:T(8,128)(2,1)S(1)}, bf16[2,128,384]{2,1,0:T(8,128)(2,1)S(1)}, u32[]{:S(2)}, u32[]{:S(2)}) collective-permute-start(bf16[2,128,384]{2,1,0:T(8,128)(2,1)S(1)} %get-tuple-element.84), channel_id=1, source_target_pairs={{0,2},{2,0},{4,6},{6,4},{1,3},{3,1},{5,7},{7,5},{8,10},{10,8},{12,... | collective-permute-start | bytes 589832 | tf_op jit(solution)/shard_map/ppermute | solution.py:240
  78.2 7.6 %collective-permute-start.29 = (bf16[2,128,384]{2,1,0:T(8,128)(2,1)S(1)}, bf16[2,128,384]{2,1,0:T(8,128)(2,1)S(1)}, u32[]{:S(2)}, u32[]{:S(2)}) collective-permute-start(bf16[2,128,384]{2,1,0:T(8,128)(2,1)S(1)} %get-tuple-element.83), channel_id=1, source_target_pairs={{0,4},{2,6},{4,0},{6,2},{1,5},{3,7},{5,1},{7,3},{8,12},{10,14},{12... | collective-permute-start | bytes 589832 | tf_op jit(solution)/shard_map/ppermute | solution.py:240
  80.1 8.1 %collective-permute-start.30 = (bf16[2,128,384]{2,1,0:T(8,128)(2,1)S(1)}, bf16[2,128,384]{2,1,0:T(8,128)(2,1)S(1)}, u32[]{:S(2)}, u32[]{:S(2)}) collective-permute-start(bf16[2,128,384]{2,1,0:T(8,128)(2,1)S(1)} %get-tuple-element.82), channel_id=1, source_target_pairs={{0,6},{2,4},{4,2},{6,0},{1,7},{3,5},{5,3},{7,1},{8,14},{10,12},{12... | collective-permute-start | bytes 589832 | tf_op jit(solution)/shard_map/ppermute | solution.py:240
  83.7 7.0 %collective-permute-start.23 = (f32[128]{0:T(128)S(1)}, f32[128]{0:T(128)S(1)}, u32[]{:S(2)}, u32[]{:S(2)}) collective-permute-start(f32[128]{0:T(128)S(1)} %slice_reduce_fusion.1), channel_id=1, source_target_pairs={{0,1},{1,0},{2,3},{3,2},{4,5},{5,4},{6,7},{7,6},{8,9},{9,8},{10,11... | collective-permute-start | bytes 1544 | tf_op jit(solution)/shard_map/ppermute | solution.py:252
  (19 other events, 97.9 us)

commit v7 on v6

--- a/solution.py
+++ b/solution.py
@@ -330,7 +330,7 @@
     kv_back = []
     for own, sent in back:
         if kv_back:
-            sent, kv_back[-1] = lax.optimization_barrier((sent, kv_back[-1]))
+            sent, kv_back[-1][half] = lax.optimization_barrier((sent, kv_back[-1][half]))
         total = []
         for m in range(group):
             x = own[m]

time: 103 us -> 103 us (level)
  starting transfers between devices: 49.7 us -> 47.2 us
  waiting for transfers between devices: 29.5 us -> 32 us
    ppermute x24, starting transfers between devices: 21.4 us -> 19.3 us  [swap(): lax.ppermute(x, 'place', [(i, i ^ m) for i in range(group)])]
    ppermute x24, waiting for transfers between devices: 22.1 us -> 24.2 us  [swap(): lax.ppermute(x, 'place', [(i, i ^ m) for i in range(group)])]
  transfers between devices with their start and end apart: 35 -> 35, of which waited for: 16 -> 15; matrix products, arithmetic and copies ran while one was open for 3% -> 3% of each run, Pallas kernels for 12% -> 12%
where the time goes in v7:
time: 103 us
  starting transfers between devices  47.2 us (46%)
  waiting for transfers between devices  32 us (31%)
  Pallas kernels  13.6 us (13%)
  other arithmetic  7.07 us (7%)
  between operations  1.83 us (2%)
  local copies, waits for them, and re-layouts  1.13 us (1%)
    ppermute x24, waiting for transfers between devices, swap(): lax.ppermute(x, 'place', [(i, i ^ m) for i in range(group)])  24.2 us
    ppermute x8, starting transfers between devices, moved(): lax.ppermute(x, 'block', [(i, i + by) for i in range(blocks) if 0 <= i +...  22.1 us
    ppermute x24, starting transfers between devices, swap(): lax.ppermute(x, 'place', [(i, i ^ m) for i in range(group)])  19.3 us
    pallas_call x2, Pallas kernels, attention(): pl.pallas_call(functools.partial(attend, plan=plan, first=first, heads=he...  10.9 us
    ppermute x8, waiting for transfers between devices, moved(): lax.ppermute(x, 'block', [(i, i + by) for i in range(blocks) if 0 <= i +...  6.07 us
    ppermute x3, starting transfers between devices, summed(): x = x + lax.ppermute(x, 'head', [(i, i ^ step) for i in range(count)])  5.75 us
    reduce_sum x2, other arithmetic, local(): jnp.sum(jnp.square(x.astype(f32)), axis=1)  2.7 us
    pallas_call x2, Pallas kernels, joined(): pl.pallas_call(functools.partial(join, plan=plan), grid_spec=pltpu.Prefet...  2.64 us
  transfers between devices with their start and end apart: 35, of which 15 were waited for; matrix products, arithmetic and copies ran while one was open for 3% of the time, Pallas kernels for 12%

profile of v7, /device:TPU:0, one launch (start us, length us, event | category | flops | bytes accessed | tf_op | source)
XLA Modules:
  0.0 102.8 jit_solution(9716843610524462558)
XLA Ops:
  3.4 3.0 %collective-permute-start = (f32[2,128]{1,0:T(2,128)S(1)}, f32[2,128]{1,0:T(2,128)S(1)}, u32[]{:S(2)}, u32[]{:S(2)}) collective-permute-start(f32[2,128]{1,0:T(2,128)S(1)} %pad_maximum_fusion.9), channel_id=1, source_target_pairs={{0,1},{1,0},{2,3},{3,2},{4,5},{5,4},{6,7},{7,6},{8,9},{9,8},{10,11... | collective-permute-start | bytes 3080 | tf_op jit(solution)/shard_map/ppermute | solution.py:252
  8.4 2.1 %collective-permute-start.1 = (bf16[2,128,384]{2,1,0:T(8,128)(2,1)S(1)}, bf16[2,128,384]{2,1,0:T(8,128)(2,1)S(1)}, u32[]{:S(2)}, u32[]{:S(2)}) collective-permute-start(bf16[2,128,384]{2,1,0:T(8,128)(2,1)S(1)} %pad_maximum_fusion.2), channel_id=1, source_target_pairs={{0,4},{2,6},{4,0},{6,2},{1,5},{3,7},{5,1},{7,3},{8,12},{10,14},{12... | collective-permute-start | bytes 589832 | tf_op jit(solution)/shard_map/ppermute | solution.py:240
  11.8 4.0 %collective-permute-done.1 = bf16[2,128,384]{2,1,0:T(8,128)(2,1)S(1)} collective-permute-done((bf16[2,128,384]{2,1,0:T(8,128)(2,1)S(1)}, bf16[2,128,384]{2,1,0:T(8,128)(2,1)S(1)}, u32[]{:S(2)}, u32[]{:S(2)}) %collective-permute-start.1) | collective-permute-done | bytes 196640 | tf_op jit(solution)/shard_map/ppermute | solution.py:240
  15.8 2.2 %collective-permute-done.7 = bf16[2,128,384]{2,1,0:T(8,128)(2,1)S(1)} collective-permute-done((bf16[2,128,384]{2,1,0:T(8,128)(2,1)S(1)}, bf16[2,128,384]{2,1,0:T(8,128)(2,1)S(1)}, u32[]{:S(2)}, u32[]{:S(2)}) %collective-permute-start.7) | collective-permute-done | bytes 196640 | tf_op jit(solution)/shard_map/ppermute | solution.py:240
  18.1 3.5 %collective-permute-start.8 = (bf16[4,2,128,384]{3,2,1,0:T(8,128)(2,1)S(1)}, bf16[4,2,128,384]{3,2,1,0:T(8,128)(2,1)S(1)}, u32[]{:S(2)}, u32[]{:S(2)}) collective-permute-start(bf16[4,2,128,384]{3,2,1,0:T(8,128)(2,1)S(1)} %pad_maximum_fusion.refs_5_), channel_id=1, source_target_pairs={{0,8},{8,16},{16,24},{1,9},{9,17},{17,25},{2,10},{10,18},{18,26},{... | collective-permute-start | bytes 2359304 | tf_op jit(solution)/shard_map/ppermute | solution.py:245
  23.5 1.5 %collective-permute-start.16 = (bf16[2,128,256]{2,1,0:T(8,128)(2,1)S(1)}, bf16[2,128,256]{2,1,0:T(8,128)(2,1)S(1)}, u32[]{:S(2)}, u32[]{:S(2)}) collective-permute-start(bf16[2,128,256]{2,1,0:T(8,128)(2,1)S(1)} %get-tuple-element.54), channel_id=1, source_target_pairs={{0,4},{2,6},{4,0},{6,2},{1,5},{3,7},{5,1},{7,3},{8,12},{10,14},{12... | collective-permute-start | bytes 393224 | tf_op jit(solution)/shard_map/ppermute | solution.py:240
  26.0 3.9 %collective-permute-done.16 = bf16[2,128,256]{2,1,0:T(8,128)(2,1)S(1)} collective-permute-done((bf16[2,128,256]{2,1,0:T(8,128)(2,1)S(1)}, bf16[2,128,256]{2,1,0:T(8,128)(2,1)S(1)}, u32[]{:S(2)}, u32[]{:S(2)}) %collective-permute-start.16) | collective-permute-done | bytes 131104 | tf_op jit(solution)/shard_map/ppermute | solution.py:240
  29.8 1.5 %collective-permute-start.4 = (bf16[272,384]{1,0:T(8,128)(2,1)S(1)}, bf16[272,384]{1,0:T(8,128)(2,1)S(1)}, u32[]{:S(2)}, u32[]{:S(2)}) collective-permute-start(bf16[272,384]{1,0:T(8,128)(2,1)S(1)} %get-tuple-element.43), channel_id=1, source_target_pairs={{0,4},{2,6},{4,0},{6,2},{1,5},{3,7},{5,1},{7,3},{8,12},{10,14},{12... | collective-permute-start | bytes 626696 | tf_op jit(solution)/shard_map/ppermute | solution.py:240
  31.7 2.2 %collective-permute-start.5 = (bf16[272,384]{1,0:T(8,128)(2,1)S(1)}, bf16[272,384]{1,0:T(8,128)(2,1)S(1)}, u32[]{:S(2)}, u32[]{:S(2)}) collective-permute-start(bf16[272,384]{1,0:T(8,128)(2,1)S(1)} %get-tuple-element.44), channel_id=1, source_target_pairs={{0,6},{2,4},{4,2},{6,0},{1,7},{3,5},{5,3},{7,1},{8,14},{10,12},{12... | collective-permute-start | bytes 626696 | tf_op jit(solution)/shard_map/ppermute | solution.py:240
  34.1 4.3 %collective-permute-start.18 = (bf16[4,2,128,256]{3,2,1,0:T(8,128)(2,1)S(1)}, bf16[4,2,128,256]{3,2,1,0:T(8,128)(2,1)S(1)}, u32[]{:S(2)}, u32[]{:S(2)}) collective-permute-start(bf16[4,2,128,256]{3,2,1,0:T(8,128)(2,1)S(1)} %pad_maximum_fusion.1.refs_5_), channel_id=1, source_target_pairs={{0,8},{8,16},{16,24},{1,9},{9,17},{17,25},{2,10},{10,18},{18,26},{... | collective-permute-start | bytes 1572872 | tf_op jit(solution)/shard_map/ppermute | solution.py:245
  40.9 1.5 %collective-permute-start.14 = (bf16[272,256]{1,0:T(8,128)(2,1)S(1)}, bf16[272,256]{1,0:T(8,128)(2,1)S(1)}, u32[]{:S(2)}, u32[]{:S(2)}) collective-permute-start(bf16[272,256]{1,0:T(8,128)(2,1)S(1)} %get-tuple-element.51), channel_id=1, source_target_pairs={{0,4},{2,6},{4,0},{6,2},{1,5},{3,7},{5,1},{7,3},{8,12},{10,14},{12... | collective-permute-start | bytes 417800 | tf_op jit(solution)/shard_map/ppermute | solution.py:240
  42.3 1.5 %collective-permute-done.9.refs_6_ = bf16[4,2,128,384]{3,2,1,0:T(8,128)(2,1)S(1)} collective-permute-done((bf16[4,2,128,384]{3,2,1,0:T(8,128)(2,1)S(1)}, bf16[4,2,128,384]{3,2,1,0:T(8,128)(2,1)S(1)}, u32[]{:S(2)}, u32[]{:S(2)}) %collective-permute-start.9) | collective-permute-done | bytes 786464 | tf_op jit(solution)/shard_map/ppermute | solution.py:245
  43.8 6.6 %attend.2 = (bf16[2,128,384]{2,1,0:T(8,128)(2,1)S(1)}, bf16[2,128,384]{2,1,0:T(8,128)(2,1)S(1)}, bf16[2,128,384]{2,1,0:T(8,128)(2,1)S(1)}, bf16[2,128,384]{2,1,0...) custom-call(s32[1]{0:T(128)} %bitcast.place, ...), custom_call_target="tpu_custom_call" | custom-call | flops 32999999488 | bytes 105000000 | tf_op jit(solution)/shard_map/attend/pallas_call | solution.py:150
  51.7 4.6 %collective-permute-start.25 = (bf16[4,2,128,384]{3,2,1,0:T(8,128)(2,1)S(1)}, bf16[4,2,128,384]{3,2,1,0:T(8,128)(2,1)S(1)}, u32[]{:S(2)}, u32[]{:S(2)}) collective-permute-start(bf16[4,2,128,384]{3,2,1,0:T(8,128)(2,1)S(1)} %get-tuple-element.66), channel_id=1, source_target_pairs={{0,8},{8,16},{16,24},{1,9},{9,17},{17,25},{2,10},{10,18},{18,26},{... | collective-permute-start | bytes 2359304 | tf_op jit(solution)/shard_map/ppermute | solution.py:245
  56.5 1.5 %collective-permute-start.11 = (bf16[2,128,384]{2,1,0:T(8,128)(2,1)S(1)}, bf16[2,128,384]{2,1,0:T(8,128)(2,1)S(1)}, u32[]{:S(2)}, u32[]{:S(2)}) collective-permute-start(bf16[2,128,384]{2,1,0:T(8,128)(2,1)S(1)} %get-tuple-element.47), channel_id=1, source_target_pairs={{0,4},{2,6},{4,0},{6,2},{1,5},{3,7},{5,1},{7,3},{8,12},{10,14},{12... | collective-permute-start | bytes 589832 | tf_op jit(solution)/shard_map/ppermute | solution.py:240
  58.3 4.4 %attend.3 = (bf16[2,128,256]{2,1,0:T(8,128)(2,1)S(1)}, bf16[2,128,256]{2,1,0:T(8,128)(2,1)S(1)}, bf16[2,128,256]{2,1,0:T(8,128)(2,1)S(1)}, bf16[2,128,256]{2,1,0...) custom-call(s32[1]{0:T(128)} %bitcast.place, ...), custom_call_target="tpu_custom_call" | custom-call | flops 22000001024 | bytes 70000000 | tf_op jit(solution)/shard_map/attend/pallas_call | solution.py:150
  64.2 4.6 %collective-permute-start.28 = (bf16[4,2,128,256]{3,2,1,0:T(8,128)(2,1)S(1)}, bf16[4,2,128,256]{3,2,1,0:T(8,128)(2,1)S(1)}, u32[]{:S(2)}, u32[]{:S(2)}) collective-permute-start(bf16[4,2,128,256]{3,2,1,0:T(8,128)(2,1)S(1)} %get-tuple-element.68), channel_id=1, source_target_pairs={{0,8},{8,16},{16,24},{1,9},{9,17},{17,25},{2,10},{10,18},{18,26},{... | collective-permute-start | bytes 1572872 | tf_op jit(solution)/shard_map/ppermute | solution.py:245
  68.9 3.8 %collective-permute-done.24 = bf16[4,2,128,384]{3,2,1,0:T(8,128)(2,1)S(1)} collective-permute-done((bf16[4,2,128,384]{3,2,1,0:T(8,128)(2,1)S(1)}, bf16[4,2,128,384]{3,2,1,0:T(8,128)(2,1)S(1)}, u32[]{:S(2)}, u32[]{:S(2)}) %collective-permute-start.24) | collective-permute-done | bytes 786464 | tf_op jit(solution)/shard_map/ppermute | solution.py:245
  75.8 2.4 %collective-permute-done.21.refs_6_ = bf16[2,128,256]{2,1,0:T(8,128)(2,1)S(1)} collective-permute-done((bf16[2,128,256]{2,1,0:T(8,128)(2,1)S(1)}, bf16[2,128,256]{2,1,0:T(8,128)(2,1)S(1)}, u32[]{:S(2)}, u32[]{:S(2)}) %collective-permute-start.21) | collective-permute-done | bytes 131104 | tf_op jit(solution)/shard_map/ppermute | solution.py:240
  78.2 1.9 %collective-permute-done.22.refs_7_ = bf16[2,128,256]{2,1,0:T(8,128)(2,1)S(1)} collective-permute-done((bf16[2,128,256]{2,1,0:T(8,128)(2,1)S(1)}, bf16[2,128,256]{2,1,0:T(8,128)(2,1)S(1)}, u32[]{:S(2)}, u32[]{:S(2)}) %collective-permute-start.22) | collective-permute-done | bytes 131104 | tf_op jit(solution)/shard_map/ppermute | solution.py:240
  81.5 1.6 %collective-permute-start.23 = (f32[128]{0:T(128)S(1)}, f32[128]{0:T(128)S(1)}, u32[]{:S(2)}, u32[]{:S(2)}) collective-permute-start(f32[128]{0:T(128)S(1)} %slice_reduce_fusion.1), channel_id=1, source_target_pairs={{0,1},{1,0},{2,3},{3,2},{4,5},{5,4},{6,7},{7,6},{8,9},{9,8},{10,11... | collective-permute-start | bytes 1544 | tf_op jit(solution)/shard_map/ppermute | solution.py:252
  87.2 3.6 %collective-permute-done.30.refs_3_ = bf16[2,128,384]{2,1,0:T(8,128)(2,1)S(1)} collective-permute-done((bf16[2,128,384]{2,1,0:T(8,128)(2,1)S(1)}, bf16[2,128,384]{2,1,0:T(8,128)(2,1)S(1)}, u32[]{:S(2)}, u32[]{:S(2)}) %collective-permute-start.30) | collective-permute-done | bytes 196640 | tf_op jit(solution)/shard_map/ppermute | solution.py:240
  90.9 3.2 %collective-permute-done.32.refs_6_ = bf16[2,128,256]{2,1,0:T(8,128)(2,1)S(1)} collective-permute-done((bf16[2,128,256]{2,1,0:T(8,128)(2,1)S(1)}, bf16[2,128,256]{2,1,0:T(8,128)(2,1)S(1)}, u32[]{:S(2)}, u32[]{:S(2)}) %collective-permute-start.32) | collective-permute-done | bytes 131104 | tf_op jit(solution)/shard_map/ppermute | solution.py:240
  94.0 2.4 %collective-permute-done.33.refs_7_ = bf16[2,128,256]{2,1,0:T(8,128)(2,1)S(1)} collective-permute-done((bf16[2,128,256]{2,1,0:T(8,128)(2,1)S(1)}, bf16[2,128,256]{2,1,0:T(8,128)(2,1)S(1)}, u32[]{:S(2)}, u32[]{:S(2)}) %collective-permute-start.33) | collective-permute-done | bytes 131104 | tf_op jit(solution)/shard_map/ppermute | solution.py:240
  (104 shorter events, 29.3 us)
Async XLA Ops:
  8.4 7.3 %collective-permute-start.1 = (bf16[2,128,384]{2,1,0:T(8,128)(2,1)S(1)}, bf16[2,128,384]{2,1,0:T(8,128)(2,1)S(1)}, u32[]{:S(2)}, u32[]{:S(2)}) collective-permute-start(bf16[2,128,384]{2,1,0:T(8,128)(2,1)S(1)} %pad_maximum_fusion.2), channel_id=1, source_target_pairs={{0,4},{2,6},{4,0},{6,2},{1,5},{3,7},{5,1},{7,3},{8,12},{10,14},{12... | collective-permute-start | bytes 589832 | tf_op jit(solution)/shard_map/ppermute | solution.py:240
  10.6 7.3 %collective-permute-start.7 = (bf16[2,128,384]{2,1,0:T(8,128)(2,1)S(1)}, bf16[2,128,384]{2,1,0:T(8,128)(2,1)S(1)}, u32[]{:S(2)}, u32[]{:S(2)}) collective-permute-start(bf16[2,128,384]{2,1,0:T(8,128)(2,1)S(1)} %pad_maximum_fusion.4), channel_id=1, source_target_pairs={{0,6},{2,4},{4,2},{6,0},{1,7},{3,5},{5,3},{7,1},{8,14},{10,12},{12... | collective-permute-start | bytes 589832 | tf_op jit(solution)/shard_map/ppermute | solution.py:240
  18.1 22.8 %collective-permute-start.8 = (bf16[4,2,128,384]{3,2,1,0:T(8,128)(2,1)S(1)}, bf16[4,2,128,384]{3,2,1,0:T(8,128)(2,1)S(1)}, u32[]{:S(2)}, u32[]{:S(2)}) collective-permute-start(bf16[4,2,128,384]{3,2,1,0:T(8,128)(2,1)S(1)} %pad_maximum_fusion.refs_5_), channel_id=1, source_target_pairs={{0,8},{8,16},{16,24},{1,9},{9,17},{17,25},{2,10},{10,18},{18,26},{... | collective-permute-start | bytes 2359304 | tf_op jit(solution)/shard_map/ppermute | solution.py:245
  21.6 22.2 %collective-permute-start.9 = (bf16[4,2,128,384]{3,2,1,0:T(8,128)(2,1)S(1)}, bf16[4,2,128,384]{3,2,1,0:T(8,128)(2,1)S(1)}, u32[]{:S(2)}, u32[]{:S(2)}) collective-permute-start(bf16[4,2,128,384]{3,2,1,0:T(8,128)(2,1)S(1)} %pad_maximum_fusion.refs_5_), channel_id=1, source_target_pairs={{8,0},{16,8},{24,16},{9,1},{17,9},{25,17},{10,2},{18,10},{26,18},{... | collective-permute-start | bytes 2359304 | tf_op jit(solution)/shard_map/ppermute | solution.py:245
  23.5 6.4 %collective-permute-start.16 = (bf16[2,128,256]{2,1,0:T(8,128)(2,1)S(1)}, bf16[2,128,256]{2,1,0:T(8,128)(2,1)S(1)}, u32[]{:S(2)}, u32[]{:S(2)}) collective-permute-start(bf16[2,128,256]{2,1,0:T(8,128)(2,1)S(1)} %get-tuple-element.54), channel_id=1, source_target_pairs={{0,4},{2,6},{4,0},{6,2},{1,5},{3,7},{5,1},{7,3},{8,12},{10,14},{12... | collective-permute-start | bytes 393224 | tf_op jit(solution)/shard_map/ppermute | solution.py:240
  25.0 6.7 %collective-permute-start.17 = (bf16[2,128,256]{2,1,0:T(8,128)(2,1)S(1)}, bf16[2,128,256]{2,1,0:T(8,128)(2,1)S(1)}, u32[]{:S(2)}, u32[]{:S(2)}) collective-permute-start(bf16[2,128,256]{2,1,0:T(8,128)(2,1)S(1)} %get-tuple-element.55), channel_id=1, source_target_pairs={{0,6},{2,4},{4,2},{6,0},{1,7},{3,5},{5,3},{7,1},{8,14},{10,12},{12... | collective-permute-start | bytes 393224 | tf_op jit(solution)/shard_map/ppermute | solution.py:240
  25.3 8.8 %collective-permute-start.3 = (bf16[272,384]{1,0:T(8,128)(2,1)S(1)}, bf16[272,384]{1,0:T(8,128)(2,1)S(1)}, u32[]{:S(2)}, u32[]{:S(2)}) collective-permute-start(bf16[272,384]{1,0:T(8,128)(2,1)S(1)} %get-tuple-element.42), channel_id=1, source_target_pairs={{0,2},{2,0},{4,6},{6,4},{1,3},{3,1},{5,7},{7,5},{8,10},{10,8},{12,... | collective-permute-start | bytes 626696 | tf_op jit(solution)/shard_map/ppermute | solution.py:240
  29.8 8.6 %collective-permute-start.4 = (bf16[272,384]{1,0:T(8,128)(2,1)S(1)}, bf16[272,384]{1,0:T(8,128)(2,1)S(1)}, u32[]{:S(2)}, u32[]{:S(2)}) collective-permute-start(bf16[272,384]{1,0:T(8,128)(2,1)S(1)} %get-tuple-element.43), channel_id=1, source_target_pairs={{0,4},{2,6},{4,0},{6,2},{1,5},{3,7},{5,1},{7,3},{8,12},{10,14},{12... | collective-permute-start | bytes 626696 | tf_op jit(solution)/shard_map/ppermute | solution.py:240
  31.7 8.1 %collective-permute-start.5 = (bf16[272,384]{1,0:T(8,128)(2,1)S(1)}, bf16[272,384]{1,0:T(8,128)(2,1)S(1)}, u32[]{:S(2)}, u32[]{:S(2)}) collective-permute-start(bf16[272,384]{1,0:T(8,128)(2,1)S(1)} %get-tuple-element.44), channel_id=1, source_target_pairs={{0,6},{2,4},{4,2},{6,0},{1,7},{3,5},{5,3},{7,1},{8,14},{10,12},{12... | collective-permute-start | bytes 626696 | tf_op jit(solution)/shard_map/ppermute | solution.py:240
  34.1 22.3 %collective-permute-start.18 = (bf16[4,2,128,256]{3,2,1,0:T(8,128)(2,1)S(1)}, bf16[4,2,128,256]{3,2,1,0:T(8,128)(2,1)S(1)}, u32[]{:S(2)}, u32[]{:S(2)}) collective-permute-start(bf16[4,2,128,256]{3,2,1,0:T(8,128)(2,1)S(1)} %pad_maximum_fusion.1.refs_5_), channel_id=1, source_target_pairs={{0,8},{8,16},{16,24},{1,9},{9,17},{17,25},{2,10},{10,18},{18,26},{... | collective-permute-start | bytes 1572872 | tf_op jit(solution)/shard_map/ppermute | solution.py:245
  38.4 19.6 %collective-permute-start.19 = (bf16[4,2,128,256]{3,2,1,0:T(8,128)(2,1)S(1)}, bf16[4,2,128,256]{3,2,1,0:T(8,128)(2,1)S(1)}, u32[]{:S(2)}, u32[]{:S(2)}) collective-permute-start(bf16[4,2,128,256]{3,2,1,0:T(8,128)(2,1)S(1)} %pad_maximum_fusion.1.refs_5_), channel_id=1, source_target_pairs={{8,0},{16,8},{24,16},{9,1},{17,9},{25,17},{10,2},{18,10},{26,18},{... | collective-permute-start | bytes 1572872 | tf_op jit(solution)/shard_map/ppermute | solution.py:245
  39.7 10.7 %collective-permute-start.13 = (bf16[272,256]{1,0:T(8,128)(2,1)S(1)}, bf16[272,256]{1,0:T(8,128)(2,1)S(1)}, u32[]{:S(2)}, u32[]{:S(2)}) collective-permute-start(bf16[272,256]{1,0:T(8,128)(2,1)S(1)} %get-tuple-element.50), channel_id=1, source_target_pairs={{0,2},{2,0},{4,6},{6,4},{1,3},{3,1},{5,7},{7,5},{8,10},{10,8},{12,... | collective-permute-start | bytes 417800 | tf_op jit(solution)/shard_map/ppermute | solution.py:240
  40.9 10.9 %collective-permute-start.14 = (bf16[272,256]{1,0:T(8,128)(2,1)S(1)}, bf16[272,256]{1,0:T(8,128)(2,1)S(1)}, u32[]{:S(2)}, u32[]{:S(2)}) collective-permute-start(bf16[272,256]{1,0:T(8,128)(2,1)S(1)} %get-tuple-element.51), channel_id=1, source_target_pairs={{0,4},{2,6},{4,0},{6,2},{1,5},{3,7},{5,1},{7,3},{8,12},{10,14},{12... | collective-permute-start | bytes 417800 | tf_op jit(solution)/shard_map/ppermute | solution.py:240
  43.8 12.5 %collective-permute-start.15 = (bf16[272,256]{1,0:T(8,128)(2,1)S(1)}, bf16[272,256]{1,0:T(8,128)(2,1)S(1)}, u32[]{:S(2)}, u32[]{:S(2)}) collective-permute-start(bf16[272,256]{1,0:T(8,128)(2,1)S(1)} %get-tuple-element.52), channel_id=1, source_target_pairs={{0,6},{2,4},{4,2},{6,0},{1,7},{3,5},{5,3},{7,1},{8,14},{10,12},{12... | collective-permute-start | bytes 417800 | tf_op jit(solution)/shard_map/ppermute | solution.py:240
  50.4 22.3 %collective-permute-start.24 = (bf16[4,2,128,384]{3,2,1,0:T(8,128)(2,1)S(1)}, bf16[4,2,128,384]{3,2,1,0:T(8,128)(2,1)S(1)}, u32[]{:S(2)}, u32[]{:S(2)}) collective-permute-start(bf16[4,2,128,384]{3,2,1,0:T(8,128)(2,1)S(1)} %get-tuple-element.65), channel_id=1, source_target_pairs={{8,0},{16,8},{24,16},{9,1},{17,9},{25,17},{10,2},{18,10},{26,18},{... | collective-permute-start | bytes 2359304 | tf_op jit(solution)/shard_map/ppermute | solution.py:245
  51.7 22.5 %collective-permute-start.25 = (bf16[4,2,128,384]{3,2,1,0:T(8,128)(2,1)S(1)}, bf16[4,2,128,384]{3,2,1,0:T(8,128)(2,1)S(1)}, u32[]{:S(2)}, u32[]{:S(2)}) collective-permute-start(bf16[4,2,128,384]{3,2,1,0:T(8,128)(2,1)S(1)} %get-tuple-element.66), channel_id=1, source_target_pairs={{0,8},{8,16},{16,24},{1,9},{9,17},{17,25},{2,10},{10,18},{18,26},{... | collective-permute-start | bytes 2359304 | tf_op jit(solution)/shard_map/ppermute | solution.py:245
  56.5 7.8 %collective-permute-start.11 = (bf16[2,128,384]{2,1,0:T(8,128)(2,1)S(1)}, bf16[2,128,384]{2,1,0:T(8,128)(2,1)S(1)}, u32[]{:S(2)}, u32[]{:S(2)}) collective-permute-start(bf16[2,128,384]{2,1,0:T(8,128)(2,1)S(1)} %get-tuple-element.47), channel_id=1, source_target_pairs={{0,4},{2,6},{4,0},{6,2},{1,5},{3,7},{5,1},{7,3},{8,12},{10,14},{12... | collective-permute-start | bytes 589832 | tf_op jit(solution)/shard_map/ppermute | solution.py:240
  58.0 10.8 %collective-permute-start.12 = (bf16[2,128,384]{2,1,0:T(8,128)(2,1)S(1)}, bf16[2,128,384]{2,1,0:T(8,128)(2,1)S(1)}, u32[]{:S(2)}, u32[]{:S(2)}) collective-permute-start(bf16[2,128,384]{2,1,0:T(8,128)(2,1)S(1)} %get-tuple-element.48), channel_id=1, source_target_pairs={{0,6},{2,4},{4,2},{6,0},{1,7},{3,5},{5,3},{7,1},{8,14},{10,12},{12... | collective-permute-start | bytes 589832 | tf_op jit(solution)/shard_map/ppermute | solution.py:240
  62.7 21.1 %collective-permute-start.27 = (bf16[4,2,128,256]{3,2,1,0:T(8,128)(2,1)S(1)}, bf16[4,2,128,256]{3,2,1,0:T(8,128)(2,1)S(1)}, u32[]{:S(2)}, u32[]{:S(2)}) collective-permute-start(bf16[4,2,128,256]{3,2,1,0:T(8,128)(2,1)S(1)} %get-tuple-element.67), channel_id=1, source_target_pairs={{8,0},{16,8},{24,16},{9,1},{17,9},{25,17},{10,2},{18,10},{26,18},{... | collective-permute-start | bytes 1572872 | tf_op jit(solution)/shard_map/ppermute | solution.py:245
  64.2 20.8 %collective-permute-start.28 = (bf16[4,2,128,256]{3,2,1,0:T(8,128)(2,1)S(1)}, bf16[4,2,128,256]{3,2,1,0:T(8,128)(2,1)S(1)}, u32[]{:S(2)}, u32[]{:S(2)}) collective-permute-start(bf16[4,2,128,256]{3,2,1,0:T(8,128)(2,1)S(1)} %get-tuple-element.68), channel_id=1, source_target_pairs={{0,8},{8,16},{16,24},{1,9},{9,17},{17,25},{2,10},{10,18},{18,26},{... | collective-permute-start | bytes 1572872 | tf_op jit(solution)/shard_map/ppermute | solution.py:245
  75.1 10.0 %collective-permute-start.29 = (bf16[2,128,384]{2,1,0:T(8,128)(2,1)S(1)}, bf16[2,128,384]{2,1,0:T(8,128)(2,1)S(1)}, u32[]{:S(2)}, u32[]{:S(2)}) collective-permute-start(bf16[2,128,384]{2,1,0:T(8,128)(2,1)S(1)} %get-tuple-element.77), channel_id=1, source_target_pairs={{0,4},{2,6},{4,0},{6,2},{1,5},{3,7},{5,1},{7,3},{8,12},{10,14},{12... | collective-permute-start | bytes 589832 | tf_op jit(solution)/shard_map/ppermute | solution.py:240
  83.8 7.0 %collective-permute-start.30 = (bf16[2,128,384]{2,1,0:T(8,128)(2,1)S(1)}, bf16[2,128,384]{2,1,0:T(8,128)(2,1)S(1)}, u32[]{:S(2)}, u32[]{:S(2)}) collective-permute-start(bf16[2,128,384]{2,1,0:T(8,128)(2,1)S(1)} %get-tuple-element.76), channel_id=1, source_target_pairs={{0,6},{2,4},{4,2},{6,0},{1,7},{3,5},{5,3},{7,1},{8,14},{10,12},{12... | collective-permute-start | bytes 589832 | tf_op jit(solution)/shard_map/ppermute | solution.py:240
  85.8 8.3 %collective-permute-start.32 = (bf16[2,128,256]{2,1,0:T(8,128)(2,1)S(1)}, bf16[2,128,256]{2,1,0:T(8,128)(2,1)S(1)}, u32[]{:S(2)}, u32[]{:S(2)}) collective-permute-start(bf16[2,128,256]{2,1,0:T(8,128)(2,1)S(1)} %get-tuple-element.81), channel_id=1, source_target_pairs={{0,4},{2,6},{4,0},{6,2},{1,5},{3,7},{5,1},{7,3},{8,12},{10,14},{12... | collective-permute-start | bytes 393224 | tf_op jit(solution)/shard_map/ppermute | solution.py:240
  86.8 9.7 %collective-permute-start.33 = (bf16[2,128,256]{2,1,0:T(8,128)(2,1)S(1)}, bf16[2,128,256]{2,1,0:T(8,128)(2,1)S(1)}, u32[]{:S(2)}, u32[]{:S(2)}) collective-permute-start(bf16[2,128,256]{2,1,0:T(8,128)(2,1)S(1)} %get-tuple-element.80), channel_id=1, source_target_pairs={{0,6},{2,4},{4,2},{6,0},{1,7},{3,5},{5,3},{7,1},{8,14},{10,12},{12... | collective-permute-start | bytes 393224 | tf_op jit(solution)/shard_map/ppermute | solution.py:240
  (19 other events, 98.6 us)
